TPU v7x, 128 devices: a whole 4x4x4 slice. The times are simulated.
128 devices in a mesh: slab: 16 (over z, y), energy: 8 (over x, core).
Axes of the slice: x: 4, y: 4, z: 4, core: 2. Of those that a mesh axis runs over, the one named last changes fastest.
Arguments:
- source: float32 [32, 2, 16, 192, 128], P('slab', None, 'energy'), may hold values from -1.2 to 1.2
- onsite_block: float32 [192, 192], replicated, may hold values from -1.3 to 1.3, as said below
- hopping_block: float32 [192, 192], replicated, may hold values from -0.5 to 1.5
- potential_table: float32 [16, 192], replicated, may hold values from -0.5 to 0.5
- slab_profile: int32 [32], P('slab'), may hold values from 0 to 15
- occupation: float32 [32, 16, 192], P('slab', 'energy'), may hold values from 0.1 to 1
- coupling: float32 [4], replicated, may hold values from 0.02 to 0.08
- phonon_shift: int32 [4], replicated, may hold values from 1 to 2, as said below
Outputs:
- amplitude: float32 [32, 2, 16, 192, 128], P('slab', None, 'energy')
- density: float32 [32, 16, 192], P('slab', 'energy')
Inputs may be any that keep to these rules, and one draw needn't show every extreme that they name: `phonon_shift`: some mode shifts by exactly 2 points and some by exactly 1. `onsite_block`: symmetric.
All inputs are finite; a program needn't handle non-finite values.
Results may differ from a plain program's by a relative error of at most 0.0003.
Values sent between devices are 32-bit elements; how exact they have to be, the bound alone decides.
No kernel may reach another device: no remote copies, remote signals or barrier semaphores. Data moves between devices by JAX's collectives and lax.ppermute only.
A program may use at most 128 MiB of HBM per device.

v0:
```python
import functools

import jax
import jax.numpy as jnp
from jax import lax
from jax.experimental import pallas as pl
from jax.experimental.pallas import tpu as pltpu
from jax.sharding import PartitionSpec as P

broadening = 0.05
energy_low = -1.2
energy_step = 0.15
N = 192
COLS = 128
WIDE = 256
BLOCK = 32


def split(x):
    hi = x.astype(jnp.bfloat16)
    lo = (x - hi.astype(jnp.float32)).astype(jnp.bfloat16)
    return hi, lo


def tn(a, b):
    return lax.dot_general(a, b, (((0,), (0,)), ((), ())), preferred_element_type=jnp.float32)


def spread(row):
    return jnp.broadcast_to(row, (8, 128))


def invert_eight(cr, ci):
    row = lax.broadcasted_iota(jnp.int32, (8, 128), 0)
    for p in range(8):
        dr, di = spread(cr[p][p : p + 1]), spread(ci[p][p : p + 1])
        inv = 1.0 / (dr * dr + di * di)
        er, ei = dr * inv, -di * inv
        here = row == p
        wr = jnp.where(here, 1.0 - er, cr[p] * er - ci[p] * ei)
        wi = jnp.where(here, -ei, cr[p] * ei + ci[p] * er)
        for j in range(8):
            if j != p:
                fr, fi = spread(cr[j][p : p + 1]), spread(ci[j][p : p + 1])
                cr[j], ci[j] = cr[j] - (wr * fr - wi * fi), ci[j] - (wr * fi + wi * fr)
        cr[p] = jnp.where(here, er, -wr)
        ci[p] = jnp.where(here, ei, -wi)
    return cr, ci


def small_inverse(m):
    lane = lax.broadcasted_iota(jnp.int32, (8, 128), 1)
    row = lax.broadcasted_iota(jnp.int32, (8, 128), 0)
    start = (lane // 64) * 64
    real = lane - start < 32
    off = lane - (lane // 32) * 32

    def turned(x):
        return jnp.where(real, -pltpu.roll(x, 96, 1), pltpu.roll(x, 32, 1))

    def group(g, _):
        o = pl.multiple_of(8 * g, 8)
        own = m[pl.ds(o, 8), :]
        parts = [m[8 * h : 8 * h + 8, :] for h in range(4)]
        take = lambda x, j: jnp.take_along_axis(x, start + (o + j), axis=1)
        cr = [take(own, j) for j in range(8)]
        ci = [take(own, j + 32) for j in range(8)]
        wide_r = [[take(x, j) for j in range(8)] for x in parts]
        wide_i = [[take(x, j + 32) for j in range(8)] for x in parts]
        inside = (off >= o) & (off < o + 8)
        eye = jnp.where(real & (off - o == row), 1.0, 0.0)
        now = jnp.where(inside, eye, own)
        side = turned(now)
        rows = [(spread(now[j : j + 1]), spread(side[j : j + 1])) for j in range(8)]
        cr, ci = invert_eight(cr, ci)
        out = sum(cr[j] * rows[j][0] + ci[j] * rows[j][1] for j in range(8))
        turn = sum(cr[j] * rows[j][1] - ci[j] * rows[j][0] for j in range(8))
        for h in range(4):
            x = jnp.where(inside, 0.0, parts[h])
            for j in range(8):
                x = x - (
                    wide_r[h][j] * spread(out[j : j + 1]) + wide_i[h][j] * spread(turn[j : j + 1])
                )
            m[8 * h : 8 * h + 8, :] = x
        m[pl.ds(o, 8), :] = out
        return 0

    lax.fori_loop(0, 4, group, 0)


def sweep(B, ar, ai, m):
    b = BLOCK
    for e in range(B):
        ar[e, :, N:] = jnp.zeros((N, WIDE - N), jnp.float32)
        ai[e, :, N:] = jnp.zeros((N, WIDE - N), jnp.float32)
    lane = lax.broadcasted_iota(jnp.int32, (b, WIDE), 1)
    row = lax.broadcasted_iota(jnp.int32, (b, WIDE), 0)
    l128 = lax.broadcasted_iota(jnp.int32, (b, 128), 1)
    r128 = lax.broadcasted_iota(jnp.int32, (b, 128), 0)
    quarter = l128 // 32

    def step(k, _):
        o = pl.multiple_of(k * b, b)
        rows = [(ar[e, pl.ds(o, b), :], ai[e, pl.ds(o, b), :]) for e in range(B)]
        q = jnp.where((lax.rem(quarter, 2) == 0) & (l128 - 32 * quarter == r128), 1.0, 0.0)
        for e in range(B):
            for part in range(2):
                turn = lax.rem(WIDE - o + 64 * e + 32 * part, WIDE)
                q = jnp.where(
                    quarter == 2 * e + part, pltpu.roll(rows[e][part], turn, 1)[:, 0:128], q
                )
        m[...] = q
        small_inverse(m)
        q = m[...]
        for e in range(B):
            rr, ri = rows[e]
            dr = q[:, 64 * e : 64 * e + 32]
            di = q[:, 64 * e + 32 : 64 * e + 64]
            inside = (lane >= o) & (lane < o + b)
            eye = lane - o == row
            r2 = jnp.where(inside, jnp.where(eye, -1.0, 0.0), rr)
            i2 = jnp.where(inside, 0.0, ri)
            drh, drl = split(dr)
            dih, dil = split(di)
            r2h, r2l = split(r2)
            i2h, i2l = split(i2)
            lhs = jnp.concatenate([drh, dih, drl, dil, drh, dih], 0)
            Rr = tn(lhs, jnp.concatenate([r2h, -i2h, r2h, -i2h, r2l, -i2l], 0))
            Ri = tn(lhs, jnp.concatenate([i2h, r2h, i2h, r2h, i2l, r2l], 0))
            Rrh, Rrl = split(Rr)
            Rih, Ril = split(Ri)
            rh, rl = split(rr)
            ih, il = split(ri)
            lhs = jnp.concatenate([rh, ih, rl, il, rh, ih], 0)[:, 0:N]
            Ur = tn(lhs, jnp.concatenate([Rrh, -Rih, Rrh, -Rih, Rrl, -Ril], 0))
            Ui = tn(lhs, jnp.concatenate([Rih, Rrh, Rih, Rrh, Ril, Rrl], 0))
            wide = lax.broadcasted_iota(jnp.int32, (N, WIDE), 1)
            strip = (wide >= o) & (wide < o + b)
            ar[e] = jnp.where(strip, 0.0, ar[e]) - Ur
            ai[e] = jnp.where(strip, 0.0, ai[e]) - Ui
            ar[e, pl.ds(o, b), :] = Rr
            ai[e, pl.ds(o, b), :] = Ri
        return 0

    lax.fori_loop(0, N // b, step, 0)


def nn(a, b):
    return jnp.dot(a, b, preferred_element_type=jnp.float32)


def nt(a, b):
    return lax.dot_general(a, b, (((1,), (1,)), ((), ())), preferred_element_type=jnp.float32)


def three(dot, a, b):
    return dot(a[0], b[0]) + (dot(a[0], b[1]) + dot(a[1], b[0]))


def csplit(x):
    return split(x[0]), split(x[1])


def cdot(dot, a, b):
    re = three(dot, a[0], b[0]) - three(dot, a[1], b[1])
    im = three(dot, a[0], b[1]) + three(dot, a[1], b[0])
    return re, im


def real_left(dot, a, b):
    return three(dot, a, b[0]), three(dot, a, b[1])


def real_right(dot, a, b):
    return three(dot, a[0], b), three(dot, a[1], b)


def put(ref, x):
    ref[0] = x[0]
    ref[1] = x[1]


def get(ref):
    return ref[0], ref[1]


def neg(x):
    return -x[0], -x[1]


def add(x, y):
    return x[0] + y[0], x[1] + y[1]


def sub(x, y):
    return x[0] - y[0], x[1] - y[1]


def pack(ref, x):
    ref[0] = x[0][:, 0:128]
    ref[1] = x[1][:, 0:128]
    ref[2] = jnp.concatenate([x[0][:, 128:N], x[1][:, 128:N]], axis=1)


def unpack(ref):
    rest = ref[2]
    return (
        jnp.concatenate([ref[0], rest[:, 0:64]], axis=1),
        jnp.concatenate([ref[1], rest[:, 64:128]], axis=1),
    )


def call(body, name, cost, outs, args, scratch=(), scalars=0):
    return pl.pallas_call(
        body,
        out_shape=tuple(jax.ShapeDtypeStruct(s, jnp.float32) for s in outs),
        in_specs=[pl.BlockSpec(memory_space=pltpu.SMEM)] * scalars
        + [pl.BlockSpec(memory_space=pltpu.VMEM)] * (len(args) - scalars),
        out_specs=tuple(pl.BlockSpec(memory_space=pltpu.VMEM) for _ in outs),
        scratch_shapes=list(scratch),
        name=name,
        cost_estimate=pl.CostEstimate(
            flops=int(cost * 1.1e9), bytes_accessed=1 << 20, transcendentals=0
        ),
    )(*args)


MATRIX = (2, N, N)
PACKED = (3, N, 128)
VECTOR = (2, N, COLS)
MESSAGE = (5, N, 128)


def work(B):
    return [pltpu.VMEM((B, N, WIDE), jnp.float32)] * 2 + [pltpu.VMEM((BLOCK, 128), jnp.float32)]


def first_body(onsite, hop, dre, dim, xa, p1, p3, q0, tl1, tu1, ar, ai, m):
    row = lax.broadcasted_iota(jnp.int32, (N, N), 0)
    col = lax.broadcasted_iota(jnp.int32, (N, N), 1)
    eye = row == col

    def block(i):
        return (
            jnp.where(eye, dre[i : i + 1, :], 0.0) - onsite[...],
            jnp.where(eye, dim[i : i + 1, :], 0.0),
        )

    for e in range(2):
        re, im = block(2 * e)
        ar[e, :, 0:N] = re
        ai[e, :, 0:N] = im
    sweep(2, ar, ai, m)
    h = split(hop[...])
    ht = split(hop[...].T)
    got = []
    for e in range(2):
        x = (-ar[e, :, 0:N], -ai[e, :, 0:N])
        put(xa.at[e], x)
        xs = csplit(x)
        up = csplit(real_left(nn, h, xs))
        down = csplit(real_left(nn, ht, xs))
        got.append((up, down))
    (up0, down0), (up2, down2) = got
    one = sub(sub(block(1), real_right(nn, down0, h)), real_right(nn, up2, ht))
    put(p1, one)
    put(p3, sub(block(3), real_right(nn, down2, h)))
    put(q0, real_right(nn, up0, ht))
    put(tl1, neg(real_right(nn, up0, h)))
    put(tu1, neg(real_right(nn, down2, ht)))


def first_rhs_body(xa, hop, r, ia, r1, r3, s0):
    h = split(hop[...])
    ht = split(hop[...].T)
    a = cdot(nn, csplit(get(xa.at[0])), csplit((r[0, 0], r[0, 1])))
    c = cdot(nn, csplit(get(xa.at[1])), csplit((r[2, 0], r[2, 1])))
    put(ia.at[0], a)
    put(ia.at[1], c)
    a = csplit(a)
    c = csplit(c)
    put(r1, add((r[1, 0], r[1, 1]), add(real_left(nn, ht, a), real_left(nn, h, c))))
    put(r3, add((r[3, 0], r[3, 1]), real_left(nn, ht, c)))
    put(s0, real_left(nn, h, a))


def second_body(p1, p3, q0, tl1, tu1, x1, z, p3n, pm, om, tl3, ar, ai, m):
    ar[0, :, 0:N] = p1[0]
    ai[0, :, 0:N] = p1[1]
    sweep(1, ar, ai, m)
    x = (-ar[0, :, 0:N], -ai[0, :, 0:N])
    put(x1, x)
    xs = csplit(x)
    tl = csplit(get(tl1))
    tu = csplit(get(tu1))
    zl = cdot(nn, tl, xs)
    zu = cdot(nn, tu, xs)
    put(z.at[0], zl)
    put(z.at[1], zu)
    zl = csplit(zl)
    zu = csplit(zu)
    put(p3n, sub(get(p3), cdot(nt, zu, tu)))
    pack(pm, add(get(q0), cdot(nt, zl, tl)))
    pack(tl3, neg(cdot(nt, zl, tu)))
    pack(om, neg(cdot(nt, zu, tl)))


def second_rhs_body(x1, z, tl1, tu1, r1, r3, s0, i1, yl, yu, r3n, rm):
    xs = csplit(get(x1))
    r = csplit(get(r1))
    put(i1, cdot(nn, xs, r))
    put(r3n, sub(get(r3), cdot(nn, csplit(get(z.at[1])), r)))
    put(rm, sub(cdot(nn, csplit(get(z.at[0])), r), get(s0)))
    put(yl, cdot(nt, xs, csplit(get(tl1))))
    put(yu, cdot(nt, xs, csplit(get(tu1))))


def invert_body(count, *refs):
    p, got = refs[0], refs[1 : 1 + count]
    pn, x, ar, ai, m = refs[1 + count :]
    now = get(p)
    for one in got:
        now = sub(now, unpack(one))
    put(pn, now)
    ar[0, :, 0:N] = now[0]
    ai[0, :, 0:N] = now[1]
    sweep(1, ar, ai, m)
    put(x, (-ar[0, :, 0:N], -ai[0, :, 0:N]))


def pivot_body(x, tl, tu, z, below, above):
    xs = csplit(get(x))
    tls = csplit(unpack(tl))
    tus = csplit(unpack(tu))
    zl = cdot(nn, tls, xs)
    zu = cdot(nn, tus, xs)
    put(z.at[0], zl)
    put(z.at[1], zu)
    pack(below, cdot(nt, csplit(zu), tus))
    pack(above, cdot(nt, csplit(zl), tls))


def rest_body(count, z, tl, tu, r, *refs):
    got, (rn, below, above) = refs[:count], refs[count:]
    now = get(r)
    for one in got:
        now = sub(now, (one[3], one[4]))
    put(rn, now)
    zl = csplit(get(z.at[0]))
    zu = csplit(get(z.at[1]))
    pack(below, neg(cdot(nt, zl, csplit(unpack(tu)))))
    pack(above, neg(cdot(nt, zu, csplit(unpack(tl)))))
    now = csplit(now)
    put(below.at[pl.ds(3, 2)], cdot(nn, zu, now))
    put(above.at[pl.ds(3, 2)], cdot(nn, zl, now))


def final_body(x, r, below, above, out):
    now = sub(sub(get(r), get(below)), get(above))
    put(out, cdot(nn, csplit(get(x)), csplit(now)))


def last_body(count, z, r, *refs):
    got, (rn, below, above) = refs[:count], refs[count:]
    now = get(r)
    for one in got:
        now = sub(now, (one[3], one[4]))
    put(rn, now)
    now = csplit(now)
    put(below, cdot(nn, csplit(get(z.at[1])), now))
    put(above, cdot(nn, csplit(get(z.at[0])), now))


def solve_pair(low, xa, ia, h, ht, first, second, out):
    t = add(real_left(nn, ht, csplit(first)), real_left(nn, h, csplit(second)))
    at = 1 - low
    x = xa[at, 0], xa[at, 1]
    put(out.at[0], add((ia[at, 0], ia[at, 1]), cdot(nn, csplit(x), csplit(t))))
    put(out.at[1], second)


def chosen_ends(low, prev, middle, last):
    pick = jnp.full((N, COLS), low, jnp.int32) == 1
    first = tuple(jnp.where(pick, a, b) for a, b in zip(prev, middle))
    second = tuple(jnp.where(pick, a, b) for a, b in zip(middle, last))
    return first, second


def back_body(odd, xa, ia, i1, yl, yu, hop, prev, x3, mid, out):
    last = get(x3)
    before = get(prev)
    one = sub(
        sub(get(i1), cdot(nn, csplit(get(yl)), csplit(before))),
        cdot(nn, csplit(get(yu)), csplit(last)),
    )
    put(mid, one)
    low = odd[0]
    first, second = chosen_ends(low, before, one, last)
    solve_pair(low, xa, ia, split(hop[...]), split(hop[...].T), first, second, out)


def own_body(odd, xa, ia, mid, hop, prev, x3, out):
    low = 1 - odd[0]
    first, second = chosen_ends(low, get(prev), get(mid), get(x3))
    solve_pair(low, xa, ia, split(hop[...]), split(hop[...].T), first, second, out)


def finish_body(side, mine, other, amplitude, density):
    for which, part in ((side[0], mine), (1 - side[0], other)):
        for slab in range(2):
            re, im = part[slab, 0], part[slab, 1]
            amplitude[slab, 0, which] = re
            amplitude[slab, 1, which] = im
            total = jnp.sum((re * re + im * im).T, axis=0, keepdims=True)
            density[slab, pl.ds(which, 1), :] = total


def per_device(
    source,
    onsite_block,
    hopping_block,
    potential_table,
    slab_profile,
    occupation,
    coupling,
    phonon_shift,
):
    slabs = lax.axis_size("slab")
    width = lax.axis_size("energy")
    energy_count = occupation.shape[1]
    place = lax.axis_index("slab")
    odd = lax.rem(place, 2)
    side = (lax.rem(place, 4) // 2 + odd + 1) % 2
    def pair(array, by=0):
        pairs = [
            (s * width + e, (s ^ 1) * width + e + by)
            for s in range(slabs)
            for e in range(width)
            if 0 <= e + by < width
        ]
        return lax.ppermute(array, ("slab", "energy"), pairs)

    def along(array, by):
        pairs = [(e, e + by) for e in range(width) if 0 <= e + by < width]
        return lax.ppermute(array, "energy", pairs)

    def shifted(array, groups):
        count = slabs // 2
        spot = lambda g, chain: 2 * g + ((1 - chain) if g % 2 == 0 else chain)
        pairs = [
            (spot(g, chain), spot(g + groups, chain))
            for g in range(count)
            for chain in range(2)
            if 0 <= g + groups < count
        ]
        return lax.ppermute(array, "slab", pairs)

    def in_order(own, other):
        return jnp.where(
            odd == 1, jnp.concatenate([other, own], axis=0), jnp.concatenate([own, other], axis=0)
        )

    chosen = (
        slab_profile[:, None] == jnp.arange(potential_table.shape[0], dtype=jnp.int32)[None, :]
    ).astype(jnp.float32)
    potential = jnp.matmul(chosen, potential_table, precision=lax.Precision.HIGHEST)
    own = jnp.concatenate([along(occupation, 1), occupation, along(occupation, -1)], axis=1)
    middle = pair(jnp.concatenate([occupation, potential[:, None, :]], axis=1))
    other = jnp.concatenate(
        [pair(occupation, 1), middle[:, :energy_count], pair(occupation, -1)], axis=1
    )
    occupied = in_order(own, other)
    potential = in_order(potential, middle[:, energy_count])
    points = jnp.arange(3 * energy_count, dtype=jnp.int32)
    weights = jnp.zeros((3 * energy_count,), jnp.float32)
    for mode in range(phonon_shift.shape[0]):
        above = (points == side + energy_count + phonon_shift[mode]).astype(jnp.float32)
        below = (points == side + energy_count - phonon_shift[mode]).astype(jnp.float32)
        weights = weights + coupling[mode] * (above + below)
    damping = jnp.sum(weights[None, :, None] * occupied, axis=1)
    point = lax.axis_index("energy") * energy_count + side
    dre = energy_low + energy_step * point.astype(jnp.float32) - potential
    dim = broadening + damping

    kept = lax.dynamic_index_in_dim(source, side, 2, keepdims=False)
    given = lax.dynamic_index_in_dim(source, 1 - side, 2, keepdims=False)
    right = in_order(kept, pair(given))

    xa, p1, p3, q0, tl1, tu1 = call(
        first_body,
        "first",
        14,
        [(2,) + MATRIX] + [MATRIX] * 5,
        (onsite_block, hopping_block, dre, dim),
        work(2),
    )
    ia, r1, r3, s0 = call(
        first_rhs_body, "first_rhs", 4, [(2,) + VECTOR] + [VECTOR] * 3, (xa, hopping_block, right)
    )
    x1, z1, p, pm, om, tl = call(
        second_body,
        "second",
        14,
        [MATRIX, (2,) + MATRIX, MATRIX, PACKED, PACKED, PACKED],
        (p1, p3, q0, tl1, tu1),
        work(1),
    )
    got_p = [shifted(pm, -1)]
    i1, yl, yu, r, rm = call(
        second_rhs_body,
        "second_rhs",
        4,
        [VECTOR, MATRIX, MATRIX, VECTOR, VECTOR],
        (x1, z1, tl1, tu1, r1, r3, s0),
    )
    message = shifted(jnp.concatenate([om, rm], axis=0), -1)
    got_m = [message]
    tu = message
    groups = slabs // 2
    levels = (groups - 1).bit_length()
    for level in range(levels):
        distance = 1 << level
        p, x = call(
            functools.partial(invert_body, len(got_p)),
            "invert",
            12,
            [MATRIX, MATRIX],
            (p, *got_p),
            work(1),
        )
        z, below, above = call(
            pivot_body, "pivot", 4, [(2,) + MATRIX, PACKED, PACKED], (x, tl, tu)
        )
        got_p = [shifted(below, distance), shifted(above, -distance)]
        if level < levels - 1:
            r, below, above = call(
                functools.partial(rest_body, len(got_m)),
                "rest",
                4,
                [VECTOR, MESSAGE, MESSAGE],
                (z, tl, tu, r, *got_m),
            )
        else:
            r, below, above = call(
                functools.partial(last_body, len(got_m)), "last", 2, [VECTOR] * 3, (z, r, *got_m)
            )
        tl = shifted(below, distance)
        tu = shifted(above, -distance)
        got_m = [tl, tu]
    p, x = call(
        functools.partial(invert_body, len(got_p)),
        "invert",
        12,
        [MATRIX, MATRIX],
        (p, *got_p),
        work(1),
    )
    (x3,) = call(final_body, "final", 2, [VECTOR], (x, r, *got_m))
    prev = shifted(x3, 1)
    low = jnp.reshape(odd, (1,))
    mid, sent = call(
        back_body,
        "back",
        3,
        [VECTOR, (2,) + VECTOR],
        (low, xa, ia, i1, yl, yu, hopping_block, prev, x3),
        scalars=1,
    )
    back = pair(sent)
    (mine,) = call(
        own_body,
        "own",
        2,
        [(2,) + VECTOR],
        (low, xa, ia, mid, hopping_block, prev, x3),
        scalars=1,
    )
    return call(
        finish_body,
        "finish",
        2,
        [source.shape, occupation.shape],
        (jnp.reshape(side, (1,)), mine, back),
        scalars=1,
    )


def solution(mesh):
    placed = (
        P("slab", None, "energy", None, None),
        P(),
        P(),
        P(),
        P("slab"),
        P("slab", "energy", None),
        P(),
        P(),
    )
    return jax.shard_map(
        per_device,
        mesh=mesh,
        in_specs=placed,
        out_specs=(P("slab", None, "energy", None, None), P("slab", "energy", None)),
        check_vma=False,
    )
```

profile of v0, /device:TPU:32, one launch (start us, length us, event | category | flops | bytes accessed | tf_op | source)
XLA Modules:
  0.0 227.8 jit_solution(1091678509893383616)
XLA Ops:
  2.6 3.0 %collective-permute-start.3 = (f32[2,2,192]{2,0,1:T(2,128)S(1)}, f32[2,2,192]{2,0,1:T(2,128)S(1)}, u32[]{:S(2)}, u32[]{:S(2)}) collective-permute-start(f32[2,2,192]{2,0,1:T(2,128)S(1)} %copy.10), channel_id=1, source_target_pairs={{0,1},{1,2},{2,3},{3,4},{4,5},{5,6},{6,7},{8,9},{9,10},{10,11},{11... | collective-permute-start | bytes 9224 | tf_op jit(solution)/shard_map/ppermute | solution.py:445
  7.0 4.8 %collective-permute-start.1 = (f32[2,2,192]{2,0,1:T(2,128)S(1)}, f32[2,2,192]{2,0,1:T(2,128)S(1)}, u32[]{:S(2)}, u32[]{:S(2)}) collective-permute-start(f32[2,2,192]{2,0,1:T(2,128)S(1)} %copy.10), channel_id=1, source_target_pairs={{0,9},{1,10},{2,11},{3,12},{4,13},{5,14},{6,15},{8,1},{9,2},{10,3}... | collective-permute-start | bytes 9224 | tf_op jit(solution)/shard_map/ppermute | solution.py:441
  27.1 15.2 %first.1 = (f32[2,2,192,192]{3,2,1,0:T(8,128)}, f32[2,192,192]{2,1,0:T(8,128)}, f32[2,192,192]{2,1,0:T(8,128)}, f32[2,192,192]{2,1,0:T(8,128)}, f32[2,192,192]{2,1,0:T(8,128)}, /*index=5*/f32[2,192,192]{2,1,0:T(8,128)}) custom-call(f32[192,192]{1,0:T(8,128)} %onsite.1, f32[192,192]{1,0:T(8,128)} %hop.7, f32[4,192]{1,0:T(4,128)} %fusion.2.dre, ...), custom_call_target="tpu_custom_call" | custom-call | flops 15399999488 | bytes 1048576 | tf_op jit(solution)/shard_map/first/pallas_call | solution.py:214
  42.3 14.6 %second.1 = (f32[2,192,192]{2,1,0:T(8,128)}, f32[2,2,192,192]{3,2,1,0:T(8,128)}, f32[2,192,192]{2,1,0:T(8,128)}, f32[3,192,128]{2,1,0:T(8,128)}, f32[3,192,128]{2,1,0:T(8,128)}, /*index=5*/f32[3,192,128]{2,1,0:T(8,128)}) custom-call(f32[2,192,192]{2,1,0:T(8,128)} %get-tuple-element.52.p1, f32[2,192,192]{2,1,0:T(8,128)} %get-tuple-element.53.p3, ...), custom_call_target="tpu_custom_call" | custom-call | flops 15399999488 | bytes 1048576 | tf_op jit(solution)/shard_map/second/pallas_call | solution.py:214
  56.9 3.9 %collective-permute-start.6 = (f32[3,192,128]{2,1,0:T(8,128)}, f32[3,192,128]{2,1,0:T(8,128)S(1)}, u32[]{:S(2)}, u32[]{:S(2)}) collective-permute-start(f32[3,192,128]{2,1,0:T(8,128)} %get-tuple-element.66), channel_id=1, source_target_pairs={{16,8},{24,0},{40,16},{32,24},{48,40},{56,32},{72,48},{64,56},{80,... | collective-permute-start | bytes 884744 | tf_op jit(solution)/shard_map/ppermute | solution.py:456
  61.8 3.6 %first_rhs.1 = (f32[2,2,192,128]{3,2,1,0:T(8,128)}, f32[2,192,128]{2,1,0:T(8,128)}, f32[2,192,128]{2,1,0:T(8,128)}, f32[2,192,128]{2,1,0:T(8,128)}) custom-call(f32[2,2,192,192]{3,2,1,0:T(8,128)} %get-tuple-element.50.xa, f32[192,192]{1,0:T(8,128)} %hop.7, f32[4,2,192,128]{3,2,1,0:T(8,128)} %maximum_select_fusion.r), custom_call_target="tpu_custom_call" | custom-call | flops 4400000000 | bytes 1048576 | tf_op jit(solution)/shard_map/first_rhs/pallas_call | solution.py:214
  65.4 4.1 %second_rhs.1 = (f32[2,192,128]{2,1,0:T(8,128)}, f32[2,192,192]{2,1,0:T(8,128)}, f32[2,192,192]{2,1,0:T(8,128)}, f32[2,192,128]{2,1,0:T(8,128)}, f32[2,192,128]{2,1,0:T(8,128)}) custom-call(f32[2,192,192]{2,1,0:T(8,128)} %get-tuple-element.57.x1, f32[2,2,192,192]{3,2,1,0:T(8,128)} %get-tuple-element.58.z, f32[2,192,192]{2,1,0:T(8,128)} %get-tuple-element.55.tl1, ...), custom_call_target="tpu_custom_call" | custom-call | flops 4400000000 | bytes 1048576 | tf_op jit(solution)/shard_map/second_rhs/pallas_call | solution.py:214
  70.5 2.7 %collective-permute-start.7 = (f32[5,192,128]{2,1,0:T(8,128)S(1)}, f32[5,192,128]{2,1,0:T(8,128)S(1)}, u32[]{:S(2)}, u32[]{:S(2)}) collective-permute-start(f32[5,192,128]{2,1,0:T(8,128)S(1)} %pad_maximum_fusion), channel_id=1, source_target_pairs={{16,8},{24,0},{40,16},{32,24},{48,40},{56,32},{72,48},{64,56},{80,... | collective-permute-start | bytes 1474568 | tf_op jit(solution)/shard_map/ppermute | solution.py:456
  73.9 12.1 %invert.4 = (f32[2,192,192]{2,1,0:T(8,128)}, f32[2,192,192]{2,1,0:T(8,128)}) custom-call(f32[2,192,192]{2,1,0:T(8,128)} %get-tuple-element.65.refs_0_, f32[3,192,128]{2,1,0:T(8,128)} %copy-done.11), custom_call_target="tpu_custom_call" | custom-call | flops 13200000000 | bytes 1048576 | tf_op jit(solution)/shard_map/invert/pallas_call | solution.py:214
  88.3 3.5 %pivot.3 = (f32[2,2,192,192]{3,2,1,0:T(8,128)}, f32[3,192,128]{2,1,0:T(8,128)}, f32[3,192,128]{2,1,0:T(8,128)}) custom-call(f32[2,192,192]{2,1,0:T(8,128)} %get-tuple-element.68.x, f32[3,192,128]{2,1,0:T(8,128)} %get-tuple-element.69.tl, f32[5,192,128]{2,1,0:T(8,128)} %copy-done.9), custom_call_target="tpu_custom_call" | custom-call | flops 4400000000 | bytes 1048576 | tf_op jit(solution)/shard_map/pivot/pallas_call | solution.py:214
  91.8 4.2 %collective-permute-start.8 = (f32[3,192,128]{2,1,0:T(8,128)}, f32[3,192,128]{2,1,0:T(8,128)S(1)}, u32[]{:S(2)}, u32[]{:S(2)}) collective-permute-start(f32[3,192,128]{2,1,0:T(8,128)} %get-tuple-element.72), channel_id=1, source_target_pairs={{8,16},{0,24},{16,40},{24,32},{40,48},{32,56},{48,72},{56,64},{72,... | collective-permute-start | bytes 884744 | tf_op jit(solution)/shard_map/ppermute | solution.py:456
  96.0 3.8 %collective-permute-start.9 = (f32[3,192,128]{2,1,0:T(8,128)}, f32[3,192,128]{2,1,0:T(8,128)S(1)}, u32[]{:S(2)}, u32[]{:S(2)}) collective-permute-start(f32[3,192,128]{2,1,0:T(8,128)} %get-tuple-element.73), channel_id=1, source_target_pairs={{16,8},{24,0},{40,16},{32,24},{48,40},{56,32},{72,48},{64,56},{80,... | collective-permute-start | bytes 884744 | tf_op jit(solution)/shard_map/ppermute | solution.py:456
  99.7 3.9 %rest.2 = (f32[2,192,128]{2,1,0:T(8,128)}, f32[5,192,128]{2,1,0:T(8,128)}, f32[5,192,128]{2,1,0:T(8,128)}) custom-call(f32[2,2,192,192]{3,2,1,0:T(8,128)} %get-tuple-element.76.z, f32[3,192,128]{2,1,0:T(8,128)} %get-tuple-element.69.tl, f32[5,192,128]{2,1,0:T(8,128)} %copy-done.9, f32[2,192,128]{2,1,0:T(8,128)} %get-tuple-element.77.r, f32[5,192,128]{2,1,0:T(8,128)} %copy-done.9), custom_call_target="tpu_custom_call" | custom-call | flops 4400000000 | bytes 1048576 | tf_op jit(solution)/shard_map/rest/pallas_call | solution.py:214
  103.6 3.3 %collective-permute-start.10 = (f32[5,192,128]{2,1,0:T(8,128)}, f32[5,192,128]{2,1,0:T(8,128)S(1)}, u32[]{:S(2)}, u32[]{:S(2)}) collective-permute-start(f32[5,192,128]{2,1,0:T(8,128)} %get-tuple-element.78), channel_id=1, source_target_pairs={{8,16},{0,24},{16,40},{24,32},{40,48},{32,56},{48,72},{56,64},{72,... | collective-permute-start | bytes 1474568 | tf_op jit(solution)/shard_map/ppermute | solution.py:456
  106.9 4.8 %collective-permute-start.11 = (f32[5,192,128]{2,1,0:T(8,128)}, f32[5,192,128]{2,1,0:T(8,128)S(1)}, u32[]{:S(2)}, u32[]{:S(2)}) collective-permute-start(f32[5,192,128]{2,1,0:T(8,128)} %get-tuple-element.79), channel_id=1, source_target_pairs={{16,8},{24,0},{40,16},{32,24},{48,40},{56,32},{72,48},{64,56},{80,... | collective-permute-start | bytes 1474568 | tf_op jit(solution)/shard_map/ppermute | solution.py:456
  113.4 12.2 %invert.5 = (f32[2,192,192]{2,1,0:T(8,128)}, f32[2,192,192]{2,1,0:T(8,128)}) custom-call(f32[2,192,192]{2,1,0:T(8,128)} %get-tuple-element.67.refs_0_, f32[3,192,128]{2,1,0:T(8,128)} %copy-done.14, f32[3,192,128]{2,1,0:T(8,128)} %copy-done.17), custom_call_target="tpu_custom_call" | custom-call | flops 13200000000 | bytes 1048576 | tf_op jit(solution)/shard_map/invert/pallas_call | solution.py:214
  125.6 7.2 %collective-permute-done.11.tu.refs_1_ = f32[5,192,128]{2,1,0:T(8,128)S(1)} collective-permute-done((f32[5,192,128]{2,1,0:T(8,128)}, f32[5,192,128]{2,1,0:T(8,128)S(1)}, u32[]{:S(2)}, u32[]{:S(2)}) %collective-permute-start.11) | collective-permute-done | bytes 491552 | tf_op jit(solution)/shard_map/ppermute | solution.py:456
  133.7 3.6 %pivot.4 = (f32[2,2,192,192]{3,2,1,0:T(8,128)}, f32[3,192,128]{2,1,0:T(8,128)}, f32[3,192,128]{2,1,0:T(8,128)}) custom-call(f32[2,192,192]{2,1,0:T(8,128)} %get-tuple-element.75.x, f32[5,192,128]{2,1,0:T(8,128)} %copy-done.5, f32[5,192,128]{2,1,0:T(8,128)} %copy-done.7), custom_call_target="tpu_custom_call" | custom-call | flops 4400000000 | bytes 1048576 | tf_op jit(solution)/shard_map/pivot/pallas_call | solution.py:214
  137.2 3.8 %collective-permute-start.12 = (f32[3,192,128]{2,1,0:T(8,128)}, f32[3,192,128]{2,1,0:T(8,128)S(1)}, u32[]{:S(2)}, u32[]{:S(2)}) collective-permute-start(f32[3,192,128]{2,1,0:T(8,128)} %get-tuple-element.80), channel_id=1, source_target_pairs={{8,40},{0,32},{16,48},{24,56},{40,72},{32,64},{48,80},{56,88},{72,... | collective-permute-start | bytes 884744 | tf_op jit(solution)/shard_map/ppermute | solution.py:456
  143.1 4.1 %rest.3 = (f32[2,192,128]{2,1,0:T(8,128)}, f32[5,192,128]{2,1,0:T(8,128)}, f32[5,192,128]{2,1,0:T(8,128)}) custom-call(f32[2,2,192,192]{3,2,1,0:T(8,128)} %get-tuple-element.84.z, f32[5,192,128]{2,1,0:T(8,128)} %copy-done.5, f32[5,192,128]{2,1,0:T(8,128)} %copy-done.7, f32[2,192,128]{2,1,0:T(8,128)} %get-tuple-element.85.r, f32[5,192,128]{2,1,0:T(8,128)} %copy-done.5, ...), custom_call_target="tpu_custom_call" | custom-call | flops 4400000000 | bytes 1048576 | tf_op jit(solution)/shard_map/rest/pallas_call | solution.py:214
  147.2 3.8 %collective-permute-start.14 = (f32[5,192,128]{2,1,0:T(8,128)}, f32[5,192,128]{2,1,0:T(8,128)S(1)}, u32[]{:S(2)}, u32[]{:S(2)}) collective-permute-start(f32[5,192,128]{2,1,0:T(8,128)} %get-tuple-element.86), channel_id=1, source_target_pairs={{8,40},{0,32},{16,48},{24,56},{40,72},{32,64},{48,80},{56,88},{72,... | collective-permute-start | bytes 1474568 | tf_op jit(solution)/shard_map/ppermute | solution.py:456
  153.9 12.2 %invert.6 = (f32[2,192,192]{2,1,0:T(8,128)}, f32[2,192,192]{2,1,0:T(8,128)}) custom-call(f32[2,192,192]{2,1,0:T(8,128)} %get-tuple-element.74.refs_0_, f32[3,192,128]{2,1,0:T(8,128)} %copy-done.12, f32[3,192,128]{2,1,0:T(8,128)} %copy-done.15), custom_call_target="tpu_custom_call" | custom-call | flops 13200000000 | bytes 1048576 | tf_op jit(solution)/shard_map/invert/pallas_call | solution.py:214
  167.1 3.6 %pivot.5 = (f32[2,2,192,192]{3,2,1,0:T(8,128)}, f32[3,192,128]{2,1,0:T(8,128)}, f32[3,192,128]{2,1,0:T(8,128)}) custom-call(f32[2,192,192]{2,1,0:T(8,128)} %get-tuple-element.83.x, f32[5,192,128]{2,1,0:T(8,128)} %copy-done.6, f32[5,192,128]{2,1,0:T(8,128)} %copy-done.8), custom_call_target="tpu_custom_call" | custom-call | flops 4400000000 | bytes 1048576 | tf_op jit(solution)/shard_map/pivot/pallas_call | solution.py:214
  170.7 3.3 %collective-permute-start.16 = (f32[3,192,128]{2,1,0:T(8,128)}, f32[3,192,128]{2,1,0:T(8,128)S(1)}, u32[]{:S(2)}, u32[]{:S(2)}) collective-permute-start(f32[3,192,128]{2,1,0:T(8,128)} %get-tuple-element.88), channel_id=1, source_target_pairs={{8,72},{0,64},{16,80},{24,88},{40,104},{32,96},{48,112},{56,120},{... | collective-permute-start | bytes 884744 | tf_op jit(solution)/shard_map/ppermute | solution.py:456
  175.3 3.0 %last.1 = (f32[2,192,128]{2,1,0:T(8,128)}, f32[2,192,128]{2,1,0:T(8,128)}, f32[2,192,128]{2,1,0:T(8,128)}) custom-call(f32[2,2,192,192]{3,2,1,0:T(8,128)} %get-tuple-element.91.z, f32[2,192,128]{2,1,0:T(8,128)} %get-tuple-element.92.r, f32[5,192,128]{2,1,0:T(8,128)} %copy-done.6, f32[5,192,128]{2,1,0:T(8,128)} %copy-done.8), custom_call_target="tpu_custom_call" | custom-call | flops 2200000000 | bytes 1048576 | tf_op jit(solution)/shard_map/last/pallas_call | solution.py:214
  178.3 6.1 %collective-permute-start.18 = (f32[2,192,128]{2,1,0:T(8,128)}, f32[2,192,128]{2,1,0:T(8,128)S(1)}, u32[]{:S(2)}, u32[]{:S(2)}) collective-permute-start(f32[2,192,128]{2,1,0:T(8,128)} %get-tuple-element.94), channel_id=1, source_target_pairs={{8,72},{0,64},{16,80},{24,88},{40,104},{32,96},{48,112},{56,120},{... | collective-permute-start | bytes 589832 | tf_op jit(solution)/shard_map/ppermute | solution.py:456
  186.5 12.2 %invert.7 = (f32[2,192,192]{2,1,0:T(8,128)}, f32[2,192,192]{2,1,0:T(8,128)}) custom-call(f32[2,192,192]{2,1,0:T(8,128)} %get-tuple-element.82.refs_0_, f32[3,192,128]{2,1,0:T(8,128)} %copy-done.13, f32[3,192,128]{2,1,0:T(8,128)} %copy-done.16), custom_call_target="tpu_custom_call" | custom-call | flops 13200000000 | bytes 1048576 | tf_op jit(solution)/shard_map/invert/pallas_call | solution.py:214
  201.9 3.7 %collective-permute-start.20 = (f32[2,192,128]{2,1,0:T(8,128)}, f32[2,192,128]{2,1,0:T(8,128)S(1)}, u32[]{:S(2)}, u32[]{:S(2)}) collective-permute-start(f32[2,192,128]{2,1,0:T(8,128)} %final.1.x3), channel_id=1, source_target_pairs={{8,16},{0,24},{16,40},{24,32},{40,48},{32,56},{48,72},{56,64},{72,... | collective-permute-start | bytes 589832 | tf_op jit(solution)/shard_map/ppermute | solution.py:456
  205.5 6.2 %collective-permute-done.20.prev = f32[2,192,128]{2,1,0:T(8,128)S(1)} collective-permute-done((f32[2,192,128]{2,1,0:T(8,128)}, f32[2,192,128]{2,1,0:T(8,128)S(1)}, u32[]{:S(2)}, u32[]{:S(2)}) %collective-permute-start.20) | collective-permute-done | bytes 196640 | tf_op jit(solution)/shard_map/ppermute | solution.py:456
  212.4 4.5 %back.1 = (f32[2,192,128]{2,1,0:T(8,128)}, f32[2,2,192,128]{3,2,1,0:T(8,128)}) custom-call(s32[1]{0:T(128)} %bitcast.1.odd, f32[2,2,192,192]{3,2,1,0:T(8,128)} %get-tuple-element.50.xa, f32[2,2,192,128]{3,2,1,0:T(8,128)} %get-tuple-element.51.ia, f32[2,192,128]{2,1,0:T(8,128)} %get-tuple-element.62.i1, f32[2,192,192]{2,1,0:T(8,128)} %get-tuple-element.63.yl, ...), custom_call_target="tpu_custom_call" | custom-call | flops 3300000000 | bytes 1048576 | tf_op jit(solution)/shard_map/back/pallas_call | solution.py:214
  216.9 3.2 %own.1.mine = f32[2,2,192,128]{3,2,1,0:T(8,128)} custom-call(s32[1]{0:T(128)} %bitcast.1.odd, f32[2,2,192,192]{3,2,1,0:T(8,128)} %get-tuple-element.50.xa, f32[2,2,192,128]{3,2,1,0:T(8,128)} %get-tuple-element.51.ia, f32[2,192,128]{2,1,0:T(8,128)} %get-tuple-element.96.mid, f32[192,192]{1,0:T(8,128)} %hop.7, f32[2,192,128]{2,1,0:T(8,128)} %copy-done.20, ...), custom_call_target="tpu_custom_call" | custom-call | flops 2200000000 | bytes 1048576 | tf_op jit(solution)/shard_map/own/pallas_call | solution.py:214
  220.1 4.9 %collective-permute-done.21.other = f32[2,2,192,128]{3,2,1,0:T(8,128)S(1)} collective-permute-done((f32[2,2,192,128]{3,2,1,0:T(8,128)}, f32[2,2,192,128]{3,2,1,0:T(8,128)S(1)}, u32[]{:S(2)}, u32[]{:S(2)}) %collective-permute-start.21) | collective-permute-done | bytes 393248 | tf_op jit(solution)/shard_map/ppermute | solution.py:441
  (91 shorter events, 36.5 us)
Async XLA Ops:
  0.6 11.2 %copy-start = (f32[16,192]{1,0:T(8,128)S(1)}, f32[16,192]{1,0:T(8,128)}, u32[]{:S(2)}) copy-start(f32[16,192]{1,0:T(8,128)} %param.11) | copy-start | bytes 36868
  0.6 11.2 %copy-start.21 = (s32[2]{0:T(128)S(1)}, s32[2]{0:T(128)}, u32[]{:S(2)}) copy-start(s32[2]{0:T(128)} %param.12) | copy-start | bytes 28
  1.4 24.4 %collective-permute-start.4 = (f32[2,2,192]{2,0,1:T(2,128)S(1)}, f32[2,2,192]{2,0,1:T(2,128)S(1)}, u32[]{:S(2)}, u32[]{:S(2)}) collective-permute-start(f32[2,2,192]{2,0,1:T(2,128)S(1)} %copy.10), channel_id=1, source_target_pairs={{1,0},{2,1},{3,2},{4,3},{5,4},{6,5},{7,6},{9,8},{10,9},{11,10},{12... | collective-permute-start | bytes 9224 | tf_op jit(solution)/shard_map/ppermute | solution.py:445
  2.6 22.0 %collective-permute-start.3 = (f32[2,2,192]{2,0,1:T(2,128)S(1)}, f32[2,2,192]{2,0,1:T(2,128)S(1)}, u32[]{:S(2)}, u32[]{:S(2)}) collective-permute-start(f32[2,2,192]{2,0,1:T(2,128)S(1)} %copy.10), channel_id=1, source_target_pairs={{0,1},{1,2},{2,3},{3,4},{4,5},{5,6},{6,7},{8,9},{9,10},{10,11},{11... | collective-permute-start | bytes 9224 | tf_op jit(solution)/shard_map/ppermute | solution.py:445
  5.7 20.1 %collective-permute-start.2 = (f32[2,2,192]{2,0,1:T(2,128)S(1)}, f32[2,2,192]{2,0,1:T(2,128)S(1)}, u32[]{:S(2)}, u32[]{:S(2)}) collective-permute-start(f32[2,2,192]{2,0,1:T(2,128)S(1)} %copy.10), channel_id=1, source_target_pairs={{1,8},{2,9},{3,10},{4,11},{5,12},{6,13},{7,14},{9,0},{10,1},{11,2}... | collective-permute-start | bytes 9224 | tf_op jit(solution)/shard_map/ppermute | solution.py:441
  7.0 18.8 %collective-permute-start.1 = (f32[2,2,192]{2,0,1:T(2,128)S(1)}, f32[2,2,192]{2,0,1:T(2,128)S(1)}, u32[]{:S(2)}, u32[]{:S(2)}) collective-permute-start(f32[2,2,192]{2,0,1:T(2,128)S(1)} %copy.10), channel_id=1, source_target_pairs={{0,9},{1,10},{2,11},{3,12},{4,13},{5,14},{6,15},{8,1},{9,2},{10,3}... | collective-permute-start | bytes 9224 | tf_op jit(solution)/shard_map/ppermute | solution.py:441
  12.0 13.7 %collective-permute-start = (f32[2,3,192]{2,0,1:T(2,128)S(1)}, f32[2,3,192]{2,0,1:T(2,128)S(1)}, u32[]{:S(2)}, u32[]{:S(2)}) collective-permute-start(f32[2,3,192]{2,0,1:T(2,128)S(1)} %pad_maximum_fusion.1), channel_id=1, source_target_pairs={{0,8},{1,9},{2,10},{3,11},{4,12},{5,13},{6,14},{7,15},{8,0},{9,1},... | collective-permute-start | bytes 13832 | tf_op jit(solution)/shard_map/ppermute | solution.py:441
  24.6 1.1 copy-start.2
  24.6 36.2 %collective-permute-start.5 = (f32[2,2,192,128]{3,2,1,0:T(8,128)S(1)}, f32[2,2,192,128]{3,2,1,0:T(8,128)S(1)}, u32[]{:S(2)}, u32[]{:S(2)}) collective-permute-start(f32[2,2,192,128]{3,2,1,0:T(8,128)S(1)} %get-tuple-element.98), channel_id=1, source_target_pairs={{0,8},{1,9},{2,10},{3,11},{4,12},{5,13},{6,14},{7,15},{8,0},{9,1},... | collective-permute-start | bytes 1179656 | tf_op jit(solution)/shard_map/ppermute | solution.py:441
  56.9 16.3 %collective-permute-start.6 = (f32[3,192,128]{2,1,0:T(8,128)}, f32[3,192,128]{2,1,0:T(8,128)S(1)}, u32[]{:S(2)}, u32[]{:S(2)}) collective-permute-start(f32[3,192,128]{2,1,0:T(8,128)} %get-tuple-element.66), channel_id=1, source_target_pairs={{16,8},{24,0},{40,16},{32,24},{48,40},{56,32},{72,48},{64,56},{80,... | collective-permute-start | bytes 884744 | tf_op jit(solution)/shard_map/ppermute | solution.py:456
  65.4 4.1 %copy-start.1 = (f32[3,192,128]{2,1,0:T(8,128)S(1)}, f32[3,192,128]{2,1,0:T(8,128)}, u32[]{:S(2)}) copy-start(f32[3,192,128]{2,1,0:T(8,128)} %get-tuple-element.70) | copy-start | bytes 884740
  70.5 17.0 %collective-permute-start.7 = (f32[5,192,128]{2,1,0:T(8,128)S(1)}, f32[5,192,128]{2,1,0:T(8,128)S(1)}, u32[]{:S(2)}, u32[]{:S(2)}) collective-permute-start(f32[5,192,128]{2,1,0:T(8,128)S(1)} %pad_maximum_fusion), channel_id=1, source_target_pairs={{16,8},{24,0},{40,16},{32,24},{48,40},{56,32},{72,48},{64,56},{80,... | collective-permute-start | bytes 1474568 | tf_op jit(solution)/shard_map/ppermute | solution.py:456
  91.8 20.0 %collective-permute-start.8 = (f32[3,192,128]{2,1,0:T(8,128)}, f32[3,192,128]{2,1,0:T(8,128)S(1)}, u32[]{:S(2)}, u32[]{:S(2)}) collective-permute-start(f32[3,192,128]{2,1,0:T(8,128)} %get-tuple-element.72), channel_id=1, source_target_pairs={{8,16},{0,24},{16,40},{24,32},{40,48},{32,56},{48,72},{56,64},{72,... | collective-permute-start | bytes 884744 | tf_op jit(solution)/shard_map/ppermute | solution.py:456
  96.0 16.7 %collective-permute-start.9 = (f32[3,192,128]{2,1,0:T(8,128)}, f32[3,192,128]{2,1,0:T(8,128)S(1)}, u32[]{:S(2)}, u32[]{:S(2)}) collective-permute-start(f32[3,192,128]{2,1,0:T(8,128)} %get-tuple-element.73), channel_id=1, source_target_pairs={{16,8},{24,0},{40,16},{32,24},{48,40},{56,32},{72,48},{64,56},{80,... | collective-permute-start | bytes 884744 | tf_op jit(solution)/shard_map/ppermute | solution.py:456
  103.6 22.0 %collective-permute-start.10 = (f32[5,192,128]{2,1,0:T(8,128)}, f32[5,192,128]{2,1,0:T(8,128)S(1)}, u32[]{:S(2)}, u32[]{:S(2)}) collective-permute-start(f32[5,192,128]{2,1,0:T(8,128)} %get-tuple-element.78), channel_id=1, source_target_pairs={{8,16},{0,24},{16,40},{24,32},{40,48},{32,56},{48,72},{56,64},{72,... | collective-permute-start | bytes 1474568 | tf_op jit(solution)/shard_map/ppermute | solution.py:456
  106.9 26.0 %collective-permute-start.11 = (f32[5,192,128]{2,1,0:T(8,128)}, f32[5,192,128]{2,1,0:T(8,128)S(1)}, u32[]{:S(2)}, u32[]{:S(2)}) collective-permute-start(f32[5,192,128]{2,1,0:T(8,128)} %get-tuple-element.79), channel_id=1, source_target_pairs={{16,8},{24,0},{40,16},{32,24},{48,40},{56,32},{72,48},{64,56},{80,... | collective-permute-start | bytes 1474568 | tf_op jit(solution)/shard_map/ppermute | solution.py:456
  111.8 0.9 copy-start.14
  125.6 7.2 %copy-start.5 = (f32[5,192,128]{2,1,0:T(8,128)}, f32[5,192,128]{2,1,0:T(8,128)S(1)}, u32[]{:S(2)}) copy-start(f32[5,192,128]{2,1,0:T(8,128)S(1)} %collective-permute-done.10.tl.refs_0_) | copy-start | bytes 1474564
  132.9 0.8 copy-start.7
  137.2 15.8 %collective-permute-start.12 = (f32[3,192,128]{2,1,0:T(8,128)}, f32[3,192,128]{2,1,0:T(8,128)S(1)}, u32[]{:S(2)}, u32[]{:S(2)}) collective-permute-start(f32[3,192,128]{2,1,0:T(8,128)} %get-tuple-element.80), channel_id=1, source_target_pairs={{8,40},{0,32},{16,48},{24,56},{40,72},{32,64},{48,80},{56,88},{72,... | collective-permute-start | bytes 884744 | tf_op jit(solution)/shard_map/ppermute | solution.py:456
  141.1 12.0 %collective-permute-start.13 = (f32[3,192,128]{2,1,0:T(8,128)}, f32[3,192,128]{2,1,0:T(8,128)S(1)}, u32[]{:S(2)}, u32[]{:S(2)}) collective-permute-start(f32[3,192,128]{2,1,0:T(8,128)} %get-tuple-element.81), channel_id=1, source_target_pairs={{40,8},{32,0},{48,16},{56,24},{72,40},{64,32},{80,48},{88,56},{104... | collective-permute-start | bytes 884744 | tf_op jit(solution)/shard_map/ppermute | solution.py:456
  147.2 19.0 %collective-permute-start.14 = (f32[5,192,128]{2,1,0:T(8,128)}, f32[5,192,128]{2,1,0:T(8,128)S(1)}, u32[]{:S(2)}, u32[]{:S(2)}) collective-permute-start(f32[5,192,128]{2,1,0:T(8,128)} %get-tuple-element.86), channel_id=1, source_target_pairs={{8,40},{0,32},{16,48},{24,56},{40,72},{32,64},{48,80},{56,88},{72,... | collective-permute-start | bytes 1474568 | tf_op jit(solution)/shard_map/ppermute | solution.py:456
  151.0 15.1 %collective-permute-start.15 = (f32[5,192,128]{2,1,0:T(8,128)}, f32[5,192,128]{2,1,0:T(8,128)S(1)}, u32[]{:S(2)}, u32[]{:S(2)}) collective-permute-start(f32[5,192,128]{2,1,0:T(8,128)} %get-tuple-element.87), channel_id=1, source_target_pairs={{40,8},{32,0},{48,16},{56,24},{72,40},{64,32},{80,48},{88,56},{104... | collective-permute-start | bytes 1474568 | tf_op jit(solution)/shard_map/ppermute | solution.py:456
  153.1 0.8 copy-start.15
  166.1 1.0 copy-start.8
  170.7 15.0 %collective-permute-start.16 = (f32[3,192,128]{2,1,0:T(8,128)}, f32[3,192,128]{2,1,0:T(8,128)S(1)}, u32[]{:S(2)}, u32[]{:S(2)}) collective-permute-start(f32[3,192,128]{2,1,0:T(8,128)} %get-tuple-element.88), channel_id=1, source_target_pairs={{8,72},{0,64},{16,80},{24,88},{40,104},{32,96},{48,112},{56,120},{... | collective-permute-start | bytes 884744 | tf_op jit(solution)/shard_map/ppermute | solution.py:456
  174.0 11.7 %collective-permute-start.17 = (f32[3,192,128]{2,1,0:T(8,128)}, f32[3,192,128]{2,1,0:T(8,128)S(1)}, u32[]{:S(2)}, u32[]{:S(2)}) collective-permute-start(f32[3,192,128]{2,1,0:T(8,128)} %get-tuple-element.89), channel_id=1, source_target_pairs={{72,8},{64,0},{80,16},{88,24},{104,40},{96,32},{112,48},{120,56},{... | collective-permute-start | bytes 884744 | tf_op jit(solution)/shard_map/ppermute | solution.py:456
  178.3 20.5 %collective-permute-start.18 = (f32[2,192,128]{2,1,0:T(8,128)}, f32[2,192,128]{2,1,0:T(8,128)S(1)}, u32[]{:S(2)}, u32[]{:S(2)}) collective-permute-start(f32[2,192,128]{2,1,0:T(8,128)} %get-tuple-element.94), channel_id=1, source_target_pairs={{8,72},{0,64},{16,80},{24,88},{40,104},{32,96},{48,112},{56,120},{... | collective-permute-start | bytes 589832 | tf_op jit(solution)/shard_map/ppermute | solution.py:456
  184.4 14.4 %collective-permute-start.19 = (f32[2,192,128]{2,1,0:T(8,128)}, f32[2,192,128]{2,1,0:T(8,128)S(1)}, u32[]{:S(2)}, u32[]{:S(2)}) collective-permute-start(f32[2,192,128]{2,1,0:T(8,128)} %get-tuple-element.95), channel_id=1, source_target_pairs={{72,8},{64,0},{80,16},{88,24},{104,40},{96,32},{112,48},{120,56},{... | collective-permute-start | bytes 589832 | tf_op jit(solution)/shard_map/ppermute | solution.py:456
  185.7 0.8 copy-start.16
  201.9 9.9 %collective-permute-start.20 = (f32[2,192,128]{2,1,0:T(8,128)}, f32[2,192,128]{2,1,0:T(8,128)S(1)}, u32[]{:S(2)}, u32[]{:S(2)}) collective-permute-start(f32[2,192,128]{2,1,0:T(8,128)} %final.1.x3), channel_id=1, source_target_pairs={{8,16},{0,24},{16,40},{24,32},{40,48},{32,56},{48,72},{56,64},{72,... | collective-permute-start | bytes 589832 | tf_op jit(solution)/shard_map/ppermute | solution.py:456
  216.9 8.1 %collective-permute-start.21 = (f32[2,2,192,128]{3,2,1,0:T(8,128)}, f32[2,2,192,128]{3,2,1,0:T(8,128)S(1)}, u32[]{:S(2)}, u32[]{:S(2)}) collective-permute-start(f32[2,2,192,128]{3,2,1,0:T(8,128)} %get-tuple-element.97), channel_id=1, source_target_pairs={{0,8},{1,9},{2,10},{3,11},{4,12},{5,13},{6,14},{7,15},{8,0},{9,1},... | collective-permute-start | bytes 1179656 | tf_op jit(solution)/shard_map/ppermute | solution.py:441
  (12 other events, 8.6 us)
where the time goes:
time: 232 us; the launch traced here: 228 us
  Pallas kernels  120 us (52%)
  starting transfers between devices  62.6 us (27%)
  waiting for transfers between devices  20.8 us (9%)
  local copies, waits for them, and re-layouts  12.3 us (5%)
  between operations  6.17 us (3%)
  other arithmetic  5.79 us (2%)
    pallas_call x18, Pallas kernels, call(): pl.pallas_call(body, out_shape=tuple((jax.ShapeDtypeStruct(s, jnp.float32...  120 us
    ppermute x15, starting transfers between devices, shifted(): return lax.ppermute(array, 'slab', pairs)  50 us
    ppermute x15, waiting for transfers between devices, shifted(): return lax.ppermute(array, 'slab', pairs)  15.8 us
    unnamed x47, local copies, waits for them, and re-layouts  9.79 us
    ppermute x5, starting transfers between devices, pair(): return lax.ppermute(array, ('slab', 'energy'), pairs)  8.31 us
    ppermute x5, waiting for transfers between devices, pair(): return lax.ppermute(array, ('slab', 'energy'), pairs)  4.9 us
  transfers between devices with their start and end apart: 22, of which 5 were waited for; matrix products, arithmetic and copies ran while one was open for 4% of the time, Pallas kernels for 44%

commit v1 on v0

--- a/solution.py
+++ b/solution.py
@@ -228,14 +228,20 @@
 MATRIX = (2, N, N)
 PACKED = (3, N, 128)
 VECTOR = (2, N, COLS)
-MESSAGE = (5, N, 128)
+ENDS = (6, N, 128)
+RHS = (4, N, COLS)
 
 
 def work(B):
     return [pltpu.VMEM((B, N, WIDE), jnp.float32)] * 2 + [pltpu.VMEM((BLOCK, 128), jnp.float32)]
 
 
-def first_body(onsite, hop, dre, dim, xa, p1, p3, q0, tl1, tu1, ar, ai, m):
+def choose(flag, yes, no):
+    pick = jnp.full(yes[0].shape, flag, jnp.int32) == 1
+    return tuple(jnp.where(pick, y, n) for y, n in zip(yes, no))
+
+
+def first_body(onsite, hop, dre, dim, xa, p, left, right, ar, ai, m):
     row = lax.broadcasted_iota(jnp.int32, (N, N), 0)
     col = lax.broadcasted_iota(jnp.int32, (N, N), 1)
     eye = row == col
@@ -262,15 +268,14 @@
         down = csplit(real_left(nn, ht, xs))
         got.append((up, down))
     (up0, down0), (up2, down2) = got
-    one = sub(sub(block(1), real_right(nn, down0, h)), real_right(nn, up2, ht))
-    put(p1, one)
-    put(p3, sub(block(3), real_right(nn, down2, h)))
-    put(q0, real_right(nn, up0, ht))
-    put(tl1, neg(real_right(nn, up0, h)))
-    put(tu1, neg(real_right(nn, down2, ht)))
-
-
-def first_rhs_body(xa, hop, r, ia, r1, r3, s0):
+    pack(p, sub(sub(block(1), real_right(nn, down0, h)), real_right(nn, up2, ht)))
+    pack(left.at[pl.ds(0, 3)], neg(real_right(nn, up0, h)))
+    pack(left.at[pl.ds(3, 3)], neg(real_right(nn, up0, ht)))
+    pack(right.at[pl.ds(0, 3)], neg(real_right(nn, down2, ht)))
+    pack(right.at[pl.ds(3, 3)], sub(block(3), real_right(nn, down2, h)))
+
+
+def first_rhs_body(xa, hop, r, ia, left, right):
     h = split(hop[...])
     ht = split(hop[...].T)
     a = cdot(nn, csplit(get(xa.at[0])), csplit((r[0, 0], r[0, 1])))
@@ -279,96 +284,77 @@
     put(ia.at[1], c)
     a = csplit(a)
     c = csplit(c)
-    put(r1, add((r[1, 0], r[1, 1]), add(real_left(nn, ht, a), real_left(nn, h, c))))
-    put(r3, add((r[3, 0], r[3, 1]), real_left(nn, ht, c)))
-    put(s0, real_left(nn, h, a))
-
-
-def second_body(p1, p3, q0, tl1, tu1, x1, z, p3n, pm, om, tl3, ar, ai, m):
-    ar[0, :, 0:N] = p1[0]
-    ai[0, :, 0:N] = p1[1]
-    sweep(1, ar, ai, m)
-    x = (-ar[0, :, 0:N], -ai[0, :, 0:N])
-    put(x1, x)
-    xs = csplit(x)
-    tl = csplit(get(tl1))
-    tu = csplit(get(tu1))
-    zl = cdot(nn, tl, xs)
-    zu = cdot(nn, tu, xs)
-    put(z.at[0], zl)
-    put(z.at[1], zu)
-    zl = csplit(zl)
-    zu = csplit(zu)
-    put(p3n, sub(get(p3), cdot(nt, zu, tu)))
-    pack(pm, add(get(q0), cdot(nt, zl, tl)))
-    pack(tl3, neg(cdot(nt, zl, tu)))
-    pack(om, neg(cdot(nt, zu, tl)))
-
-
-def second_rhs_body(x1, z, tl1, tu1, r1, r3, s0, i1, yl, yu, r3n, rm):
-    xs = csplit(get(x1))
-    r = csplit(get(r1))
-    put(i1, cdot(nn, xs, r))
-    put(r3n, sub(get(r3), cdot(nn, csplit(get(z.at[1])), r)))
-    put(rm, sub(cdot(nn, csplit(get(z.at[0])), r), get(s0)))
-    put(yl, cdot(nt, xs, csplit(get(tl1))))
-    put(yu, cdot(nt, xs, csplit(get(tu1))))
+    put(
+        left.at[pl.ds(0, 2)],
+        add((r[1, 0], r[1, 1]), add(real_left(nn, ht, a), real_left(nn, h, c))),
+    )
+    put(left.at[pl.ds(2, 2)], real_left(nn, h, a))
+    right[0] = jnp.zeros((N, COLS), jnp.float32)
+    right[1] = jnp.zeros((N, COLS), jnp.float32)
+    put(right.at[pl.ds(2, 2)], add((r[3, 0], r[3, 1]), real_left(nn, ht, c)))
 
 
 def invert_body(count, *refs):
-    p, got = refs[0], refs[1 : 1 + count]
-    pn, x, ar, ai, m = refs[1 + count :]
-    now = get(p)
-    for one in got:
-        now = sub(now, unpack(one))
-    put(pn, now)
+    got = refs[:count]
+    x, ar, ai, m = refs[count:]
+    now = unpack(got[0])
+    for one in got[1:]:
+        now = add(now, unpack(one))
     ar[0, :, 0:N] = now[0]
     ai[0, :, 0:N] = now[1]
     sweep(1, ar, ai, m)
     put(x, (-ar[0, :, 0:N], -ai[0, :, 0:N]))
 
 
-def pivot_body(x, tl, tu, z, below, above):
-    xs = csplit(get(x))
-    tls = csplit(unpack(tl))
-    tus = csplit(unpack(tu))
-    zl = cdot(nn, tls, xs)
-    zu = cdot(nn, tus, xs)
-    put(z.at[0], zl)
-    put(z.at[1], zu)
-    pack(below, cdot(nt, csplit(zu), tus))
-    pack(above, cdot(nt, csplit(zl), tls))
-
-
-def rest_body(count, z, tl, tu, r, *refs):
-    got, (rn, below, above) = refs[:count], refs[count:]
-    now = get(r)
-    for one in got:
-        now = sub(now, (one[3], one[4]))
-    put(rn, now)
-    zl = csplit(get(z.at[0]))
-    zu = csplit(get(z.at[1]))
-    pack(below, neg(cdot(nt, zl, csplit(unpack(tu)))))
-    pack(above, neg(cdot(nt, zu, csplit(unpack(tl)))))
-    now = csplit(now)
-    put(below.at[pl.ds(3, 2)], cdot(nn, zu, now))
-    put(above.at[pl.ds(3, 2)], cdot(nn, zl, now))
-
-
-def final_body(x, r, below, above, out):
-    now = sub(sub(get(r), get(below)), get(above))
-    put(out, cdot(nn, csplit(get(x)), csplit(now)))
-
-
-def last_body(count, z, r, *refs):
-    got, (rn, below, above) = refs[:count], refs[count:]
-    now = get(r)
-    for one in got:
-        now = sub(now, (one[3], one[4]))
-    put(rn, now)
-    now = csplit(now)
-    put(below, cdot(nn, csplit(get(z.at[1])), now))
-    put(above, cdot(nn, csplit(get(z.at[0])), now))
+def coupling(ref):
+    return unpack(ref.at[pl.ds(0, 3)])
+
+
+def end_block(ref):
+    return unpack(ref.at[pl.ds(3, 3)])
+
+
+def near_body(flag, x, own, other, zn, near):
+    t = csplit(choose(flag[0], coupling(other), coupling(own)))
+    z = cdot(nn, t, csplit(get(x)))
+    put(zn, z)
+    f = choose(flag[0], end_block(other), end_block(own))
+    pack(near, sub(f, cdot(nt, csplit(z), t)))
+
+
+def far_body(flag, x, own, other, zf, out):
+    tn_ = csplit(choose(flag[0], coupling(other), coupling(own)))
+    tf = csplit(choose(flag[0], coupling(own), coupling(other)))
+    z = cdot(nn, tf, csplit(get(x)))
+    put(zf, z)
+    z = csplit(z)
+    pack(out.at[pl.ds(0, 3)], neg(cdot(nt, z, tn_)))
+    f = choose(flag[0], end_block(own), end_block(other))
+    pack(out.at[pl.ds(3, 3)], sub(f, cdot(nt, z, tf)))
+
+
+def rhs_ends(ref):
+    return (ref[0], ref[1]), (ref[2], ref[3])
+
+
+def rhs_body(flag, x, zn, zf, own, other, w, out):
+    mine, mine_far = rhs_ends(own)
+    theirs, theirs_far = rhs_ends(other)
+    r = csplit(add(mine, theirs))
+    put(w, cdot(nn, csplit(get(x)), r))
+    near = choose(flag[0], theirs_far, mine_far)
+    far = choose(flag[0], mine_far, theirs_far)
+    put(out.at[pl.ds(0, 2)], sub(near, cdot(nn, csplit(get(zn)), r)))
+    put(out.at[pl.ds(2, 2)], sub(far, cdot(nn, csplit(get(zf)), r)))
+
+
+def last_rhs_body(flag, x, zn, own, other, w, out):
+    mine, mine_far = rhs_ends(own)
+    theirs, theirs_far = rhs_ends(other)
+    r = csplit(add(mine, theirs))
+    put(w, cdot(nn, csplit(get(x)), r))
+    near = choose(flag[0], theirs_far, mine_far)
+    put(out, sub(near, cdot(nn, csplit(get(zn)), r)))
 
 
 def solve_pair(low, xa, ia, h, ht, first, second, out):
@@ -380,22 +366,37 @@
 
 
 def chosen_ends(low, prev, middle, last):
-    pick = jnp.full((N, COLS), low, jnp.int32) == 1
-    first = tuple(jnp.where(pick, a, b) for a, b in zip(prev, middle))
-    second = tuple(jnp.where(pick, a, b) for a, b in zip(middle, last))
-    return first, second
-
-
-def back_body(odd, xa, ia, i1, yl, yu, hop, prev, x3, mid, out):
-    last = get(x3)
-    before = get(prev)
-    one = sub(
-        sub(get(i1), cdot(nn, csplit(get(yl)), csplit(before))),
-        cdot(nn, csplit(get(yu)), csplit(last)),
-    )
+    return choose(low, prev, middle), choose(low, middle, last)
+
+
+def back_body(count, odd, flags, x, r, *refs):
+    levels = [refs[3 * i : 3 * i + 3] for i in range(count)]
+    top, xa, ia, hop, prev_out, mid, last_out, out = (
+        refs[3 * count : 3 * count + 2],
+        *refs[3 * count + 2 :],
+    )
+    end = cdot(nn, csplit(get(x)), csplit(get(r)))
+    zero = (jnp.zeros((N, COLS), jnp.float32),) * 2
+    w, zn = top
+    one = sub(get(w), cdot(tn, csplit(get(zn)), csplit(end)))
+    flag = flags[count]
+    near, far = one, choose(flag, zero, end)
+    for i in range(count - 1, -1, -1):
+        w, zn, zf = levels[i]
+        one = sub(
+            sub(get(w), cdot(tn, csplit(get(zn)), csplit(near))),
+            cdot(tn, csplit(get(zf)), csplit(far)),
+        )
+        flag = flags[i]
+        if i:
+            near, far = one, choose(flag, far, near)
+    prev = choose(flag, far, near)
+    last = choose(flag, near, far)
+    put(prev_out, prev)
     put(mid, one)
+    put(last_out, last)
     low = odd[0]
-    first, second = chosen_ends(low, before, one, last)
+    first, second = chosen_ends(low, prev, one, last)
     solve_pair(low, xa, ia, split(hop[...]), split(hop[...].T), first, second, out)
 
 
@@ -426,32 +427,24 @@
     phonon_shift,
 ):
     slabs = lax.axis_size("slab")
-    width = lax.axis_size("energy")
     energy_count = occupation.shape[1]
     place = lax.axis_index("slab")
     odd = lax.rem(place, 2)
     side = (lax.rem(place, 4) // 2 + odd + 1) % 2
-    def pair(array, by=0):
-        pairs = [
-            (s * width + e, (s ^ 1) * width + e + by)
-            for s in range(slabs)
-            for e in range(width)
-            if 0 <= e + by < width
-        ]
-        return lax.ppermute(array, ("slab", "energy"), pairs)
+    def pair(array):
+        return lax.ppermute(array, "slab", [(s, s ^ 1) for s in range(slabs)])
 
     def along(array, by):
+        width = lax.axis_size("energy")
         pairs = [(e, e + by) for e in range(width) if 0 <= e + by < width]
         return lax.ppermute(array, "energy", pairs)
 
-    def shifted(array, groups):
-        count = slabs // 2
+    def swapped(array, distance):
         spot = lambda g, chain: 2 * g + ((1 - chain) if g % 2 == 0 else chain)
         pairs = [
-            (spot(g, chain), spot(g + groups, chain))
-            for g in range(count)
+            (spot(g, chain), spot(g ^ distance, chain))
+            for g in range(slabs // 2)
             for chain in range(2)
-            if 0 <= g + groups < count
         ]
         return lax.ppermute(array, "slab", pairs)
 
@@ -464,107 +457,85 @@
         slab_profile[:, None] == jnp.arange(potential_table.shape[0], dtype=jnp.int32)[None, :]
     ).astype(jnp.float32)
     potential = jnp.matmul(chosen, potential_table, precision=lax.Precision.HIGHEST)
-    own = jnp.concatenate([along(occupation, 1), occupation, along(occupation, -1)], axis=1)
-    middle = pair(jnp.concatenate([occupation, potential[:, None, :]], axis=1))
-    other = jnp.concatenate(
-        [pair(occupation, 1), middle[:, :energy_count], pair(occupation, -1)], axis=1
-    )
-    occupied = in_order(own, other)
-    potential = in_order(potential, middle[:, energy_count])
-    points = jnp.arange(3 * energy_count, dtype=jnp.int32)
-    weights = jnp.zeros((3 * energy_count,), jnp.float32)
+    widened = jnp.concatenate([along(occupation, 1), occupation, along(occupation, -1)], axis=1)
+    own_points = jnp.arange(energy_count, dtype=jnp.int32)[:, None]
+    points = jnp.arange(3 * energy_count, dtype=jnp.int32)[None, :]
+    weights = jnp.zeros((energy_count, 3 * energy_count), jnp.float32)
     for mode in range(phonon_shift.shape[0]):
-        above = (points == side + energy_count + phonon_shift[mode]).astype(jnp.float32)
-        below = (points == side + energy_count - phonon_shift[mode]).astype(jnp.float32)
+        above = (points == own_points + energy_count + phonon_shift[mode]).astype(jnp.float32)
+        below = (points == own_points + energy_count - phonon_shift[mode]).astype(jnp.float32)
         weights = weights + coupling[mode] * (above + below)
-    damping = jnp.sum(weights[None, :, None] * occupied, axis=1)
+    damping = jnp.sum(weights[None, :, :, None] * widened[:, None, :, :], axis=2)
+    first_side = side == 0
+    mine = jnp.where(first_side, damping[:, 0], damping[:, 1])
+    yours = jnp.where(first_side, damping[:, 1], damping[:, 0])
+    both = in_order(
+        jnp.stack([mine, potential], axis=1), pair(jnp.stack([yours, potential], axis=1))
+    )
     point = lax.axis_index("energy") * energy_count + side
-    dre = energy_low + energy_step * point.astype(jnp.float32) - potential
-    dim = broadening + damping
+    dre = energy_low + energy_step * point.astype(jnp.float32) - both[:, 1]
+    dim = broadening + both[:, 0]
 
     kept = lax.dynamic_index_in_dim(source, side, 2, keepdims=False)
     given = lax.dynamic_index_in_dim(source, 1 - side, 2, keepdims=False)
     right = in_order(kept, pair(given))
 
-    xa, p1, p3, q0, tl1, tu1 = call(
+    xa, near, own, other = call(
         first_body,
         "first",
         14,
-        [(2,) + MATRIX] + [MATRIX] * 5,
+        [(2,) + MATRIX, PACKED, ENDS, ENDS],
         (onsite_block, hopping_block, dre, dim),
         work(2),
     )
-    ia, r1, r3, s0 = call(
-        first_rhs_body, "first_rhs", 4, [(2,) + VECTOR] + [VECTOR] * 3, (xa, hopping_block, right)
-    )
-    x1, z1, p, pm, om, tl = call(
-        second_body,
-        "second",
-        14,
-        [MATRIX, (2,) + MATRIX, MATRIX, PACKED, PACKED, PACKED],
-        (p1, p3, q0, tl1, tu1),
-        work(1),
-    )
-    got_p = [shifted(pm, -1)]
-    i1, yl, yu, r, rm = call(
-        second_rhs_body,
-        "second_rhs",
-        4,
-        [VECTOR, MATRIX, MATRIX, VECTOR, VECTOR],
-        (x1, z1, tl1, tu1, r1, r3, s0),
-    )
-    message = shifted(jnp.concatenate([om, rm], axis=0), -1)
-    got_m = [message]
-    tu = message
-    groups = slabs // 2
-    levels = (groups - 1).bit_length()
-    for level in range(levels):
+    ia, own_r, other_r = call(
+        first_rhs_body, "first_rhs", 4, [(2,) + VECTOR, RHS, RHS], (xa, hopping_block, right)
+    )
+    blocks = (near,)
+    group = place // 2
+    count = (slabs // 2 - 1).bit_length()
+    bit = lambda k: (group >> k) & 1
+    flags = []
+    kept_levels = []
+    for level in range(count + 1):
+        before = bit(level - 1) if level else 0
+        after = bit(level) if level < count else 0
+        flag = jnp.reshape((before == after).astype(jnp.int32), (1,))
+        flags.append(flag)
+        (x,) = call(
+            functools.partial(invert_body, len(blocks)), "invert", 12, [MATRIX], blocks, work(1)
+        )
+        zn, near = call(
+            near_body, "near", 3, [MATRIX, PACKED], (flag, x, own, other), scalars=1
+        )
+        if level == count:
+            w, rest = call(
+                last_rhs_body,
+                "last_rhs",
+                2,
+                [VECTOR, VECTOR],
+                (flag, x, zn, own_r, other_r),
+                scalars=1,
+            )
+            break
         distance = 1 << level
-        p, x = call(
-            functools.partial(invert_body, len(got_p)),
-            "invert",
-            12,
-            [MATRIX, MATRIX],
-            (p, *got_p),
-            work(1),
+        blocks = (near, swapped(near, distance))
+        zf, ends = call(far_body, "far", 3, [MATRIX, ENDS], (flag, x, own, other), scalars=1)
+        own, other = ends, swapped(ends, distance)
+        w, rest = call(
+            rhs_body, "rhs", 2, [VECTOR, RHS], (flag, x, zn, zf, own_r, other_r), scalars=1
         )
-        z, below, above = call(
-            pivot_body, "pivot", 4, [(2,) + MATRIX, PACKED, PACKED], (x, tl, tu)
-        )
-        got_p = [shifted(below, distance), shifted(above, -distance)]
-        if level < levels - 1:
-            r, below, above = call(
-                functools.partial(rest_body, len(got_m)),
-                "rest",
-                4,
-                [VECTOR, MESSAGE, MESSAGE],
-                (z, tl, tu, r, *got_m),
-            )
-        else:
-            r, below, above = call(
-                functools.partial(last_body, len(got_m)), "last", 2, [VECTOR] * 3, (z, r, *got_m)
-            )
-        tl = shifted(below, distance)
-        tu = shifted(above, -distance)
-        got_m = [tl, tu]
-    p, x = call(
-        functools.partial(invert_body, len(got_p)),
-        "invert",
-        12,
-        [MATRIX, MATRIX],
-        (p, *got_p),
-        work(1),
-    )
-    (x3,) = call(final_body, "final", 2, [VECTOR], (x, r, *got_m))
-    prev = shifted(x3, 1)
+        own_r, other_r = rest, swapped(rest, distance)
+        kept_levels += [w, zn, zf]
+    (x,) = call(functools.partial(invert_body, 1), "invert", 12, [MATRIX], (near,), work(1))
     low = jnp.reshape(odd, (1,))
-    mid, sent = call(
-        back_body,
+    prev, mid, x3, sent = call(
+        functools.partial(back_body, count),
         "back",
-        3,
-        [VECTOR, (2,) + VECTOR],
-        (low, xa, ia, i1, yl, yu, hopping_block, prev, x3),
-        scalars=1,
+        8,
+        [VECTOR, VECTOR, VECTOR, (2,) + VECTOR],
+        (low, jnp.concatenate(flags), x, rest, *kept_levels, w, zn, xa, ia, hopping_block),
+        scalars=2,
     )
     back = pair(sent)
     (mine,) = call(

time: 232 us -> 191 us (0.82)
  starting transfers between devices: 62.6 us -> 19.6 us
  Pallas kernels: 120 us -> 127 us
  between operations: 6.17 us -> 0.88 us
    ppermute x20 -> x12, starting transfers between devices: 58.3 us -> 16.6 us  [the longest x9 14.3 us: swapped(): return lax.ppermute(array, 'slab', pairs)]
    pallas_call x18 -> x21, Pallas kernels: 120 us -> 127 us  [call(): pl.pallas_call(body, out_shape=tuple((jax.ShapeDtypeStruct(s, jnp.float32...]
    unnamed x47 -> x32, local copies, waits for them, and re-layouts: 9.79 us -> 8.38 us
    ppermute x20 -> x12, waiting for transfers between devices: 20.7 us -> 21.8 us  [the longest x9 13.5 us: swapped(): return lax.ppermute(array, 'slab', pairs)]
  transfers between devices with their start and end apart: 22 -> 14, of which waited for: 5 -> 5; matrix products, arithmetic and copies ran while one was open for 4% -> 5% of each run, Pallas kernels for 44% -> 61%
where the time goes in v1:
time: 191 us; the launch traced here: 188 us
  Pallas kernels  127 us (66%)
  waiting for transfers between devices  21.8 us (11%)
  starting transfers between devices  19.6 us (10%)
  local copies, waits for them, and re-layouts  10.9 us (6%)
  other arithmetic  7.34 us (4%)
    pallas_call x21, Pallas kernels, call(): pl.pallas_call(body, out_shape=tuple((jax.ShapeDtypeStruct(s, jnp.float32...  127 us
    ppermute x9, starting transfers between devices, swapped(): return lax.ppermute(array, 'slab', pairs)  14.3 us
    ppermute x9, waiting for transfers between devices, swapped(): return lax.ppermute(array, 'slab', pairs)  13.5 us
    unnamed x32, local copies, waits for them, and re-layouts  8.38 us
    ppermute x3, waiting for transfers between devices, pair(): return lax.ppermute(array, 'slab', [(s, s ^ 1) for s in range(slabs)])  8.32 us
  transfers between devices with their start and end apart: 14, of which 5 were waited for; matrix products, arithmetic and copies ran while one was open for 5% of the time, Pallas kernels for 61%

profile of v1, /device:TPU:32, one launch (start us, length us, event | category | flops | bytes accessed | tf_op | source)
XLA Modules:
  0.0 188.1 jit_solution(4537054462935351103)
XLA Ops:
  0.6 1.7 collective-permute-start
  10.5 2.5 %multiply_add_fusion = f32[2,6]{0,1:T(8,128)S(1)} fusion(s32[2]{0:T(128)S(1)} %get-tuple-element.84, s32[2]{0:T(128)S(1)} %get-tuple-element.85, f32[]{:T(128)} %bitcast.8, s32[2]{0:T(128)S(1)} %get-tuple-element.86, s32[2]{0:T(128)S(1)} %get-tuple-element.87, f32[]{:T(128)} %bitcast.6, s32[2]{0:T(128)S(1)} %get-tuple-element.88, ...), kind=kLoop, calls=%fused_computation.12 | loop fusion | flops 324 | bytes 128 | tf_op jit(solution)/shard_map/add | solution.py:467
  15.3 2.5 %collective-permute-done.2 = f32[2,2,192]{2,0,1:T(2,128)S(1)} collective-permute-done((f32[2,2,192]{2,0,1:T(2,128)S(1)}, f32[2,2,192]{2,0,1:T(2,128)S(1)}, u32[]{:S(2)}, u32[]{:S(2)}) %collective-permute-start.2) | collective-permute-done | bytes 3104 | tf_op jit(solution)/shard_map/ppermute | solution.py:435
  18.4 15.3 %first.1 = (f32[2,2,192,192]{3,2,1,0:T(8,128)}, f32[3,192,128]{2,1,0:T(8,128)}, f32[6,192,128]{2,1,0:T(8,128)}, f32[6,192,128]{2,1,0:T(8,128)}) custom-call(f32[192,192]{1,0:T(8,128)} %onsite.1, f32[192,192]{1,0:T(8,128)} %hop.5, f32[4,192]{1,0:T(4,128)} %get-tuple-element.71.dre, f32[4,192]{1,0:T(4,128)} %get-tuple-element.70.dim), custom_call_target="tpu_custom_call" | custom-call | flops 15399999488 | bytes 1048576 | tf_op jit(solution)/shard_map/first/pallas_call | solution.py:214
  33.7 12.0 %invert.5.x = f32[2,192,192]{2,1,0:T(8,128)} custom-call(f32[3,192,128]{2,1,0:T(8,128)} %get-tuple-element.37.refs_0_), custom_call_target="tpu_custom_call" | custom-call | flops 13200000000 | bytes 1048576 | tf_op jit(solution)/shard_map/invert/pallas_call | solution.py:214
  45.7 3.0 %near.4 = (f32[2,192,192]{2,1,0:T(8,128)}, f32[3,192,128]{2,1,0:T(8,128)}) custom-call(s32[1]{0:T(128)} %bitcast.15.flag, f32[2,192,192]{2,1,0:T(8,128)} %invert.5.x, f32[6,192,128]{2,1,0:T(8,128)} %get-tuple-element.38.own, f32[6,192,128]{2,1,0:T(8,128)} %get-tuple-element.39.other), custom_call_target="tpu_custom_call" | custom-call | flops 3300000000 | bytes 1048576 | tf_op jit(solution)/shard_map/near/pallas_call | solution.py:214
  48.7 2.2 %collective-permute-start.4 = (f32[3,192,128]{2,1,0:T(8,128)}, f32[3,192,128]{2,1,0:T(8,128)S(1)}, u32[]{:S(2)}, u32[]{:S(2)}) collective-permute-start(f32[3,192,128]{2,1,0:T(8,128)} %get-tuple-element.40.refs_0_), channel_id=1, source_target_pairs={{8,16},{0,24},{16,8},{24,0},{40,48},{32,56},{48,40},{56,32},{72,80... | collective-permute-start | bytes 884744 | tf_op jit(solution)/shard_map/ppermute | solution.py:449
  50.9 3.4 %far.3 = (f32[2,192,192]{2,1,0:T(8,128)}, f32[6,192,128]{2,1,0:T(8,128)}) custom-call(s32[1]{0:T(128)} %bitcast.15.flag, f32[2,192,192]{2,1,0:T(8,128)} %invert.5.x, f32[6,192,128]{2,1,0:T(8,128)} %get-tuple-element.38.own, f32[6,192,128]{2,1,0:T(8,128)} %get-tuple-element.39.other), custom_call_target="tpu_custom_call" | custom-call | flops 3300000000 | bytes 1048576 | tf_op jit(solution)/shard_map/far/pallas_call | solution.py:214
  55.4 4.6 %collective-permute-done.4.refs_1_ = f32[3,192,128]{2,1,0:T(8,128)S(1)} collective-permute-done((f32[3,192,128]{2,1,0:T(8,128)}, f32[3,192,128]{2,1,0:T(8,128)S(1)}, u32[]{:S(2)}, u32[]{:S(2)}) %collective-permute-start.4) | collective-permute-done | bytes 294944 | tf_op jit(solution)/shard_map/ppermute | solution.py:449
  60.7 12.1 %invert.6.x = f32[2,192,192]{2,1,0:T(8,128)} custom-call(f32[3,192,128]{2,1,0:T(8,128)} %get-tuple-element.40.refs_0_, f32[3,192,128]{2,1,0:T(8,128)} %copy-done.14), custom_call_target="tpu_custom_call" | custom-call | flops 13200000000 | bytes 1048576 | tf_op jit(solution)/shard_map/invert/pallas_call | solution.py:214
  73.7 3.7 %first_rhs.1 = (f32[2,2,192,128]{3,2,1,0:T(8,128)}, f32[4,192,128]{2,1,0:T(8,128)}, f32[4,192,128]{2,1,0:T(8,128)}) custom-call(f32[2,2,192,192]{3,2,1,0:T(8,128)} %get-tuple-element.35.xa.refs_11_, f32[192,192]{1,0:T(8,128)} %hop.5, f32[4,2,192,128]{3,2,1,0:T(8,128)} %maximum_select_fusion.r), custom_call_target="tpu_custom_call" | custom-call | flops 4400000000 | bytes 1048576 | tf_op jit(solution)/shard_map/first_rhs/pallas_call | solution.py:214
  77.4 3.3 %rhs.3 = (f32[2,192,128]{2,1,0:T(8,128)}, f32[4,192,128]{2,1,0:T(8,128)}) custom-call(s32[1]{0:T(128)} %bitcast.15.flag, f32[2,192,192]{2,1,0:T(8,128)} %invert.5.x, f32[2,192,192]{2,1,0:T(8,128)} %get-tuple-element.52.zn.refs_1_, f32[2,192,192]{2,1,0:T(8,128)} %get-tuple-element.53.zf.refs_2_, f32[4,192,128]{2,1,0:T(8,128)} %get-tuple-element.54.own, ...), custom_call_target="tpu_custom_call" | custom-call | flops 2200000000 | bytes 1048576 | tf_op jit(solution)/shard_map/rhs/pallas_call | solution.py:214
  80.8 2.1 %collective-permute-start.10 = (f32[4,192,128]{2,1,0:T(8,128)}, f32[4,192,128]{2,1,0:T(8,128)S(1)}, u32[]{:S(2)}, u32[]{:S(2)}) collective-permute-start(f32[4,192,128]{2,1,0:T(8,128)} %get-tuple-element.56.own), channel_id=1, source_target_pairs={{8,16},{0,24},{16,8},{24,0},{40,48},{32,56},{48,40},{56,32},{72,80... | collective-permute-start | bytes 1179656 | tf_op jit(solution)/shard_map/ppermute | solution.py:449
  83.7 3.0 %near.5 = (f32[2,192,192]{2,1,0:T(8,128)}, f32[3,192,128]{2,1,0:T(8,128)}) custom-call(s32[1]{0:T(128)} %bitcast.16.flag, f32[2,192,192]{2,1,0:T(8,128)} %invert.6.x, f32[6,192,128]{2,1,0:T(8,128)} %get-tuple-element.41.own, f32[6,192,128]{2,1,0:T(8,128)} %copy-done.4), custom_call_target="tpu_custom_call" | custom-call | flops 3300000000 | bytes 1048576 | tf_op jit(solution)/shard_map/near/pallas_call | solution.py:214
  86.9 3.4 %far.4 = (f32[2,192,192]{2,1,0:T(8,128)}, f32[6,192,128]{2,1,0:T(8,128)}) custom-call(s32[1]{0:T(128)} %bitcast.16.flag, f32[2,192,192]{2,1,0:T(8,128)} %invert.6.x, f32[6,192,128]{2,1,0:T(8,128)} %get-tuple-element.41.own, f32[6,192,128]{2,1,0:T(8,128)} %copy-done.4), custom_call_target="tpu_custom_call" | custom-call | flops 3300000000 | bytes 1048576 | tf_op jit(solution)/shard_map/far/pallas_call | solution.py:214
  90.4 1.9 collective-permute-start.7
  94.1 3.3 %rhs.4 = (f32[2,192,128]{2,1,0:T(8,128)}, f32[4,192,128]{2,1,0:T(8,128)}) custom-call(s32[1]{0:T(128)} %bitcast.16.flag, f32[2,192,192]{2,1,0:T(8,128)} %invert.6.x, f32[2,192,192]{2,1,0:T(8,128)} %get-tuple-element.50.zn.refs_4_, f32[2,192,192]{2,1,0:T(8,128)} %get-tuple-element.51.zf.refs_5_, f32[4,192,128]{2,1,0:T(8,128)} %get-tuple-element.56.own, ...), custom_call_target="tpu_custom_call" | custom-call | flops 2200000000 | bytes 1048576 | tf_op jit(solution)/shard_map/rhs/pallas_call | solution.py:214
  98.2 12.1 %invert.7.x = f32[2,192,192]{2,1,0:T(8,128)} custom-call(f32[3,192,128]{2,1,0:T(8,128)} %get-tuple-element.42.refs_0_, f32[3,192,128]{2,1,0:T(8,128)} %copy-done.12), custom_call_target="tpu_custom_call" | custom-call | flops 13200000000 | bytes 1048576 | tf_op jit(solution)/shard_map/invert/pallas_call | solution.py:214
  111.2 3.0 %near.6 = (f32[2,192,192]{2,1,0:T(8,128)}, f32[3,192,128]{2,1,0:T(8,128)}) custom-call(s32[1]{0:T(128)} %bitcast.17.flag, f32[2,192,192]{2,1,0:T(8,128)} %invert.7.x, f32[6,192,128]{2,1,0:T(8,128)} %get-tuple-element.43.own, f32[6,192,128]{2,1,0:T(8,128)} %copy-done.5), custom_call_target="tpu_custom_call" | custom-call | flops 3300000000 | bytes 1048576 | tf_op jit(solution)/shard_map/near/pallas_call | solution.py:214
  114.2 3.3 %collective-permute-start.8 = (f32[3,192,128]{2,1,0:T(8,128)}, f32[3,192,128]{2,1,0:T(8,128)S(1)}, u32[]{:S(2)}, u32[]{:S(2)}) collective-permute-start(f32[3,192,128]{2,1,0:T(8,128)} %get-tuple-element.44.refs_0_), channel_id=1, source_target_pairs={{8,72},{0,64},{16,80},{24,88},{40,104},{32,96},{48,112},{56,120},{... | collective-permute-start | bytes 884744 | tf_op jit(solution)/shard_map/ppermute | solution.py:449
  117.4 3.4 %far.5 = (f32[2,192,192]{2,1,0:T(8,128)}, f32[6,192,128]{2,1,0:T(8,128)}) custom-call(s32[1]{0:T(128)} %bitcast.17.flag, f32[2,192,192]{2,1,0:T(8,128)} %invert.7.x, f32[6,192,128]{2,1,0:T(8,128)} %get-tuple-element.43.own, f32[6,192,128]{2,1,0:T(8,128)} %copy-done.5), custom_call_target="tpu_custom_call" | custom-call | flops 3300000000 | bytes 1048576 | tf_op jit(solution)/shard_map/far/pallas_call | solution.py:214
  121.6 3.4 %rhs.5 = (f32[2,192,128]{2,1,0:T(8,128)}, f32[4,192,128]{2,1,0:T(8,128)}) custom-call(s32[1]{0:T(128)} %bitcast.17.flag, f32[2,192,192]{2,1,0:T(8,128)} %invert.7.x, f32[2,192,192]{2,1,0:T(8,128)} %get-tuple-element.48.zn.refs_7_, f32[2,192,192]{2,1,0:T(8,128)} %get-tuple-element.49.zf.refs_8_, f32[4,192,128]{2,1,0:T(8,128)} %get-tuple-element.57.own, ...), custom_call_target="tpu_custom_call" | custom-call | flops 2200000000 | bytes 1048576 | tf_op jit(solution)/shard_map/rhs/pallas_call | solution.py:214
  125.3 3.3 %collective-permute-start.9 = (f32[6,192,128]{2,1,0:T(8,128)S(1)}, f32[6,192,128]{2,1,0:T(8,128)S(1)}, u32[]{:S(2)}, u32[]{:S(2)}) collective-permute-start(f32[6,192,128]{2,1,0:T(8,128)S(1)} %copy-done.6), channel_id=1, source_target_pairs={{8,72},{0,64},{16,80},{24,88},{40,104},{32,96},{48,112},{56,120},{... | collective-permute-start | bytes 1769480 | tf_op jit(solution)/shard_map/ppermute | solution.py:449
  129.3 12.1 %invert.8.x = f32[2,192,192]{2,1,0:T(8,128)} custom-call(f32[3,192,128]{2,1,0:T(8,128)} %get-tuple-element.44.refs_0_, f32[3,192,128]{2,1,0:T(8,128)} %copy-done.13), custom_call_target="tpu_custom_call" | custom-call | flops 13200000000 | bytes 1048576 | tf_op jit(solution)/shard_map/invert/pallas_call | solution.py:214
  141.4 7.7 %collective-permute-done.9.other = f32[6,192,128]{2,1,0:T(8,128)S(1)} collective-permute-done((f32[6,192,128]{2,1,0:T(8,128)S(1)}, f32[6,192,128]{2,1,0:T(8,128)S(1)}, u32[]{:S(2)}, u32[]{:S(2)}) %collective-permute-start.9) | collective-permute-done | bytes 589856 | tf_op jit(solution)/shard_map/ppermute | solution.py:449
  150.0 3.0 %near.7 = (f32[2,192,192]{2,1,0:T(8,128)}, f32[3,192,128]{2,1,0:T(8,128)}) custom-call(s32[1]{0:T(128)} %bitcast.18.flag, f32[2,192,192]{2,1,0:T(8,128)} %invert.8.x, f32[6,192,128]{2,1,0:T(8,128)} %get-tuple-element.45.own, f32[6,192,128]{2,1,0:T(8,128)} %copy-done.7), custom_call_target="tpu_custom_call" | custom-call | flops 3300000000 | bytes 1048576 | tf_op jit(solution)/shard_map/near/pallas_call | solution.py:214
  153.0 12.0 %invert.9.x = f32[2,192,192]{2,1,0:T(8,128)} custom-call(f32[3,192,128]{2,1,0:T(8,128)} %get-tuple-element.46.refs_0_), custom_call_target="tpu_custom_call" | custom-call | flops 13200000000 | bytes 1048576 | tf_op jit(solution)/shard_map/invert/pallas_call | solution.py:214
  165.7 2.8 %last_rhs.1 = (f32[2,192,128]{2,1,0:T(8,128)}, f32[2,192,128]{2,1,0:T(8,128)}) custom-call(s32[1]{0:T(128)} %bitcast.18.flag, f32[2,192,192]{2,1,0:T(8,128)} %invert.8.x, f32[2,192,192]{2,1,0:T(8,128)} %get-tuple-element.47.zn.refs_10_, f32[4,192,128]{2,1,0:T(8,128)} %get-tuple-element.58.own, f32[4,192,128]{2,1,0:T(8,128)} %copy-done.10), custom_call_target="tpu_custom_call" | custom-call | flops 2200000000 | bytes 1048576 | tf_op jit(solution)/shard_map/last_rhs/pallas_call | solution.py:214
  168.5 7.7 %back.1 = (f32[2,192,128]{2,1,0:T(8,128)}, f32[2,192,128]{2,1,0:T(8,128)}, f32[2,192,128]{2,1,0:T(8,128)}, f32[2,2,192,128]{3,2,1,0:T(8,128)}) custom-call(s32[1]{0:T(128)} %bitcast.1.odd, s32[4]{0:T(128)} %pad_add_fusion.flags, f32[2,192,192]{2,1,0:T(8,128)} %invert.9.x, f32[2,192,128]{2,1,0:T(8,128)} %get-tuple-element.59.r, ...), custom_call_target="tpu_custom_call" | custom-call | flops 8800000000 | bytes 1048576 | tf_op jit(solution)/shard_map/back/pallas_call | solution.py:214
  176.2 3.2 %own.1.mine = f32[2,2,192,128]{3,2,1,0:T(8,128)} custom-call(s32[1]{0:T(128)} %bitcast.1.odd, f32[2,2,192,192]{3,2,1,0:T(8,128)} %get-tuple-element.35.xa.refs_11_, f32[2,2,192,128]{3,2,1,0:T(8,128)} %get-tuple-element.36.refs_12_.ia, f32[2,192,128]{2,1,0:T(8,128)} %get-tuple-element.64.mid, f32[192,192]{1,0:T(8,128)} %hop.5, ...), custom_call_target="tpu_custom_call" | custom-call | flops 2200000000 | bytes 1048576 | tf_op jit(solution)/shard_map/own/pallas_call | solution.py:214
  179.5 5.9 %collective-permute-done.13.other = f32[2,2,192,128]{3,2,1,0:T(8,128)S(1)} collective-permute-done((f32[2,2,192,128]{3,2,1,0:T(8,128)}, f32[2,2,192,128]{3,2,1,0:T(8,128)S(1)}, u32[]{:S(2)}, u32[]{:S(2)}) %collective-permute-start.13) | collective-permute-done | bytes 393248 | tf_op jit(solution)/shard_map/ppermute | solution.py:435
  186.1 2.1 %finish.1 = (f32[2,2,2,192,128]{4,3,2,1,0:T(8,128)}, f32[2,2,192]{2,1,0:T(2,128)}) custom-call(s32[1]{0:T(128)} %bitcast.side, f32[2,2,192,128]{3,2,1,0:T(8,128)} %own.1.mine, f32[2,2,192,128]{3,2,1,0:T(8,128)} %copy-done.11), custom_call_target="tpu_custom_call" | custom-call | flops 2200000000 | bytes 1048576 | tf_op jit(solution)/shard_map/finish/pallas_call | solution.py:214
  (67 shorter events, 22.2 us)
Async XLA Ops:
  0.6 12.4 %copy-start = (f32[16,192]{1,0:T(8,128)S(1)}, f32[16,192]{1,0:T(8,128)}, u32[]{:S(2)}) copy-start(f32[16,192]{1,0:T(8,128)} %param.11) | copy-start | bytes 36868
  0.6 12.6 %collective-permute-start = (f32[2,2,192]{2,1,0:T(2,128)}, f32[2,2,192]{2,1,0:T(2,128)S(1)}, u32[]{:S(2)}, u32[]{:S(2)}) collective-permute-start(f32[2,2,192]{2,1,0:T(2,128)} %param.13), channel_id=1, source_target_pairs={{0,1},{1,2},{2,3},{3,4},{4,5},{5,6},{6,7},{8,9},{9,10},{10,11},{11... | collective-permute-start | bytes 9224 | tf_op jit(solution)/shard_map/ppermute | solution.py:440
  2.4 10.9 %collective-permute-start.1 = (f32[2,2,192]{2,1,0:T(2,128)}, f32[2,2,192]{2,1,0:T(2,128)S(1)}, u32[]{:S(2)}, u32[]{:S(2)}) collective-permute-start(f32[2,2,192]{2,1,0:T(2,128)} %param.13), channel_id=1, source_target_pairs={{1,0},{2,1},{3,2},{4,3},{5,4},{6,5},{7,6},{9,8},{10,9},{11,10},{12... | collective-permute-start | bytes 9224 | tf_op jit(solution)/shard_map/ppermute | solution.py:440
  3.7 3.5 %copy-start.2 = (s32[4]{0:T(128)S(1)}, s32[4]{0:T(128)}, u32[]{:S(2)}) copy-start(s32[4]{0:T(128)} %param.15) | copy-start | bytes 52
  4.9 1.7 copy-start.1
  5.0 67.8 %collective-permute-start.3 = (f32[2,2,192,128]{3,2,1,0:T(8,128)S(1)}, f32[2,2,192,128]{3,2,1,0:T(8,128)S(1)}, u32[]{:S(2)}, u32[]{:S(2)}) collective-permute-start(f32[2,2,192,128]{3,2,1,0:T(8,128)S(1)} %get-tuple-element.68), channel_id=1, source_target_pairs={{0,8},{8,0},{16,24},{24,16},{32,40},{40,32},{48,56},{56,48},{64,72... | collective-permute-start | bytes 1179656 | tf_op jit(solution)/shard_map/ppermute | solution.py:435
  10.5 2.5 %copy-start.15 = (s32[2]{0:T(128)S(1)}, s32[2]{0:T(128)}, u32[]{:S(2)}) copy-start(s32[2]{0:T(128)} %param.12) | copy-start | bytes 28
  13.2 0.7 copy-start.3
  14.1 3.7 %collective-permute-start.2 = (f32[2,2,192]{2,0,1:T(2,128)S(1)}, f32[2,2,192]{2,0,1:T(2,128)S(1)}, u32[]{:S(2)}, u32[]{:S(2)}) collective-permute-start(f32[2,2,192]{2,0,1:T(2,128)S(1)} %pad_maximum_fusion.1), channel_id=1, source_target_pairs={{0,8},{8,0},{16,24},{24,16},{32,40},{40,32},{48,56},{56,48},{64,72... | collective-permute-start | bytes 9224 | tf_op jit(solution)/shard_map/ppermute | solution.py:435
  48.7 11.3 %collective-permute-start.4 = (f32[3,192,128]{2,1,0:T(8,128)}, f32[3,192,128]{2,1,0:T(8,128)S(1)}, u32[]{:S(2)}, u32[]{:S(2)}) collective-permute-start(f32[3,192,128]{2,1,0:T(8,128)} %get-tuple-element.40.refs_0_), channel_id=1, source_target_pairs={{8,16},{0,24},{16,8},{24,0},{40,48},{32,56},{48,40},{56,32},{72,80... | collective-permute-start | bytes 884744 | tf_op jit(solution)/shard_map/ppermute | solution.py:449
  54.3 28.5 %collective-permute-start.5 = (f32[6,192,128]{2,1,0:T(8,128)}, f32[6,192,128]{2,1,0:T(8,128)S(1)}, u32[]{:S(2)}, u32[]{:S(2)}) collective-permute-start(f32[6,192,128]{2,1,0:T(8,128)} %get-tuple-element.41.own), channel_id=1, source_target_pairs={{8,16},{0,24},{16,8},{24,0},{40,48},{32,56},{48,40},{56,32},{72,80... | collective-permute-start | bytes 1769480 | tf_op jit(solution)/shard_map/ppermute | solution.py:449
  60.0 0.7 copy-start.14
  80.8 12.6 %collective-permute-start.10 = (f32[4,192,128]{2,1,0:T(8,128)}, f32[4,192,128]{2,1,0:T(8,128)S(1)}, u32[]{:S(2)}, u32[]{:S(2)}) collective-permute-start(f32[4,192,128]{2,1,0:T(8,128)} %get-tuple-element.56.own), channel_id=1, source_target_pairs={{8,16},{0,24},{16,8},{24,0},{40,48},{32,56},{48,40},{56,32},{72,80... | collective-permute-start | bytes 1179656 | tf_op jit(solution)/shard_map/ppermute | solution.py:449
  82.9 0.8 copy-start.4
  86.8 10.8 %collective-permute-start.6 = (f32[3,192,128]{2,1,0:T(8,128)}, f32[3,192,128]{2,1,0:T(8,128)S(1)}, u32[]{:S(2)}, u32[]{:S(2)}) collective-permute-start(f32[3,192,128]{2,1,0:T(8,128)} %get-tuple-element.42.refs_0_), channel_id=1, source_target_pairs={{8,40},{0,32},{16,48},{24,56},{40,8},{32,0},{48,16},{56,24},{72,10... | collective-permute-start | bytes 884744 | tf_op jit(solution)/shard_map/ppermute | solution.py:449
  90.4 19.9 %collective-permute-start.7 = (f32[6,192,128]{2,1,0:T(8,128)}, f32[6,192,128]{2,1,0:T(8,128)S(1)}, u32[]{:S(2)}, u32[]{:S(2)}) collective-permute-start(f32[6,192,128]{2,1,0:T(8,128)} %get-tuple-element.43.own), channel_id=1, source_target_pairs={{8,40},{0,32},{16,48},{24,56},{40,8},{32,0},{48,16},{56,24},{72,10... | collective-permute-start | bytes 1769480 | tf_op jit(solution)/shard_map/ppermute | solution.py:449
  93.3 0.7 copy-start.8
  97.4 23.5 %collective-permute-start.11 = (f32[4,192,128]{2,1,0:T(8,128)}, f32[4,192,128]{2,1,0:T(8,128)S(1)}, u32[]{:S(2)}, u32[]{:S(2)}) collective-permute-start(f32[4,192,128]{2,1,0:T(8,128)} %get-tuple-element.57.own), channel_id=1, source_target_pairs={{8,40},{0,32},{16,48},{24,56},{40,8},{32,0},{48,16},{56,24},{72,10... | collective-permute-start | bytes 1179656 | tf_op jit(solution)/shard_map/ppermute | solution.py:449
  97.5 0.7 copy-start.12
  110.3 0.8 copy-start.5
  114.2 14.4 %collective-permute-start.8 = (f32[3,192,128]{2,1,0:T(8,128)}, f32[3,192,128]{2,1,0:T(8,128)S(1)}, u32[]{:S(2)}, u32[]{:S(2)}) collective-permute-start(f32[3,192,128]{2,1,0:T(8,128)} %get-tuple-element.44.refs_0_), channel_id=1, source_target_pairs={{8,72},{0,64},{16,80},{24,88},{40,104},{32,96},{48,112},{56,120},{... | collective-permute-start | bytes 884744 | tf_op jit(solution)/shard_map/ppermute | solution.py:449
  120.9 0.8 copy-start.9
  121.6 3.7 %copy-start.6 = (f32[6,192,128]{2,1,0:T(8,128)S(1)}, f32[6,192,128]{2,1,0:T(8,128)}, u32[]{:S(2)}) copy-start(f32[6,192,128]{2,1,0:T(8,128)} %get-tuple-element.45.own) | copy-start | bytes 1769476
  125.0 40.0 %collective-permute-start.12 = (f32[4,192,128]{2,1,0:T(8,128)}, f32[4,192,128]{2,1,0:T(8,128)S(1)}, u32[]{:S(2)}, u32[]{:S(2)}) collective-permute-start(f32[4,192,128]{2,1,0:T(8,128)} %get-tuple-element.58.own), channel_id=1, source_target_pairs={{8,72},{0,64},{16,80},{24,88},{40,104},{32,96},{48,112},{56,120},{... | collective-permute-start | bytes 1179656 | tf_op jit(solution)/shard_map/ppermute | solution.py:449
  125.3 23.8 %collective-permute-start.9 = (f32[6,192,128]{2,1,0:T(8,128)S(1)}, f32[6,192,128]{2,1,0:T(8,128)S(1)}, u32[]{:S(2)}, u32[]{:S(2)}) collective-permute-start(f32[6,192,128]{2,1,0:T(8,128)S(1)} %copy-done.6), channel_id=1, source_target_pairs={{8,72},{0,64},{16,80},{24,88},{40,104},{32,96},{48,112},{56,120},{... | collective-permute-start | bytes 1769480 | tf_op jit(solution)/shard_map/ppermute | solution.py:449
  128.6 0.7 copy-start.13
  149.1 0.8 copy-start.7
  165.0 0.8 copy-start.10
  176.2 9.1 %collective-permute-start.13 = (f32[2,2,192,128]{3,2,1,0:T(8,128)}, f32[2,2,192,128]{3,2,1,0:T(8,128)S(1)}, u32[]{:S(2)}, u32[]{:S(2)}) collective-permute-start(f32[2,2,192,128]{3,2,1,0:T(8,128)} %get-tuple-element.67), channel_id=1, source_target_pairs={{0,8},{8,0},{16,24},{24,16},{32,40},{40,32},{48,56},{56,48},{64,72... | collective-permute-start | bytes 1179656 | tf_op jit(solution)/shard_map/ppermute | solution.py:435
  185.3 0.8 copy-start.11

commit v2 on v1

--- a/solution.py
+++ b/solution.py
@@ -230,10 +230,23 @@
 VECTOR = (2, N, COLS)
 ENDS = (6, N, 128)
 RHS = (4, N, COLS)
+MESSAGE = (10, N, 128)
 
 
 def work(B):
     return [pltpu.VMEM((B, N, WIDE), jnp.float32)] * 2 + [pltpu.VMEM((BLOCK, 128), jnp.float32)]
+
+
+def vdot(dot, a, v):
+    high, low = split(jnp.concatenate(v, axis=1))
+    turn = lambda s: jnp.concatenate([-s[:, COLS:], s[:, :COLS]], axis=1)
+    both = three(dot, a[0], (high, low)) + three(dot, a[1], (turn(high), turn(low)))
+    return both[:, :COLS], both[:, COLS:]
+
+
+def real_vdot(a, v):
+    both = three(nn, a, split(jnp.concatenate(v, axis=1)))
+    return both[:, :COLS], both[:, COLS:]
 
 
 def choose(flag, yes, no):
@@ -241,15 +254,35 @@
     return tuple(jnp.where(pick, y, n) for y, n in zip(yes, no))
 
 
-def first_body(onsite, hop, dre, dim, xa, p, left, right, ar, ai, m):
+def damping_body(info, shift, profile, coupling, low, occ, high, table, mine, yours):
+    for out, k in ((mine, info[1]), (yours, 1 - info[1])):
+        for slab in range(2):
+            total = jnp.full((1, N), broadening, jnp.float32)
+            for q in range(6):
+                w = jnp.float32(0.0)
+                for mode in range(shift.shape[0]):
+                    c = coupling[mode]
+                    w = w + jnp.where(q == k + 2 + shift[mode], c, 0.0)
+                    w = w + jnp.where(q == k + 2 - shift[mode], c, 0.0)
+                row = (low, occ, high)[q // 2][slab, q % 2 : q % 2 + 1, :]
+                total = total + w * row
+            out[slab, 0:1, :] = total
+            out[slab, 1:2, :] = table[pl.ds(profile[slab], 1), :]
+
+
+def first_body(info, onsite, hop, mine, theirs, xa, x, zn, left, right, near, ar, ai, m):
     row = lax.broadcasted_iota(jnp.int32, (N, N), 0)
     col = lax.broadcasted_iota(jnp.int32, (N, N), 1)
     eye = row == col
+    energy = energy_low + energy_step * info[2].astype(jnp.float32)
 
     def block(i):
+        flag = info[0] if i // 2 else 1 - info[0]
+        at = i % 2
+        (both,) = choose(flag, (mine[at],), (theirs[at],))
         return (
-            jnp.where(eye, dre[i : i + 1, :], 0.0) - onsite[...],
-            jnp.where(eye, dim[i : i + 1, :], 0.0),
+            jnp.where(eye, energy - both[1:2], 0.0) - onsite[...],
+            jnp.where(eye, both[0:1], 0.0),
         )
 
     for e in range(2):
@@ -261,52 +294,54 @@
     ht = split(hop[...].T)
     got = []
     for e in range(2):
-        x = (-ar[e, :, 0:N], -ai[e, :, 0:N])
-        put(xa.at[e], x)
-        xs = csplit(x)
+        one = (-ar[e, :, 0:N], -ai[e, :, 0:N])
+        put(xa.at[e], one)
+        xs = csplit(one)
         up = csplit(real_left(nn, h, xs))
         down = csplit(real_left(nn, ht, xs))
         got.append((up, down))
     (up0, down0), (up2, down2) = got
-    pack(p, sub(sub(block(1), real_right(nn, down0, h)), real_right(nn, up2, ht)))
+    middle = sub(sub(block(1), real_right(nn, down0, h)), real_right(nn, up2, ht))
     pack(left.at[pl.ds(0, 3)], neg(real_right(nn, up0, h)))
     pack(left.at[pl.ds(3, 3)], neg(real_right(nn, up0, ht)))
     pack(right.at[pl.ds(0, 3)], neg(real_right(nn, down2, ht)))
     pack(right.at[pl.ds(3, 3)], sub(block(3), real_right(nn, down2, h)))
-
-
-def first_rhs_body(xa, hop, r, ia, left, right):
+    ar[0, :, 0:N] = middle[0]
+    ai[0, :, 0:N] = middle[1]
+    sweep(1, ar, ai, m)
+    put(x, (-ar[0, :, 0:N], -ai[0, :, 0:N]))
+    near_end(info[3], get(x), left, right, zn, lambda v: pack(near, v))
+
+
+def first_rhs_body(info, xa, hop, kept, other, ia, left, right):
     h = split(hop[...])
     ht = split(hop[...].T)
-    a = cdot(nn, csplit(get(xa.at[0])), csplit((r[0, 0], r[0, 1])))
-    c = cdot(nn, csplit(get(xa.at[1])), csplit((r[2, 0], r[2, 1])))
+
+    def r(i):
+        flag = info[0] if i // 2 else 1 - info[0]
+        at = i % 2
+        return choose(flag, (kept[at, 0], kept[at, 1]), (other[at, 0], other[at, 1]))
+
+    a = vdot(nn, csplit(get(xa.at[0])), r(0))
+    c = vdot(nn, csplit(get(xa.at[1])), r(2))
     put(ia.at[0], a)
     put(ia.at[1], c)
-    a = csplit(a)
-    c = csplit(c)
-    put(
-        left.at[pl.ds(0, 2)],
-        add((r[1, 0], r[1, 1]), add(real_left(nn, ht, a), real_left(nn, h, c))),
-    )
-    put(left.at[pl.ds(2, 2)], real_left(nn, h, a))
+    put(left.at[pl.ds(0, 2)], add(r(1), add(real_vdot(ht, a), real_vdot(h, c))))
+    put(left.at[pl.ds(2, 2)], real_vdot(h, a))
     right[0] = jnp.zeros((N, COLS), jnp.float32)
     right[1] = jnp.zeros((N, COLS), jnp.float32)
-    put(right.at[pl.ds(2, 2)], add((r[3, 0], r[3, 1]), real_left(nn, ht, c)))
-
-
-def invert_body(count, *refs):
-    got = refs[:count]
-    x, ar, ai, m = refs[count:]
-    now = unpack(got[0])
-    for one in got[1:]:
-        now = add(now, unpack(one))
+    put(right.at[pl.ds(2, 2)], add(r(3), real_vdot(ht, c)))
+
+
+def invert_body(own, other, x, ar, ai, m):
+    now = add(unpack(own), unpack(other))
     ar[0, :, 0:N] = now[0]
     ai[0, :, 0:N] = now[1]
     sweep(1, ar, ai, m)
     put(x, (-ar[0, :, 0:N], -ai[0, :, 0:N]))
 
 
-def coupling(ref):
+def coupling_of(ref):
     return unpack(ref.at[pl.ds(0, 3)])
 
 
@@ -314,80 +349,79 @@
     return unpack(ref.at[pl.ds(3, 3)])
 
 
-def near_body(flag, x, own, other, zn, near):
-    t = csplit(choose(flag[0], coupling(other), coupling(own)))
-    z = cdot(nn, t, csplit(get(x)))
+def near_end(flag, x, own, other, zn, store):
+    t = csplit(choose(flag, coupling_of(other), coupling_of(own)))
+    z = cdot(nn, t, csplit(x))
     put(zn, z)
-    f = choose(flag[0], end_block(other), end_block(own))
-    pack(near, sub(f, cdot(nt, csplit(z), t)))
-
-
-def far_body(flag, x, own, other, zf, out):
-    tn_ = csplit(choose(flag[0], coupling(other), coupling(own)))
-    tf = csplit(choose(flag[0], coupling(own), coupling(other)))
-    z = cdot(nn, tf, csplit(get(x)))
+    f = choose(flag, end_block(other), end_block(own))
+    store(sub(f, cdot(nt, csplit(z), t)))
+
+
+def near_body(level, info, x, own, other, zn, near):
+    near_end(info[3 + level], get(x), own, other, zn, lambda v: pack(near, v))
+
+
+def rhs_ends(ref, base):
+    return (ref[base], ref[base + 1]), (ref[base + 2], ref[base + 3])
+
+
+def rest_body(level, base, info, x, zn, own, other, own_r, other_r, w, zf, out):
+    flag = info[3 + level]
+    xs = csplit(get(x))
+    zns = csplit(get(zn))
+    t_near = csplit(choose(flag, coupling_of(other), coupling_of(own)))
+    t_far = csplit(choose(flag, coupling_of(own), coupling_of(other)))
+    mine, mine_far = rhs_ends(own_r, base)
+    theirs, theirs_far = rhs_ends(other_r, base)
+    r = add(mine, theirs)
+    z = cdot(nn, t_far, xs)
+    put(w, vdot(nn, xs, r))
+    put(out.at[pl.ds(6, 2)], sub(choose(flag, theirs_far, mine_far), vdot(nn, zns, r)))
     put(zf, z)
     z = csplit(z)
-    pack(out.at[pl.ds(0, 3)], neg(cdot(nt, z, tn_)))
-    f = choose(flag[0], end_block(own), end_block(other))
-    pack(out.at[pl.ds(3, 3)], sub(f, cdot(nt, z, tf)))
-
-
-def rhs_ends(ref):
-    return (ref[0], ref[1]), (ref[2], ref[3])
-
-
-def rhs_body(flag, x, zn, zf, own, other, w, out):
-    mine, mine_far = rhs_ends(own)
-    theirs, theirs_far = rhs_ends(other)
-    r = csplit(add(mine, theirs))
-    put(w, cdot(nn, csplit(get(x)), r))
-    near = choose(flag[0], theirs_far, mine_far)
-    far = choose(flag[0], mine_far, theirs_far)
-    put(out.at[pl.ds(0, 2)], sub(near, cdot(nn, csplit(get(zn)), r)))
-    put(out.at[pl.ds(2, 2)], sub(far, cdot(nn, csplit(get(zf)), r)))
-
-
-def last_rhs_body(flag, x, zn, own, other, w, out):
-    mine, mine_far = rhs_ends(own)
-    theirs, theirs_far = rhs_ends(other)
-    r = csplit(add(mine, theirs))
-    put(w, cdot(nn, csplit(get(x)), r))
-    near = choose(flag[0], theirs_far, mine_far)
-    put(out, sub(near, cdot(nn, csplit(get(zn)), r)))
-
-
-def solve_pair(low, xa, ia, h, ht, first, second, out):
-    t = add(real_left(nn, ht, csplit(first)), real_left(nn, h, csplit(second)))
+    pack(out.at[pl.ds(0, 3)], neg(cdot(nt, z, t_near)))
+    f = choose(flag, end_block(own), end_block(other))
+    pack(out.at[pl.ds(3, 3)], sub(f, cdot(nt, z, t_far)))
+    put(out.at[pl.ds(8, 2)], sub(choose(flag, mine_far, theirs_far), vdot(nn, z, r)))
+
+
+def solve_pair(low, xa, ia, hop, prev, middle, last, out):
+    first = choose(low, prev, middle)
+    second = choose(low, middle, last)
+    t = add(real_vdot(split(hop[...].T), first), real_vdot(split(hop[...]), second))
     at = 1 - low
     x = xa[at, 0], xa[at, 1]
-    put(out.at[0], add((ia[at, 0], ia[at, 1]), cdot(nn, csplit(x), csplit(t))))
+    put(out.at[0], add((ia[at, 0], ia[at, 1]), vdot(nn, csplit(x), t)))
     put(out.at[1], second)
 
 
-def chosen_ends(low, prev, middle, last):
-    return choose(low, prev, middle), choose(low, middle, last)
-
-
-def back_body(count, odd, flags, x, r, *refs):
+def back_body(count, info, x, own, other, *refs):
     levels = [refs[3 * i : 3 * i + 3] for i in range(count)]
-    top, xa, ia, hop, prev_out, mid, last_out, out = (
-        refs[3 * count : 3 * count + 2],
-        *refs[3 * count + 2 :],
-    )
-    end = cdot(nn, csplit(get(x)), csplit(get(r)))
-    zero = (jnp.zeros((N, COLS), jnp.float32),) * 2
-    w, zn = top
-    one = sub(get(w), cdot(tn, csplit(get(zn)), csplit(end)))
-    flag = flags[count]
-    near, far = one, choose(flag, zero, end)
+    xa, ia, hop, prev_out, mid, last_out, out, zn, ar, ai, m = refs[3 * count :]
+    flag = info[3 + count]
+    xs = get(x)
+
+    def store(v):
+        ar[0, :, 0:N] = v[0]
+        ai[0, :, 0:N] = v[1]
+
+    near_end(flag, xs, own, other, zn, store)
+    mine, mine_far = rhs_ends(own, 6)
+    theirs, theirs_far = rhs_ends(other, 6)
+    r = add(mine, theirs)
+    w = vdot(nn, csplit(xs), r)
+    rest = sub(choose(flag, theirs_far, mine_far), vdot(nn, csplit(get(zn)), r))
+    sweep(1, ar, ai, m)
+    end = vdot(nn, csplit((-ar[0, :, 0:N], -ai[0, :, 0:N])), rest)
+    one = sub(w, vdot(tn, csplit(get(zn)), end))
+    near, far = one, choose(flag, (jnp.zeros((N, COLS), jnp.float32),) * 2, end)
     for i in range(count - 1, -1, -1):
-        w, zn, zf = levels[i]
+        w, z_near, z_far = levels[i]
         one = sub(
-            sub(get(w), cdot(tn, csplit(get(zn)), csplit(near))),
-            cdot(tn, csplit(get(zf)), csplit(far)),
+            sub(get(w), vdot(tn, csplit(get(z_near)), near)),
+            vdot(tn, csplit(get(z_far)), far),
         )
-        flag = flags[i]
+        flag = info[3 + i]
         if i:
             near, far = one, choose(flag, far, near)
     prev = choose(flag, far, near)
@@ -395,19 +429,15 @@
     put(prev_out, prev)
     put(mid, one)
     put(last_out, last)
-    low = odd[0]
-    first, second = chosen_ends(low, prev, one, last)
-    solve_pair(low, xa, ia, split(hop[...]), split(hop[...].T), first, second, out)
-
-
-def own_body(odd, xa, ia, mid, hop, prev, x3, out):
-    low = 1 - odd[0]
-    first, second = chosen_ends(low, get(prev), get(mid), get(x3))
-    solve_pair(low, xa, ia, split(hop[...]), split(hop[...].T), first, second, out)
-
-
-def finish_body(side, mine, other, amplitude, density):
-    for which, part in ((side[0], mine), (1 - side[0], other)):
+    solve_pair(info[0], xa, ia, hop, prev, one, last, out)
+
+
+def own_body(info, xa, ia, mid, hop, prev, last, out):
+    solve_pair(1 - info[0], xa, ia, hop, get(prev), get(mid), get(last), out)
+
+
+def finish_body(info, mine, other, amplitude, density):
+    for which, part in ((info[1], mine), (1 - info[1], other)):
         for slab in range(2):
             re, im = part[slab, 0], part[slab, 1]
             amplitude[slab, 0, which] = re
@@ -448,94 +478,83 @@
         ]
         return lax.ppermute(array, "slab", pairs)
 
-    def in_order(own, other):
-        return jnp.where(
-            odd == 1, jnp.concatenate([other, own], axis=0), jnp.concatenate([own, other], axis=0)
-        )
-
-    chosen = (
-        slab_profile[:, None] == jnp.arange(potential_table.shape[0], dtype=jnp.int32)[None, :]
-    ).astype(jnp.float32)
-    potential = jnp.matmul(chosen, potential_table, precision=lax.Precision.HIGHEST)
-    widened = jnp.concatenate([along(occupation, 1), occupation, along(occupation, -1)], axis=1)
-    own_points = jnp.arange(energy_count, dtype=jnp.int32)[:, None]
-    points = jnp.arange(3 * energy_count, dtype=jnp.int32)[None, :]
-    weights = jnp.zeros((energy_count, 3 * energy_count), jnp.float32)
-    for mode in range(phonon_shift.shape[0]):
-        above = (points == own_points + energy_count + phonon_shift[mode]).astype(jnp.float32)
-        below = (points == own_points + energy_count - phonon_shift[mode]).astype(jnp.float32)
-        weights = weights + coupling[mode] * (above + below)
-    damping = jnp.sum(weights[None, :, :, None] * widened[:, None, :, :], axis=2)
-    first_side = side == 0
-    mine = jnp.where(first_side, damping[:, 0], damping[:, 1])
-    yours = jnp.where(first_side, damping[:, 1], damping[:, 0])
-    both = in_order(
-        jnp.stack([mine, potential], axis=1), pair(jnp.stack([yours, potential], axis=1))
-    )
+    group = place // 2
+    count = (slabs // 2 - 1).bit_length()
+    bit = lambda k: (group >> k) & 1 if 0 <= k < count else 0
+    facing = [(bit(k - 1) == bit(k)) * 1 for k in range(count + 1)]
     point = lax.axis_index("energy") * energy_count + side
-    dre = energy_low + energy_step * point.astype(jnp.float32) - both[:, 1]
-    dim = broadening + both[:, 0]
-
+    info = jnp.stack([jnp.asarray(v, jnp.int32) for v in (odd, side, point, *facing)])
+    mine, yours = call(
+        damping_body,
+        "damping",
+        1,
+        [(2, 2, N)] * 2,
+        (
+            info,
+            phonon_shift,
+            slab_profile,
+            coupling,
+            along(occupation, 1),
+            occupation,
+            along(occupation, -1),
+            potential_table,
+        ),
+        scalars=4,
+    )
+    theirs = pair(yours)
     kept = lax.dynamic_index_in_dim(source, side, 2, keepdims=False)
-    given = lax.dynamic_index_in_dim(source, 1 - side, 2, keepdims=False)
-    right = in_order(kept, pair(given))
-
-    xa, near, own, other = call(
+    given = pair(lax.dynamic_index_in_dim(source, 1 - side, 2, keepdims=False))
+
+    xa, x, zn, own, other, near = call(
         first_body,
         "first",
-        14,
-        [(2,) + MATRIX, PACKED, ENDS, ENDS],
-        (onsite_block, hopping_block, dre, dim),
+        30,
+        [(2,) + MATRIX, MATRIX, MATRIX, ENDS, ENDS, PACKED],
+        (info, onsite_block, hopping_block, mine, theirs),
         work(2),
+        scalars=1,
     )
     ia, own_r, other_r = call(
-        first_rhs_body, "first_rhs", 4, [(2,) + VECTOR, RHS, RHS], (xa, hopping_block, right)
-    )
-    blocks = (near,)
-    group = place // 2
-    count = (slabs // 2 - 1).bit_length()
-    bit = lambda k: (group >> k) & 1
-    flags = []
-    kept_levels = []
-    for level in range(count + 1):
-        before = bit(level - 1) if level else 0
-        after = bit(level) if level < count else 0
-        flag = jnp.reshape((before == after).astype(jnp.int32), (1,))
-        flags.append(flag)
-        (x,) = call(
-            functools.partial(invert_body, len(blocks)), "invert", 12, [MATRIX], blocks, work(1)
+        first_rhs_body,
+        "first_rhs",
+        3,
+        [(2,) + VECTOR, RHS, RHS],
+        (info, xa, hopping_block, kept, given),
+        scalars=1,
+    )
+    held = []
+    for level in range(count):
+        distance = 1 << level
+        facing_block = swapped(near, distance)
+        w, zf, rest = call(
+            functools.partial(rest_body, level, 6 if level else 0),
+            "rest",
+            5,
+            [VECTOR, MATRIX, MESSAGE],
+            (info, x, zn, own, other, own_r, other_r),
+            scalars=1,
         )
-        zn, near = call(
-            near_body, "near", 3, [MATRIX, PACKED], (flag, x, own, other), scalars=1
-        )
-        if level == count:
-            w, rest = call(
-                last_rhs_body,
-                "last_rhs",
-                2,
-                [VECTOR, VECTOR],
-                (flag, x, zn, own_r, other_r),
+        held += [w, zn, zf]
+        own = own_r = rest
+        other = other_r = swapped(rest, distance)
+        (x,) = call(invert_body, "invert", 12, [MATRIX], (near, facing_block), work(1))
+        if level < count - 1:
+            zn, near = call(
+                functools.partial(near_body, level + 1),
+                "near",
+                3,
+                [MATRIX, PACKED],
+                (info, x, own, other),
                 scalars=1,
             )
-            break
-        distance = 1 << level
-        blocks = (near, swapped(near, distance))
-        zf, ends = call(far_body, "far", 3, [MATRIX, ENDS], (flag, x, own, other), scalars=1)
-        own, other = ends, swapped(ends, distance)
-        w, rest = call(
-            rhs_body, "rhs", 2, [VECTOR, RHS], (flag, x, zn, zf, own_r, other_r), scalars=1
-        )
-        own_r, other_r = rest, swapped(rest, distance)
-        kept_levels += [w, zn, zf]
-    (x,) = call(functools.partial(invert_body, 1), "invert", 12, [MATRIX], (near,), work(1))
-    low = jnp.reshape(odd, (1,))
-    prev, mid, x3, sent = call(
+    prev, mid, last, sent = call(
         functools.partial(back_body, count),
         "back",
-        8,
+        22,
         [VECTOR, VECTOR, VECTOR, (2,) + VECTOR],
-        (low, jnp.concatenate(flags), x, rest, *kept_levels, w, zn, xa, ia, hopping_block),
-        scalars=2,
+        (info, x, own, other, *held, xa, ia, hopping_block),
+        [pltpu.VMEM(MATRIX, jnp.float32)] + work(1),
+        scalars=1,
     )
     back = pair(sent)
     (mine,) = call(
@@ -543,7 +562,7 @@
         "own",
         2,
         [(2,) + VECTOR],
-        (low, xa, ia, mid, hopping_block, prev, x3),
+        (info, xa, ia, mid, hopping_block, prev, last),
         scalars=1,
     )
     return call(
@@ -551,7 +570,7 @@
         "finish",
         2,
         [source.shape, occupation.shape],
-        (jnp.reshape(side, (1,)), mine, back),
+        (info, mine, back),
         scalars=1,
     )
 

time: 191 us -> 180 us (0.942); the launches traced: 188 us -> 179 us
  waiting for transfers between devices: 21.8 us -> 44 us
  Pallas kernels: 127 us -> 111 us
  other arithmetic: 7.34 us -> 0 us
  starting transfers between devices: 19.6 us -> 13.9 us
    ppermute x9 -> x6, waiting for transfers between devices: 13.5 us -> 34.3 us  [swapped(): return lax.ppermute(array, 'slab', pairs)]
    pallas_call x21 -> x14, Pallas kernels: 127 us -> 111 us  [call(): pl.pallas_call(body, out_shape=tuple((jax.ShapeDtypeStruct(s, jnp.float32...]
    ppermute x9 -> x6, starting transfers between devices: 14.3 us -> 8.8 us  [swapped(): return lax.ppermute(array, 'slab', pairs)]
    add x2 -> x0, other arithmetic: 3.12 us -> none  [the longest x1 2.52 us: per_device(): weights = weights + coupling[mode] * (above + below)]
    sub x4 -> x0, other arithmetic: 2.56 us -> none  [per_device(): own_points + energy_count - phonon_shift[mode]]
    ppermute x2, waiting for transfers between devices: 0.01 us -> 2.54 us  [along(): return lax.ppermute(array, 'energy', pairs)]
    unnamed x32 -> x24, local copies, waits for them, and re-layouts: 8.38 us -> 7.76 us
  transfers between devices with their start and end apart: 14 -> 11, of which waited for: 5 -> 8; matrix products, arithmetic and copies ran while one was open for 5% -> 1% of each run, Pallas kernels for 61% -> 46%
where the time goes in v2:
time: 180 us; the launch traced here: 179 us
  Pallas kernels  111 us (62%)
  waiting for transfers between devices  44 us (24%)
  starting transfers between devices  13.9 us (8%)
  local copies, waits for them, and re-layouts  9.2 us (5%)
    pallas_call x14, Pallas kernels, call(): pl.pallas_call(body, out_shape=tuple((jax.ShapeDtypeStruct(s, jnp.float32...  111 us
    ppermute x6, waiting for transfers between devices, swapped(): return lax.ppermute(array, 'slab', pairs)  34.3 us
    ppermute x6, starting transfers between devices, swapped(): return lax.ppermute(array, 'slab', pairs)  8.8 us
    unnamed x24, local copies, waits for them, and re-layouts  7.76 us
    ppermute x3, waiting for transfers between devices, pair(): return lax.ppermute(array, 'slab', [(s, s ^ 1) for s in range(slabs)])  7.16 us
  transfers between devices with their start and end apart: 11, of which 8 were waited for; matrix products, arithmetic and copies ran while one was open for 1% of the time, Pallas kernels for 46%

profile of v2, /device:TPU:32, one launch (start us, length us, event | category | flops | bytes accessed | tf_op | source)
XLA Modules:
  0.0 179.2 jit_solution(2122699022701929179)
XLA Ops:
  0.6 1.7 collective-permute-start
  2.4 1.3 collective-permute-start.1
  4.4 2.5 %collective-permute-done.1.high = f32[2,2,192]{2,1,0:T(2,128)S(1)} collective-permute-done((f32[2,2,192]{2,1,0:T(2,128)}, f32[2,2,192]{2,1,0:T(2,128)S(1)}, u32[]{:S(2)}, u32[]{:S(2)}) %collective-permute-start.1) | collective-permute-done | bytes 3104 | tf_op jit(solution)/shard_map/ppermute | solution.py:470
  7.5 1.6 damping.1
  9.1 1.6 collective-permute-start.2
  10.7 0.8 dynamic-slice_bitcast_fusion
  12.0 1.0 collective-permute-done.2.theirs
  13.5 26.3 %first.1 = (f32[2,2,192,192]{3,2,1,0:T(8,128)}, f32[2,192,192]{2,1,0:T(8,128)}, f32[2,192,192]{2,1,0:T(8,128)}, f32[6,192,128]{2,1,0:T(8,128)}, f32[6,192,128]{2,1,0:T(8,128)}, /*index=5*/f32[3,192,128]{2,1,0:T(8,128)}) custom-call(s32[7]{0:T(128)} %stack.47.info, f32[192,192]{1,0:T(8,128)} %onsite.1, f32[192,192]{1,0:T(8,128)} %hop.5, ...), custom_call_target="tpu_custom_call" | custom-call | flops 32999999488 | bytes 1048576 | tf_op jit(solution)/shard_map/first/pallas_call | solution.py:214
  39.9 3.0 %collective-permute-start.4 = (f32[3,192,128]{2,1,0:T(8,128)}, f32[3,192,128]{2,1,0:T(8,128)S(1)}, u32[]{:S(2)}, u32[]{:S(2)}) collective-permute-start(f32[3,192,128]{2,1,0:T(8,128)} %get-tuple-element.34.own), channel_id=1, source_target_pairs={{8,16},{0,24},{16,8},{24,0},{40,48},{32,56},{48,40},{56,32},{72,80... | collective-permute-start | bytes 884744 | tf_op jit(solution)/shard_map/ppermute | solution.py:479
  43.6 3.3 %first_rhs.1 = (f32[2,2,192,128]{3,2,1,0:T(8,128)}, f32[4,192,128]{2,1,0:T(8,128)}, f32[4,192,128]{2,1,0:T(8,128)}) custom-call(s32[7]{0:T(128)} %stack.47.info, f32[2,2,192,192]{3,2,1,0:T(8,128)} %get-tuple-element.32.xa.refs_9_, f32[192,192]{1,0:T(8,128)} %hop.5, f32[2,2,192,128]{3,2,1,0:T(8,128)} %get-tuple-element.59.kept, f32[2,2,192,128]{3,2,1,0:T(8,128)} %copy-done.4), custom_call_target="tpu_custom_call" | custom-call | flops 3300000000 | bytes 1048576 | tf_op jit(solution)/shard_map/first_rhs/pallas_call | solution.py:214
  46.9 4.3 %rest.3 = (f32[2,192,128]{2,1,0:T(8,128)}, f32[2,192,192]{2,1,0:T(8,128)}, f32[10,192,128]{2,1,0:T(8,128)}) custom-call(s32[7]{0:T(128)} %stack.47.info, f32[2,192,192]{2,1,0:T(8,128)} %get-tuple-element.35.x, f32[2,192,192]{2,1,0:T(8,128)} %get-tuple-element.36.zn.refs_1_, f32[6,192,128]{2,1,0:T(8,128)} %get-tuple-element.37.own, ...), custom_call_target="tpu_custom_call" | custom-call | flops 5500000256 | bytes 1048576 | tf_op jit(solution)/shard_map/rest/pallas_call | solution.py:214
  52.2 12.1 %invert.3.x = f32[2,192,192]{2,1,0:T(8,128)} custom-call(f32[3,192,128]{2,1,0:T(8,128)} %get-tuple-element.34.own, f32[3,192,128]{2,1,0:T(8,128)} %copy-done.6), custom_call_target="tpu_custom_call" | custom-call | flops 13200000000 | bytes 1048576 | tf_op jit(solution)/shard_map/invert/pallas_call | solution.py:214
  64.3 12.7 %collective-permute-done.5.other.other_r = f32[10,192,128]{2,1,0:T(8,128)S(1)} collective-permute-done((f32[10,192,128]{2,1,0:T(8,128)}, f32[10,192,128]{2,1,0:T(8,128)S(1)}, u32[]{:S(2)}, u32[]{:S(2)}) %collective-permute-start.5) | collective-permute-done | bytes 983072 | tf_op jit(solution)/shard_map/ppermute | solution.py:479
  77.0 1.0 copy-done.2
  77.9 3.3 %near.2 = (f32[2,192,192]{2,1,0:T(8,128)}, f32[3,192,128]{2,1,0:T(8,128)}) custom-call(s32[7]{0:T(128)} %stack.47.info, f32[2,192,192]{2,1,0:T(8,128)} %invert.3.x, f32[10,192,128]{2,1,0:T(8,128)} %get-tuple-element.41.own.own_r, f32[10,192,128]{2,1,0:T(8,128)} %copy-done.2), custom_call_target="tpu_custom_call" | custom-call | flops 3300000000 | bytes 1048576 | tf_op jit(solution)/shard_map/near/pallas_call | solution.py:214
  81.3 4.9 %rest.4 = (f32[2,192,128]{2,1,0:T(8,128)}, f32[2,192,192]{2,1,0:T(8,128)}, f32[10,192,128]{2,1,0:T(8,128)}) custom-call(s32[7]{0:T(128)} %stack.47.info, f32[2,192,192]{2,1,0:T(8,128)} %invert.3.x, f32[2,192,192]{2,1,0:T(8,128)} %get-tuple-element.43.zn.refs_4_, f32[10,192,128]{2,1,0:T(8,128)} %get-tuple-element.41.own.own_r, f32[10,192,128]{2,1,0:T(8,128)} %copy-done.2, ...), custom_call_target="tpu_custom_call" | custom-call | flops 5500000256 | bytes 1048576 | tf_op jit(solution)/shard_map/rest/pallas_call | solution.py:214
  86.2 1.9 %collective-permute-start.7 = (f32[10,192,128]{2,1,0:T(8,128)}, f32[10,192,128]{2,1,0:T(8,128)S(1)}, u32[]{:S(2)}, u32[]{:S(2)}) collective-permute-start(f32[10,192,128]{2,1,0:T(8,128)} %get-tuple-element.44.own.own_r), channel_id=1, source_target_pairs={{8,40},{0,32},{16,48},{24,56},{40,8},{32,0},{48,16},{56,24},{72,10... | collective-permute-start | bytes 2949128 | tf_op jit(solution)/shard_map/ppermute | solution.py:479
  88.1 3.2 %collective-permute-done.6.other = f32[3,192,128]{2,1,0:T(8,128)S(1)} collective-permute-done((f32[3,192,128]{2,1,0:T(8,128)}, f32[3,192,128]{2,1,0:T(8,128)S(1)}, u32[]{:S(2)}, u32[]{:S(2)}) %collective-permute-start.6) | collective-permute-done | bytes 294944 | tf_op jit(solution)/shard_map/ppermute | solution.py:479
  92.0 12.1 %invert.4.x = f32[2,192,192]{2,1,0:T(8,128)} custom-call(f32[3,192,128]{2,1,0:T(8,128)} %get-tuple-element.42.own, f32[3,192,128]{2,1,0:T(8,128)} %copy-done.7), custom_call_target="tpu_custom_call" | custom-call | flops 13200000000 | bytes 1048576 | tf_op jit(solution)/shard_map/invert/pallas_call | solution.py:214
  104.1 7.4 %collective-permute-done.7.other.other_r = f32[10,192,128]{2,1,0:T(8,128)S(1)} collective-permute-done((f32[10,192,128]{2,1,0:T(8,128)}, f32[10,192,128]{2,1,0:T(8,128)S(1)}, u32[]{:S(2)}, u32[]{:S(2)}) %collective-permute-start.7) | collective-permute-done | bytes 983072 | tf_op jit(solution)/shard_map/ppermute | solution.py:479
  111.5 1.0 copy-done.3
  112.5 3.3 %near.3 = (f32[2,192,192]{2,1,0:T(8,128)}, f32[3,192,128]{2,1,0:T(8,128)}) custom-call(s32[7]{0:T(128)} %stack.47.info, f32[2,192,192]{2,1,0:T(8,128)} %invert.4.x, f32[10,192,128]{2,1,0:T(8,128)} %get-tuple-element.44.own.own_r, f32[10,192,128]{2,1,0:T(8,128)} %copy-done.3), custom_call_target="tpu_custom_call" | custom-call | flops 3300000000 | bytes 1048576 | tf_op jit(solution)/shard_map/near/pallas_call | solution.py:214
  115.8 3.0 %collective-permute-start.8 = (f32[3,192,128]{2,1,0:T(8,128)}, f32[3,192,128]{2,1,0:T(8,128)S(1)}, u32[]{:S(2)}, u32[]{:S(2)}) collective-permute-start(f32[3,192,128]{2,1,0:T(8,128)} %get-tuple-element.45.own), channel_id=1, source_target_pairs={{8,72},{0,64},{16,80},{24,88},{40,104},{32,96},{48,112},{56,120},{... | collective-permute-start | bytes 884744 | tf_op jit(solution)/shard_map/ppermute | solution.py:479
  118.8 4.9 %rest.5 = (f32[2,192,128]{2,1,0:T(8,128)}, f32[2,192,192]{2,1,0:T(8,128)}, f32[10,192,128]{2,1,0:T(8,128)}) custom-call(s32[7]{0:T(128)} %stack.47.info, f32[2,192,192]{2,1,0:T(8,128)} %invert.4.x, f32[2,192,192]{2,1,0:T(8,128)} %get-tuple-element.46.zn.refs_7_, f32[10,192,128]{2,1,0:T(8,128)} %get-tuple-element.44.own.own_r, f32[10,192,128]{2,1,0:T(8,128)} %copy-done.3, ...), custom_call_target="tpu_custom_call" | custom-call | flops 5500000256 | bytes 1048576 | tf_op jit(solution)/shard_map/rest/pallas_call | solution.py:214
  124.2 1.7 collective-permute-done.8.other
  126.7 12.1 %invert.5.x = f32[2,192,192]{2,1,0:T(8,128)} custom-call(f32[3,192,128]{2,1,0:T(8,128)} %get-tuple-element.45.own, f32[3,192,128]{2,1,0:T(8,128)} %copy-done.8), custom_call_target="tpu_custom_call" | custom-call | flops 13200000000 | bytes 1048576 | tf_op jit(solution)/shard_map/invert/pallas_call | solution.py:214
  138.8 9.3 %collective-permute-done.9.other = f32[10,192,128]{2,1,0:T(8,128)S(1)} collective-permute-done((f32[10,192,128]{2,1,0:T(8,128)}, f32[10,192,128]{2,1,0:T(8,128)S(1)}, u32[]{:S(2)}, u32[]{:S(2)}) %collective-permute-start.9) | collective-permute-done | bytes 983072 | tf_op jit(solution)/shard_map/ppermute | solution.py:479
  148.1 0.9 copy-done.1
  149.0 18.0 %back.1 = (f32[2,192,128]{2,1,0:T(8,128)}, f32[2,192,128]{2,1,0:T(8,128)}, f32[2,192,128]{2,1,0:T(8,128)}, f32[2,2,192,128]{3,2,1,0:T(8,128)}) custom-call(s32[7]{0:T(128)} %stack.47.info, f32[2,192,192]{2,1,0:T(8,128)} %invert.5.x, f32[10,192,128]{2,1,0:T(8,128)} %get-tuple-element.47.own, f32[10,192,128]{2,1,0:T(8,128)} %copy-done.1, ...), custom_call_target="tpu_custom_call" | custom-call | flops 24199999488 | bytes 1048576 | tf_op jit(solution)/shard_map/back/pallas_call | solution.py:214
  167.0 3.2 %own.1.mine = f32[2,2,192,128]{3,2,1,0:T(8,128)} custom-call(s32[7]{0:T(128)} %stack.47.info, f32[2,2,192,192]{3,2,1,0:T(8,128)} %get-tuple-element.32.xa.refs_9_, f32[2,2,192,128]{3,2,1,0:T(8,128)} %get-tuple-element.33.refs_10_.ia, f32[2,192,128]{2,1,0:T(8,128)} %get-tuple-element.54.mid, f32[192,192]{1,0:T(8,128)} %hop.5, ...), custom_call_target="tpu_custom_call" | custom-call | flops 2200000000 | bytes 1048576 | tf_op jit(solution)/shard_map/own/pallas_call | solution.py:214
  170.2 6.2 %collective-permute-done.10.other = f32[2,2,192,128]{3,2,1,0:T(8,128)S(1)} collective-permute-done((f32[2,2,192,128]{3,2,1,0:T(8,128)}, f32[2,2,192,128]{3,2,1,0:T(8,128)S(1)}, u32[]{:S(2)}, u32[]{:S(2)}) %collective-permute-start.10) | collective-permute-done | bytes 393248 | tf_op jit(solution)/shard_map/ppermute | solution.py:465
  177.1 2.1 %finish.1 = (f32[2,2,2,192,128]{4,3,2,1,0:T(8,128)}, f32[2,2,192]{2,1,0:T(2,128)}) custom-call(s32[7]{0:T(128)} %stack.47.info, f32[2,2,192,128]{3,2,1,0:T(8,128)} %own.1.mine, f32[2,2,192,128]{3,2,1,0:T(8,128)} %copy-done.5), custom_call_target="tpu_custom_call" | custom-call | flops 2200000000 | bytes 1048576 | tf_op jit(solution)/shard_map/finish/pallas_call | solution.py:214
  (30 shorter events, 6.9 us)
Async XLA Ops:
  0.6 3.8 %collective-permute-start = (f32[2,2,192]{2,1,0:T(2,128)}, f32[2,2,192]{2,1,0:T(2,128)S(1)}, u32[]{:S(2)}, u32[]{:S(2)}) collective-permute-start(f32[2,2,192]{2,1,0:T(2,128)} %occ.1), channel_id=1, source_target_pairs={{0,1},{1,2},{2,3},{3,4},{4,5},{5,6},{6,7},{8,9},{9,10},{10,11},{11... | collective-permute-start | bytes 9224 | tf_op jit(solution)/shard_map/ppermute | solution.py:470
  2.4 4.6 %collective-permute-start.1 = (f32[2,2,192]{2,1,0:T(2,128)}, f32[2,2,192]{2,1,0:T(2,128)S(1)}, u32[]{:S(2)}, u32[]{:S(2)}) collective-permute-start(f32[2,2,192]{2,1,0:T(2,128)} %occ.1), channel_id=1, source_target_pairs={{1,0},{2,1},{3,2},{4,3},{5,4},{6,5},{7,6},{9,8},{10,9},{11,10},{12... | collective-permute-start | bytes 9224 | tf_op jit(solution)/shard_map/ppermute | solution.py:470
  4.4 6.3 %copy-start = (f32[2,2,2,192,128]{4,3,2,1,0:T(8,128)S(1)}, f32[2,2,2,192,128]{4,3,2,1,0:T(8,128)}, u32[]{:S(2)}) copy-start(f32[2,2,2,192,128]{4,3,2,1,0:T(8,128)} %param.8) | copy-start | bytes 2359300
  4.4 2.5 %copy-start.9 = (f32[2,2,192]{2,1,0:T(2,128)}, f32[2,2,192]{2,1,0:T(2,128)S(1)}, u32[]{:S(2)}) copy-start(f32[2,2,192]{2,1,0:T(2,128)S(1)} %collective-permute-done.low) | copy-start | bytes 9220
  6.9 0.6 copy-start.10
  9.1 3.8 %collective-permute-start.2 = (f32[2,2,192]{2,1,0:T(2,128)}, f32[2,2,192]{2,1,0:T(2,128)S(1)}, u32[]{:S(2)}, u32[]{:S(2)}) collective-permute-start(f32[2,2,192]{2,1,0:T(2,128)} %get-tuple-element.31), channel_id=1, source_target_pairs={{0,8},{8,0},{16,24},{24,16},{32,40},{40,32},{48,56},{56,48},{64,72... | collective-permute-start | bytes 9224 | tf_op jit(solution)/shard_map/ppermute | solution.py:465
  11.5 31.4 %collective-permute-start.3 = (f32[2,2,192,128]{3,2,1,0:T(8,128)S(1)}, f32[2,2,192,128]{3,2,1,0:T(8,128)S(1)}, u32[]{:S(2)}, u32[]{:S(2)}) collective-permute-start(f32[2,2,192,128]{3,2,1,0:T(8,128)S(1)} %get-tuple-element.58), channel_id=1, source_target_pairs={{0,8},{8,0},{16,24},{24,16},{32,40},{40,32},{48,56},{56,48},{64,72... | collective-permute-start | bytes 1179656 | tf_op jit(solution)/shard_map/ppermute | solution.py:465
  12.9 0.6 copy-start.11
  39.9 11.6 %collective-permute-start.4 = (f32[3,192,128]{2,1,0:T(8,128)}, f32[3,192,128]{2,1,0:T(8,128)S(1)}, u32[]{:S(2)}, u32[]{:S(2)}) collective-permute-start(f32[3,192,128]{2,1,0:T(8,128)} %get-tuple-element.34.own), channel_id=1, source_target_pairs={{8,16},{0,24},{16,8},{24,0},{40,48},{32,56},{48,40},{56,32},{72,80... | collective-permute-start | bytes 884744 | tf_op jit(solution)/shard_map/ppermute | solution.py:479
  42.9 0.7 copy-start.4
  51.2 25.7 %collective-permute-start.5 = (f32[10,192,128]{2,1,0:T(8,128)}, f32[10,192,128]{2,1,0:T(8,128)S(1)}, u32[]{:S(2)}, u32[]{:S(2)}) collective-permute-start(f32[10,192,128]{2,1,0:T(8,128)} %get-tuple-element.41.own.own_r), channel_id=1, source_target_pairs={{8,16},{0,24},{16,8},{24,0},{40,48},{32,56},{48,40},{56,32},{72,80... | collective-permute-start | bytes 2949128 | tf_op jit(solution)/shard_map/ppermute | solution.py:479
  51.4 0.7 copy-start.6
  77.0 1.0 copy-start.2
  81.2 10.1 %collective-permute-start.6 = (f32[3,192,128]{2,1,0:T(8,128)}, f32[3,192,128]{2,1,0:T(8,128)S(1)}, u32[]{:S(2)}, u32[]{:S(2)}) collective-permute-start(f32[3,192,128]{2,1,0:T(8,128)} %get-tuple-element.42.own), channel_id=1, source_target_pairs={{8,40},{0,32},{16,48},{24,56},{40,8},{32,0},{48,16},{56,24},{72,10... | collective-permute-start | bytes 884744 | tf_op jit(solution)/shard_map/ppermute | solution.py:479
  86.2 25.3 %collective-permute-start.7 = (f32[10,192,128]{2,1,0:T(8,128)}, f32[10,192,128]{2,1,0:T(8,128)S(1)}, u32[]{:S(2)}, u32[]{:S(2)}) collective-permute-start(f32[10,192,128]{2,1,0:T(8,128)} %get-tuple-element.44.own.own_r), channel_id=1, source_target_pairs={{8,40},{0,32},{16,48},{24,56},{40,8},{32,0},{48,16},{56,24},{72,10... | collective-permute-start | bytes 2949128 | tf_op jit(solution)/shard_map/ppermute | solution.py:479
  91.3 0.7 copy-start.7
  111.5 1.0 copy-start.3
  115.8 10.1 %collective-permute-start.8 = (f32[3,192,128]{2,1,0:T(8,128)}, f32[3,192,128]{2,1,0:T(8,128)S(1)}, u32[]{:S(2)}, u32[]{:S(2)}) collective-permute-start(f32[3,192,128]{2,1,0:T(8,128)} %get-tuple-element.45.own), channel_id=1, source_target_pairs={{8,72},{0,64},{16,80},{24,88},{40,104},{32,96},{48,112},{56,120},{... | collective-permute-start | bytes 884744 | tf_op jit(solution)/shard_map/ppermute | solution.py:479
  123.7 24.4 %collective-permute-start.9 = (f32[10,192,128]{2,1,0:T(8,128)}, f32[10,192,128]{2,1,0:T(8,128)S(1)}, u32[]{:S(2)}, u32[]{:S(2)}) collective-permute-start(f32[10,192,128]{2,1,0:T(8,128)} %get-tuple-element.47.own), channel_id=1, source_target_pairs={{8,72},{0,64},{16,80},{24,88},{40,104},{32,96},{48,112},{56,120},{... | collective-permute-start | bytes 2949128 | tf_op jit(solution)/shard_map/ppermute | solution.py:479
  125.9 0.7 copy-start.8
  148.1 0.9 copy-start.1
  167.0 9.4 %collective-permute-start.10 = (f32[2,2,192,128]{3,2,1,0:T(8,128)}, f32[2,2,192,128]{3,2,1,0:T(8,128)S(1)}, u32[]{:S(2)}, u32[]{:S(2)}) collective-permute-start(f32[2,2,192,128]{3,2,1,0:T(8,128)} %get-tuple-element.57), channel_id=1, source_target_pairs={{0,8},{8,0},{16,24},{24,16},{32,40},{40,32},{48,56},{56,48},{64,72... | collective-permute-start | bytes 1179656 | tf_op jit(solution)/shard_map/ppermute | solution.py:465
  176.4 0.8 copy-start.5

commit v3 on v2

--- a/solution.py
+++ b/solution.py
@@ -230,7 +230,6 @@
 VECTOR = (2, N, COLS)
 ENDS = (6, N, 128)
 RHS = (4, N, COLS)
-MESSAGE = (10, N, 128)
 
 
 def work(B):
@@ -361,28 +360,28 @@
     near_end(info[3 + level], get(x), own, other, zn, lambda v: pack(near, v))
 
 
-def rhs_ends(ref, base):
-    return (ref[base], ref[base + 1]), (ref[base + 2], ref[base + 3])
-
-
-def rest_body(level, base, info, x, zn, own, other, own_r, other_r, w, zf, out):
+def rhs_ends(ref):
+    return (ref[0], ref[1]), (ref[2], ref[3])
+
+
+def rest_body(level, info, x, zn, own, other, own_r, other_r, w, zf, out, out_r):
     flag = info[3 + level]
     xs = csplit(get(x))
     zns = csplit(get(zn))
     t_near = csplit(choose(flag, coupling_of(other), coupling_of(own)))
     t_far = csplit(choose(flag, coupling_of(own), coupling_of(other)))
-    mine, mine_far = rhs_ends(own_r, base)
-    theirs, theirs_far = rhs_ends(other_r, base)
+    mine, mine_far = rhs_ends(own_r)
+    theirs, theirs_far = rhs_ends(other_r)
     r = add(mine, theirs)
     z = cdot(nn, t_far, xs)
     put(w, vdot(nn, xs, r))
-    put(out.at[pl.ds(6, 2)], sub(choose(flag, theirs_far, mine_far), vdot(nn, zns, r)))
+    put(out_r.at[pl.ds(0, 2)], sub(choose(flag, theirs_far, mine_far), vdot(nn, zns, r)))
     put(zf, z)
     z = csplit(z)
     pack(out.at[pl.ds(0, 3)], neg(cdot(nt, z, t_near)))
     f = choose(flag, end_block(own), end_block(other))
     pack(out.at[pl.ds(3, 3)], sub(f, cdot(nt, z, t_far)))
-    put(out.at[pl.ds(8, 2)], sub(choose(flag, mine_far, theirs_far), vdot(nn, z, r)))
+    put(out_r.at[pl.ds(2, 2)], sub(choose(flag, mine_far, theirs_far), vdot(nn, z, r)))
 
 
 def solve_pair(low, xa, ia, hop, prev, middle, last, out):
@@ -395,7 +394,7 @@
     put(out.at[1], second)
 
 
-def back_body(count, info, x, own, other, *refs):
+def back_body(count, info, x, own, other, own_r, other_r, *refs):
     levels = [refs[3 * i : 3 * i + 3] for i in range(count)]
     xa, ia, hop, prev_out, mid, last_out, out, zn, ar, ai, m = refs[3 * count :]
     flag = info[3 + count]
@@ -406,8 +405,8 @@
         ai[0, :, 0:N] = v[1]
 
     near_end(flag, xs, own, other, zn, store)
-    mine, mine_far = rhs_ends(own, 6)
-    theirs, theirs_far = rhs_ends(other, 6)
+    mine, mine_far = rhs_ends(own_r)
+    theirs, theirs_far = rhs_ends(other_r)
     r = add(mine, theirs)
     w = vdot(nn, csplit(xs), r)
     rest = sub(choose(flag, theirs_far, mine_far), vdot(nn, csplit(get(zn)), r))
@@ -526,17 +525,17 @@
     for level in range(count):
         distance = 1 << level
         facing_block = swapped(near, distance)
-        w, zf, rest = call(
-            functools.partial(rest_body, level, 6 if level else 0),
+        w, zf, ends, sides = call(
+            functools.partial(rest_body, level),
             "rest",
             5,
-            [VECTOR, MATRIX, MESSAGE],
+            [VECTOR, MATRIX, ENDS, RHS],
             (info, x, zn, own, other, own_r, other_r),
             scalars=1,
         )
         held += [w, zn, zf]
-        own = own_r = rest
-        other = other_r = swapped(rest, distance)
+        own, other = ends, swapped(ends, distance)
+        own_r, other_r = sides, swapped(sides, distance)
         (x,) = call(invert_body, "invert", 12, [MATRIX], (near, facing_block), work(1))
         if level < count - 1:
             zn, near = call(
@@ -552,7 +551,7 @@
         "back",
         22,
         [VECTOR, VECTOR, VECTOR, (2,) + VECTOR],
-        (info, x, own, other, *held, xa, ia, hopping_block),
+        (info, x, own, other, own_r, other_r, *held, xa, ia, hopping_block),
         [pltpu.VMEM(MATRIX, jnp.float32)] + work(1),
         scalars=1,
     )

time: 180 us -> 179 us (level)
  waiting for transfers between devices: 44 us -> 37.6 us
  starting transfers between devices: 13.9 us -> 20.1 us
    ppermute x6 -> x9, waiting for transfers between devices: 34.3 us -> 27.9 us  [swapped(): return lax.ppermute(array, 'slab', pairs)]
    ppermute x6 -> x9, starting transfers between devices: 8.8 us -> 15 us  [swapped(): return lax.ppermute(array, 'slab', pairs)]
    pallas_call x14, Pallas kernels: 111 us -> 110 us  [call(): pl.pallas_call(body, out_shape=tuple((jax.ShapeDtypeStruct(s, jnp.float32...]
    unnamed x24 -> x30, local copies, waits for them, and re-layouts: 7.76 us -> 8.93 us
  transfers between devices with their start and end apart: 11 -> 14, of which waited for: 8 -> 7; matrix products, arithmetic and copies ran while one was open for 1% -> 1% of each run, Pallas kernels for 46% -> 49%
where the time goes in v3:
time: 179 us; the launch traced here: 178 us
  Pallas kernels  110 us (61%)
  waiting for transfers between devices  37.6 us (21%)
  starting transfers between devices  20.1 us (11%)
  local copies, waits for them, and re-layouts  10.4 us (6%)
    pallas_call x14, Pallas kernels, call(): pl.pallas_call(body, out_shape=tuple((jax.ShapeDtypeStruct(s, jnp.float32...  110 us
    ppermute x9, waiting for transfers between devices, swapped(): return lax.ppermute(array, 'slab', pairs)  27.9 us
    ppermute x9, starting transfers between devices, swapped(): return lax.ppermute(array, 'slab', pairs)  15 us
    unnamed x30, local copies, waits for them, and re-layouts  8.93 us
    ppermute x3, waiting for transfers between devices, pair(): return lax.ppermute(array, 'slab', [(s, s ^ 1) for s in range(slabs)])  7.17 us
  transfers between devices with their start and end apart: 14, of which 7 were waited for; matrix products, arithmetic and copies ran while one was open for 1% of the time, Pallas kernels for 49%

profile of v3, /device:TPU:32, one launch (start us, length us, event | category | flops | bytes accessed | tf_op | source)
XLA Modules:
  0.0 178.4 jit_solution(5698070412197108592)
XLA Ops:
  0.6 1.7 collective-permute-start
  2.4 1.3 collective-permute-start.1
  4.4 2.5 %collective-permute-done.1.high = f32[2,2,192]{2,1,0:T(2,128)S(1)} collective-permute-done((f32[2,2,192]{2,1,0:T(2,128)}, f32[2,2,192]{2,1,0:T(2,128)S(1)}, u32[]{:S(2)}, u32[]{:S(2)}) %collective-permute-start.1) | collective-permute-done | bytes 3104 | tf_op jit(solution)/shard_map/ppermute | solution.py:469
  7.5 1.6 damping.1
  9.1 1.6 collective-permute-start.2
  11.9 1.0 collective-permute-done.2.theirs
  13.5 26.3 %first.1 = (f32[2,2,192,192]{3,2,1,0:T(8,128)}, f32[2,192,192]{2,1,0:T(8,128)}, f32[2,192,192]{2,1,0:T(8,128)}, f32[6,192,128]{2,1,0:T(8,128)}, f32[6,192,128]{2,1,0:T(8,128)}, /*index=5*/f32[3,192,128]{2,1,0:T(8,128)}) custom-call(s32[7]{0:T(128)} %stack.47.info, f32[192,192]{1,0:T(8,128)} %onsite.1, f32[192,192]{1,0:T(8,128)} %hop.5, ...), custom_call_target="tpu_custom_call" | custom-call | flops 32999999488 | bytes 1048576 | tf_op jit(solution)/shard_map/first/pallas_call | solution.py:214
  39.8 3.0 %collective-permute-start.4 = (f32[3,192,128]{2,1,0:T(8,128)}, f32[3,192,128]{2,1,0:T(8,128)S(1)}, u32[]{:S(2)}, u32[]{:S(2)}) collective-permute-start(f32[3,192,128]{2,1,0:T(8,128)} %get-tuple-element.37.own), channel_id=1, source_target_pairs={{8,16},{0,24},{16,8},{24,0},{40,48},{32,56},{48,40},{56,32},{72,80... | collective-permute-start | bytes 884744 | tf_op jit(solution)/shard_map/ppermute | solution.py:478
  43.6 3.3 %first_rhs.1 = (f32[2,2,192,128]{3,2,1,0:T(8,128)}, f32[4,192,128]{2,1,0:T(8,128)}, f32[4,192,128]{2,1,0:T(8,128)}) custom-call(s32[7]{0:T(128)} %stack.47.info, f32[2,2,192,192]{3,2,1,0:T(8,128)} %get-tuple-element.35.xa.refs_9_, f32[192,192]{1,0:T(8,128)} %hop.5, f32[2,2,192,128]{3,2,1,0:T(8,128)} %get-tuple-element.65.kept, f32[2,2,192,128]{3,2,1,0:T(8,128)} %copy-done.7), custom_call_target="tpu_custom_call" | custom-call | flops 3300000000 | bytes 1048576 | tf_op jit(solution)/shard_map/first_rhs/pallas_call | solution.py:214
  47.0 4.3 %rest.3 = (f32[2,192,128]{2,1,0:T(8,128)}, f32[2,192,192]{2,1,0:T(8,128)}, f32[6,192,128]{2,1,0:T(8,128)}, f32[4,192,128]{2,1,0:T(8,128)}) custom-call(s32[7]{0:T(128)} %stack.47.info, f32[2,192,192]{2,1,0:T(8,128)} %get-tuple-element.38.x, f32[2,192,192]{2,1,0:T(8,128)} %get-tuple-element.39.zn.refs_1_, f32[6,192,128]{2,1,0:T(8,128)} %get-tuple-element.40.own, ...), custom_call_target="tpu_custom_call" | custom-call | flops 5500000256 | bytes 1048576 | tf_op jit(solution)/shard_map/rest/pallas_call | solution.py:214
  51.4 3.0 %collective-permute-start.5 = (f32[6,192,128]{2,1,0:T(8,128)}, f32[6,192,128]{2,1,0:T(8,128)S(1)}, u32[]{:S(2)}, u32[]{:S(2)}) collective-permute-start(f32[6,192,128]{2,1,0:T(8,128)} %get-tuple-element.44.own), channel_id=1, source_target_pairs={{8,16},{0,24},{16,8},{24,0},{40,48},{32,56},{48,40},{56,32},{72,80... | collective-permute-start | bytes 1769480 | tf_op jit(solution)/shard_map/ppermute | solution.py:478
  55.2 12.1 %invert.3.x = f32[2,192,192]{2,1,0:T(8,128)} custom-call(f32[3,192,128]{2,1,0:T(8,128)} %get-tuple-element.37.own, f32[3,192,128]{2,1,0:T(8,128)} %copy-done.9), custom_call_target="tpu_custom_call" | custom-call | flops 13200000000 | bytes 1048576 | tf_op jit(solution)/shard_map/invert/pallas_call | solution.py:214
  67.2 9.7 %collective-permute-done.5.other = f32[6,192,128]{2,1,0:T(8,128)S(1)} collective-permute-done((f32[6,192,128]{2,1,0:T(8,128)}, f32[6,192,128]{2,1,0:T(8,128)S(1)}, u32[]{:S(2)}, u32[]{:S(2)}) %collective-permute-start.5) | collective-permute-done | bytes 589856 | tf_op jit(solution)/shard_map/ppermute | solution.py:478
  77.0 0.8 copy-done.2
  77.8 3.0 %near.2 = (f32[2,192,192]{2,1,0:T(8,128)}, f32[3,192,128]{2,1,0:T(8,128)}) custom-call(s32[7]{0:T(128)} %stack.47.info, f32[2,192,192]{2,1,0:T(8,128)} %invert.3.x, f32[6,192,128]{2,1,0:T(8,128)} %get-tuple-element.44.own, f32[6,192,128]{2,1,0:T(8,128)} %copy-done.2), custom_call_target="tpu_custom_call" | custom-call | flops 3300000000 | bytes 1048576 | tf_op jit(solution)/shard_map/near/pallas_call | solution.py:214
  81.7 4.3 %rest.4 = (f32[2,192,128]{2,1,0:T(8,128)}, f32[2,192,192]{2,1,0:T(8,128)}, f32[6,192,128]{2,1,0:T(8,128)}, f32[4,192,128]{2,1,0:T(8,128)}) custom-call(s32[7]{0:T(128)} %stack.47.info, f32[2,192,192]{2,1,0:T(8,128)} %invert.3.x, f32[2,192,192]{2,1,0:T(8,128)} %get-tuple-element.46.zn.refs_4_, f32[6,192,128]{2,1,0:T(8,128)} %get-tuple-element.44.own, ...), custom_call_target="tpu_custom_call" | custom-call | flops 5500000256 | bytes 1048576 | tf_op jit(solution)/shard_map/rest/pallas_call | solution.py:214
  86.0 1.9 %collective-permute-start.10 = (f32[4,192,128]{2,1,0:T(8,128)}, f32[4,192,128]{2,1,0:T(8,128)S(1)}, u32[]{:S(2)}, u32[]{:S(2)}) collective-permute-start(f32[4,192,128]{2,1,0:T(8,128)} %get-tuple-element.51.own_r), channel_id=1, source_target_pairs={{8,40},{0,32},{16,48},{24,56},{40,8},{32,0},{48,16},{56,24},{72,10... | collective-permute-start | bytes 1179656 | tf_op jit(solution)/shard_map/ppermute | solution.py:478
  88.2 2.8 %collective-permute-done.6.other = f32[3,192,128]{2,1,0:T(8,128)S(1)} collective-permute-done((f32[3,192,128]{2,1,0:T(8,128)}, f32[3,192,128]{2,1,0:T(8,128)S(1)}, u32[]{:S(2)}, u32[]{:S(2)}) %collective-permute-start.6) | collective-permute-done | bytes 294944 | tf_op jit(solution)/shard_map/ppermute | solution.py:478
  91.6 12.1 %invert.4.x = f32[2,192,192]{2,1,0:T(8,128)} custom-call(f32[3,192,128]{2,1,0:T(8,128)} %get-tuple-element.45.own, f32[3,192,128]{2,1,0:T(8,128)} %copy-done.10), custom_call_target="tpu_custom_call" | custom-call | flops 13200000000 | bytes 1048576 | tf_op jit(solution)/shard_map/invert/pallas_call | solution.py:214
  103.7 7.4 %collective-permute-done.8.other = f32[6,192,128]{2,1,0:T(8,128)S(1)} collective-permute-done((f32[6,192,128]{2,1,0:T(8,128)}, f32[6,192,128]{2,1,0:T(8,128)S(1)}, u32[]{:S(2)}, u32[]{:S(2)}) %collective-permute-start.8) | collective-permute-done | bytes 589856 | tf_op jit(solution)/shard_map/ppermute | solution.py:478
  111.1 0.8 copy-done.3
  112.0 3.0 %near.3 = (f32[2,192,192]{2,1,0:T(8,128)}, f32[3,192,128]{2,1,0:T(8,128)}) custom-call(s32[7]{0:T(128)} %stack.47.info, f32[2,192,192]{2,1,0:T(8,128)} %invert.4.x, f32[6,192,128]{2,1,0:T(8,128)} %get-tuple-element.48.own, f32[6,192,128]{2,1,0:T(8,128)} %copy-done.3), custom_call_target="tpu_custom_call" | custom-call | flops 3300000000 | bytes 1048576 | tf_op jit(solution)/shard_map/near/pallas_call | solution.py:214
  115.0 3.0 %collective-permute-start.9 = (f32[3,192,128]{2,1,0:T(8,128)}, f32[3,192,128]{2,1,0:T(8,128)S(1)}, u32[]{:S(2)}, u32[]{:S(2)}) collective-permute-start(f32[3,192,128]{2,1,0:T(8,128)} %get-tuple-element.49.own), channel_id=1, source_target_pairs={{8,72},{0,64},{16,80},{24,88},{40,104},{32,96},{48,112},{56,120},{... | collective-permute-start | bytes 884744 | tf_op jit(solution)/shard_map/ppermute | solution.py:478
  118.7 4.2 %rest.5 = (f32[2,192,128]{2,1,0:T(8,128)}, f32[2,192,192]{2,1,0:T(8,128)}, f32[6,192,128]{2,1,0:T(8,128)}, f32[4,192,128]{2,1,0:T(8,128)}) custom-call(s32[7]{0:T(128)} %stack.47.info, f32[2,192,192]{2,1,0:T(8,128)} %invert.4.x, f32[2,192,192]{2,1,0:T(8,128)} %get-tuple-element.50.zn.refs_7_, f32[6,192,128]{2,1,0:T(8,128)} %get-tuple-element.48.own, ...), custom_call_target="tpu_custom_call" | custom-call | flops 5500000256 | bytes 1048576 | tf_op jit(solution)/shard_map/rest/pallas_call | solution.py:214
  123.5 3.0 %collective-permute-start.11 = (f32[6,192,128]{2,1,0:T(8,128)}, f32[6,192,128]{2,1,0:T(8,128)S(1)}, u32[]{:S(2)}, u32[]{:S(2)}) collective-permute-start(f32[6,192,128]{2,1,0:T(8,128)} %get-tuple-element.52.own), channel_id=1, source_target_pairs={{8,72},{0,64},{16,80},{24,88},{40,104},{32,96},{48,112},{56,120},{... | collective-permute-start | bytes 1769480 | tf_op jit(solution)/shard_map/ppermute | solution.py:478
  127.2 12.1 %invert.5.x = f32[2,192,192]{2,1,0:T(8,128)} custom-call(f32[3,192,128]{2,1,0:T(8,128)} %get-tuple-element.49.own, f32[3,192,128]{2,1,0:T(8,128)} %copy-done.11), custom_call_target="tpu_custom_call" | custom-call | flops 13200000000 | bytes 1048576 | tf_op jit(solution)/shard_map/invert/pallas_call | solution.py:214
  139.3 8.0 %collective-permute-done.11.other = f32[6,192,128]{2,1,0:T(8,128)S(1)} collective-permute-done((f32[6,192,128]{2,1,0:T(8,128)}, f32[6,192,128]{2,1,0:T(8,128)S(1)}, u32[]{:S(2)}, u32[]{:S(2)}) %collective-permute-start.11) | collective-permute-done | bytes 589856 | tf_op jit(solution)/shard_map/ppermute | solution.py:478
  147.3 0.9 copy-done.1
  148.2 18.0 %back.1 = (f32[2,192,128]{2,1,0:T(8,128)}, f32[2,192,128]{2,1,0:T(8,128)}, f32[2,192,128]{2,1,0:T(8,128)}, f32[2,2,192,128]{3,2,1,0:T(8,128)}) custom-call(s32[7]{0:T(128)} %stack.47.info, f32[2,192,192]{2,1,0:T(8,128)} %invert.5.x, f32[6,192,128]{2,1,0:T(8,128)} %get-tuple-element.52.own, f32[6,192,128]{2,1,0:T(8,128)} %copy-done.1, ...), custom_call_target="tpu_custom_call" | custom-call | flops 24199999488 | bytes 1048576 | tf_op jit(solution)/shard_map/back/pallas_call | solution.py:214
  166.3 3.2 %own.1.mine = f32[2,2,192,128]{3,2,1,0:T(8,128)} custom-call(s32[7]{0:T(128)} %stack.47.info, f32[2,2,192,192]{3,2,1,0:T(8,128)} %get-tuple-element.35.xa.refs_9_, f32[2,2,192,128]{3,2,1,0:T(8,128)} %get-tuple-element.36.refs_10_.ia, f32[2,192,128]{2,1,0:T(8,128)} %get-tuple-element.60.mid, f32[192,192]{1,0:T(8,128)} %hop.5, ...), custom_call_target="tpu_custom_call" | custom-call | flops 2200000000 | bytes 1048576 | tf_op jit(solution)/shard_map/own/pallas_call | solution.py:214
  169.4 6.2 %collective-permute-done.13.other = f32[2,2,192,128]{3,2,1,0:T(8,128)S(1)} collective-permute-done((f32[2,2,192,128]{3,2,1,0:T(8,128)}, f32[2,2,192,128]{3,2,1,0:T(8,128)S(1)}, u32[]{:S(2)}, u32[]{:S(2)}) %collective-permute-start.13) | collective-permute-done | bytes 393248 | tf_op jit(solution)/shard_map/ppermute | solution.py:464
  176.4 2.1 %finish.1 = (f32[2,2,2,192,128]{4,3,2,1,0:T(8,128)}, f32[2,2,192]{2,1,0:T(2,128)}) custom-call(s32[7]{0:T(128)} %stack.47.info, f32[2,2,192,128]{3,2,1,0:T(8,128)} %own.1.mine, f32[2,2,192,128]{3,2,1,0:T(8,128)} %copy-done.8), custom_call_target="tpu_custom_call" | custom-call | flops 2200000000 | bytes 1048576 | tf_op jit(solution)/shard_map/finish/pallas_call | solution.py:214
  (42 shorter events, 9.5 us)
Async XLA Ops:
  0.6 3.8 %collective-permute-start = (f32[2,2,192]{2,1,0:T(2,128)}, f32[2,2,192]{2,1,0:T(2,128)S(1)}, u32[]{:S(2)}, u32[]{:S(2)}) collective-permute-start(f32[2,2,192]{2,1,0:T(2,128)} %occ.1), channel_id=1, source_target_pairs={{0,1},{1,2},{2,3},{3,4},{4,5},{5,6},{6,7},{8,9},{9,10},{10,11},{11... | collective-permute-start | bytes 9224 | tf_op jit(solution)/shard_map/ppermute | solution.py:469
  2.4 4.6 %collective-permute-start.1 = (f32[2,2,192]{2,1,0:T(2,128)}, f32[2,2,192]{2,1,0:T(2,128)S(1)}, u32[]{:S(2)}, u32[]{:S(2)}) collective-permute-start(f32[2,2,192]{2,1,0:T(2,128)} %occ.1), channel_id=1, source_target_pairs={{1,0},{2,1},{3,2},{4,3},{5,4},{6,5},{7,6},{9,8},{10,9},{11,10},{12... | collective-permute-start | bytes 9224 | tf_op jit(solution)/shard_map/ppermute | solution.py:469
  4.4 6.3 %copy-start = (f32[2,2,2,192,128]{4,3,2,1,0:T(8,128)S(1)}, f32[2,2,2,192,128]{4,3,2,1,0:T(8,128)}, u32[]{:S(2)}) copy-start(f32[2,2,2,192,128]{4,3,2,1,0:T(8,128)} %param.8) | copy-start | bytes 2359300
  4.4 2.5 %copy-start.12 = (f32[2,2,192]{2,1,0:T(2,128)}, f32[2,2,192]{2,1,0:T(2,128)S(1)}, u32[]{:S(2)}) copy-start(f32[2,2,192]{2,1,0:T(2,128)S(1)} %collective-permute-done.low) | copy-start | bytes 9220
  6.9 0.6 copy-start.13
  9.1 3.8 %collective-permute-start.2 = (f32[2,2,192]{2,1,0:T(2,128)}, f32[2,2,192]{2,1,0:T(2,128)S(1)}, u32[]{:S(2)}, u32[]{:S(2)}) collective-permute-start(f32[2,2,192]{2,1,0:T(2,128)} %get-tuple-element.34), channel_id=1, source_target_pairs={{0,8},{8,0},{16,24},{24,16},{32,40},{40,32},{48,56},{56,48},{64,72... | collective-permute-start | bytes 9224 | tf_op jit(solution)/shard_map/ppermute | solution.py:464
  11.5 31.4 %collective-permute-start.3 = (f32[2,2,192,128]{3,2,1,0:T(8,128)S(1)}, f32[2,2,192,128]{3,2,1,0:T(8,128)S(1)}, u32[]{:S(2)}, u32[]{:S(2)}) collective-permute-start(f32[2,2,192,128]{3,2,1,0:T(8,128)S(1)} %get-tuple-element.64), channel_id=1, source_target_pairs={{0,8},{8,0},{16,24},{24,16},{32,40},{40,32},{48,56},{56,48},{64,72... | collective-permute-start | bytes 1179656 | tf_op jit(solution)/shard_map/ppermute | solution.py:464
  12.9 0.6 copy-start.14
  39.8 14.6 %collective-permute-start.4 = (f32[3,192,128]{2,1,0:T(8,128)}, f32[3,192,128]{2,1,0:T(8,128)S(1)}, u32[]{:S(2)}, u32[]{:S(2)}) collective-permute-start(f32[3,192,128]{2,1,0:T(8,128)} %get-tuple-element.37.own), channel_id=1, source_target_pairs={{8,16},{0,24},{16,8},{24,0},{40,48},{32,56},{48,40},{56,32},{72,80... | collective-permute-start | bytes 884744 | tf_op jit(solution)/shard_map/ppermute | solution.py:478
  42.9 0.8 copy-start.7
  51.2 29.7 %collective-permute-start.7 = (f32[4,192,128]{2,1,0:T(8,128)}, f32[4,192,128]{2,1,0:T(8,128)S(1)}, u32[]{:S(2)}, u32[]{:S(2)}) collective-permute-start(f32[4,192,128]{2,1,0:T(8,128)} %get-tuple-element.47.own_r), channel_id=1, source_target_pairs={{8,16},{0,24},{16,8},{24,0},{40,48},{32,56},{48,40},{56,32},{72,80... | collective-permute-start | bytes 1179656 | tf_op jit(solution)/shard_map/ppermute | solution.py:478
  51.4 25.5 %collective-permute-start.5 = (f32[6,192,128]{2,1,0:T(8,128)}, f32[6,192,128]{2,1,0:T(8,128)S(1)}, u32[]{:S(2)}, u32[]{:S(2)}) collective-permute-start(f32[6,192,128]{2,1,0:T(8,128)} %get-tuple-element.44.own), channel_id=1, source_target_pairs={{8,16},{0,24},{16,8},{24,0},{40,48},{32,56},{48,40},{56,32},{72,80... | collective-permute-start | bytes 1769480 | tf_op jit(solution)/shard_map/ppermute | solution.py:478
  54.4 0.7 copy-start.9
  77.0 0.8 copy-start.2
  80.8 10.1 %collective-permute-start.6 = (f32[3,192,128]{2,1,0:T(8,128)}, f32[3,192,128]{2,1,0:T(8,128)S(1)}, u32[]{:S(2)}, u32[]{:S(2)}) collective-permute-start(f32[3,192,128]{2,1,0:T(8,128)} %get-tuple-element.45.own), channel_id=1, source_target_pairs={{8,40},{0,32},{16,48},{24,56},{40,8},{32,0},{48,16},{56,24},{72,10... | collective-permute-start | bytes 884744 | tf_op jit(solution)/shard_map/ppermute | solution.py:478
  80.9 0.8 copy-start.5
  86.0 32.0 %collective-permute-start.10 = (f32[4,192,128]{2,1,0:T(8,128)}, f32[4,192,128]{2,1,0:T(8,128)S(1)}, u32[]{:S(2)}, u32[]{:S(2)}) collective-permute-start(f32[4,192,128]{2,1,0:T(8,128)} %get-tuple-element.51.own_r), channel_id=1, source_target_pairs={{8,40},{0,32},{16,48},{24,56},{40,8},{32,0},{48,16},{56,24},{72,10... | collective-permute-start | bytes 1179656 | tf_op jit(solution)/shard_map/ppermute | solution.py:478
  87.9 23.2 %collective-permute-start.8 = (f32[6,192,128]{2,1,0:T(8,128)}, f32[6,192,128]{2,1,0:T(8,128)S(1)}, u32[]{:S(2)}, u32[]{:S(2)}) collective-permute-start(f32[6,192,128]{2,1,0:T(8,128)} %get-tuple-element.48.own), channel_id=1, source_target_pairs={{8,40},{0,32},{16,48},{24,56},{40,8},{32,0},{48,16},{56,24},{72,10... | collective-permute-start | bytes 1769480 | tf_op jit(solution)/shard_map/ppermute | solution.py:478
  90.9 0.7 copy-start.10
  111.1 0.8 copy-start.3
  115.0 11.5 %collective-permute-start.9 = (f32[3,192,128]{2,1,0:T(8,128)}, f32[3,192,128]{2,1,0:T(8,128)S(1)}, u32[]{:S(2)}, u32[]{:S(2)}) collective-permute-start(f32[3,192,128]{2,1,0:T(8,128)} %get-tuple-element.49.own), channel_id=1, source_target_pairs={{8,72},{0,64},{16,80},{24,88},{40,104},{32,96},{48,112},{56,120},{... | collective-permute-start | bytes 884744 | tf_op jit(solution)/shard_map/ppermute | solution.py:478
  118.0 0.7 copy-start.6
  123.0 16.3 %collective-permute-start.12 = (f32[4,192,128]{2,1,0:T(8,128)}, f32[4,192,128]{2,1,0:T(8,128)S(1)}, u32[]{:S(2)}, u32[]{:S(2)}) collective-permute-start(f32[4,192,128]{2,1,0:T(8,128)} %get-tuple-element.53.own_r), channel_id=1, source_target_pairs={{8,72},{0,64},{16,80},{24,88},{40,104},{32,96},{48,112},{56,120},{... | collective-permute-start | bytes 1179656 | tf_op jit(solution)/shard_map/ppermute | solution.py:478
  123.5 23.8 %collective-permute-start.11 = (f32[6,192,128]{2,1,0:T(8,128)}, f32[6,192,128]{2,1,0:T(8,128)S(1)}, u32[]{:S(2)}, u32[]{:S(2)}) collective-permute-start(f32[6,192,128]{2,1,0:T(8,128)} %get-tuple-element.52.own), channel_id=1, source_target_pairs={{8,72},{0,64},{16,80},{24,88},{40,104},{32,96},{48,112},{56,120},{... | collective-permute-start | bytes 1769480 | tf_op jit(solution)/shard_map/ppermute | solution.py:478
  126.5 0.7 copy-start.11
  139.3 8.0 %copy-start.4 = (f32[4,192,128]{2,1,0:T(8,128)}, f32[4,192,128]{2,1,0:T(8,128)S(1)}, u32[]{:S(2)}) copy-start(f32[4,192,128]{2,1,0:T(8,128)S(1)} %collective-permute-done.12.other_r) | copy-start | bytes 1179652
  147.3 0.9 copy-start.1
  166.2 9.4 %collective-permute-start.13 = (f32[2,2,192,128]{3,2,1,0:T(8,128)}, f32[2,2,192,128]{3,2,1,0:T(8,128)S(1)}, u32[]{:S(2)}, u32[]{:S(2)}) collective-permute-start(f32[2,2,192,128]{3,2,1,0:T(8,128)} %get-tuple-element.63), channel_id=1, source_target_pairs={{0,8},{8,0},{16,24},{24,16},{32,40},{40,32},{48,56},{56,48},{64,72... | collective-permute-start | bytes 1179656 | tf_op jit(solution)/shard_map/ppermute | solution.py:464
  175.6 0.8 copy-start.8

commit v4 on v3

--- a/solution.py
+++ b/solution.py
@@ -30,7 +30,7 @@
     return jnp.broadcast_to(row, (8, 128))
 
 
-def invert_eight(cr, ci):
+def solve_eight(cr, ci, now, side):
     row = lax.broadcasted_iota(jnp.int32, (8, 128), 0)
     for p in range(8):
         dr, di = spread(cr[p][p : p + 1]), spread(ci[p][p : p + 1])
@@ -39,13 +39,28 @@
         here = row == p
         wr = jnp.where(here, 1.0 - er, cr[p] * er - ci[p] * ei)
         wi = jnp.where(here, -ei, cr[p] * ei + ci[p] * er)
-        for j in range(8):
-            if j != p:
-                fr, fi = spread(cr[j][p : p + 1]), spread(ci[j][p : p + 1])
-                cr[j], ci[j] = cr[j] - (wr * fr - wi * fi), ci[j] - (wr * fi + wi * fr)
-        cr[p] = jnp.where(here, er, -wr)
-        ci[p] = jnp.where(here, ei, -wi)
-    return cr, ci
+        for j in range(p + 1, 8):
+            fr, fi = spread(cr[j][p : p + 1]), spread(ci[j][p : p + 1])
+            cr[j], ci[j] = cr[j] - (wr * fr - wi * fi), ci[j] - (wr * fi + wi * fr)
+        n, t = spread(now[p : p + 1]), spread(side[p : p + 1])
+        now, side = now - (wr * n + wi * t), side - (wr * t - wi * n)
+    return now, side
+
+
+def take(x, index):
+    return lax.gather(
+        x,
+        index[:, :, None],
+        lax.GatherDimensionNumbers(
+            offset_dims=(),
+            collapsed_slice_dims=(1,),
+            start_index_map=(1,),
+            operand_batching_dims=(0,),
+            start_indices_batching_dims=(0,),
+        ),
+        slice_sizes=(1, 1),
+        mode=lax.GatherScatterMode.PROMISE_IN_BOUNDS,
+    )
 
 
 def small_inverse(m):
@@ -62,19 +77,16 @@
         o = pl.multiple_of(8 * g, 8)
         own = m[pl.ds(o, 8), :]
         parts = [m[8 * h : 8 * h + 8, :] for h in range(4)]
-        take = lambda x, j: jnp.take_along_axis(x, start + (o + j), axis=1)
-        cr = [take(own, j) for j in range(8)]
-        ci = [take(own, j + 32) for j in range(8)]
-        wide_r = [[take(x, j) for j in range(8)] for x in parts]
-        wide_i = [[take(x, j + 32) for j in range(8)] for x in parts]
+        at = [start + (o + j) for j in range(8)]
+        far = [a + 32 for a in at]
+        cr = [take(own, a) for a in at]
+        ci = [take(own, a) for a in far]
+        wide_r = [[take(x, a) for a in at] for x in parts]
+        wide_i = [[take(x, a) for a in far] for x in parts]
         inside = (off >= o) & (off < o + 8)
         eye = jnp.where(real & (off - o == row), 1.0, 0.0)
         now = jnp.where(inside, eye, own)
-        side = turned(now)
-        rows = [(spread(now[j : j + 1]), spread(side[j : j + 1])) for j in range(8)]
-        cr, ci = invert_eight(cr, ci)
-        out = sum(cr[j] * rows[j][0] + ci[j] * rows[j][1] for j in range(8))
-        turn = sum(cr[j] * rows[j][1] - ci[j] * rows[j][0] for j in range(8))
+        out, turn = solve_eight(cr, ci, now, turned(now))
         for h in range(4):
             x = jnp.where(inside, 0.0, parts[h])
             for j in range(8):
@@ -210,7 +222,7 @@
     )
 
 
-def call(body, name, cost, outs, args, scratch=(), scalars=0):
+def call(body, cost, outs, args, scratch=(), scalars=0):
     return pl.pallas_call(
         body,
         out_shape=tuple(jax.ShapeDtypeStruct(s, jnp.float32) for s in outs),
@@ -218,7 +230,6 @@
         + [pl.BlockSpec(memory_space=pltpu.VMEM)] * (len(args) - scalars),
         out_specs=tuple(pl.BlockSpec(memory_space=pltpu.VMEM) for _ in outs),
         scratch_shapes=list(scratch),
-        name=name,
         cost_estimate=pl.CostEstimate(
             flops=int(cost * 1.1e9), bytes_accessed=1 << 20, transcendentals=0
         ),
@@ -460,6 +471,7 @@
     place = lax.axis_index("slab")
     odd = lax.rem(place, 2)
     side = (lax.rem(place, 4) // 2 + odd + 1) % 2
+
     def pair(array):
         return lax.ppermute(array, "slab", [(s, s ^ 1) for s in range(slabs)])
 
@@ -485,7 +497,6 @@
     info = jnp.stack([jnp.asarray(v, jnp.int32) for v in (odd, side, point, *facing)])
     mine, yours = call(
         damping_body,
-        "damping",
         1,
         [(2, 2, N)] * 2,
         (
@@ -506,7 +517,6 @@
 
     xa, x, zn, own, other, near = call(
         first_body,
-        "first",
         30,
         [(2,) + MATRIX, MATRIX, MATRIX, ENDS, ENDS, PACKED],
         (info, onsite_block, hopping_block, mine, theirs),
@@ -515,7 +525,6 @@
     )
     ia, own_r, other_r = call(
         first_rhs_body,
-        "first_rhs",
         3,
         [(2,) + VECTOR, RHS, RHS],
         (info, xa, hopping_block, kept, given),
@@ -527,20 +536,19 @@
         facing_block = swapped(near, distance)
         w, zf, ends, sides = call(
             functools.partial(rest_body, level),
-            "rest",
             5,
             [VECTOR, MATRIX, ENDS, RHS],
             (info, x, zn, own, other, own_r, other_r),
             scalars=1,
         )
         held += [w, zn, zf]
-        own, other = ends, swapped(ends, distance)
-        own_r, other_r = sides, swapped(sides, distance)
-        (x,) = call(invert_body, "invert", 12, [MATRIX], (near, facing_block), work(1))
+        other = swapped(ends, distance)
+        other_r = swapped(sides, distance)
+        own, own_r = ends, sides
+        (x,) = call(invert_body, 12, [MATRIX], (near, facing_block), work(1))
         if level < count - 1:
             zn, near = call(
                 functools.partial(near_body, level + 1),
-                "near",
                 3,
                 [MATRIX, PACKED],
                 (info, x, own, other),
@@ -548,7 +556,6 @@
             )
     prev, mid, last, sent = call(
         functools.partial(back_body, count),
-        "back",
         22,
         [VECTOR, VECTOR, VECTOR, (2,) + VECTOR],
         (info, x, own, other, own_r, other_r, *held, xa, ia, hopping_block),
@@ -558,19 +565,13 @@
     back = pair(sent)
     (mine,) = call(
         own_body,
-        "own",
         2,
         [(2,) + VECTOR],
         (info, xa, ia, mid, hopping_block, prev, last),
         scalars=1,
     )
     return call(
-        finish_body,
-        "finish",
-        2,
-        [source.shape, occupation.shape],
-        (info, mine, back),
-        scalars=1,
+        finish_body, 2, [source.shape, occupation.shape], (info, mine, back), scalars=1
     )
 
 

time: 179 us -> 179 us (level)
  no operation moved by 1% of the time
where the time goes in v4:
time: 179 us; the launch traced here: 178 us
  Pallas kernels  109 us (61%)
  waiting for transfers between devices  37.7 us (21%)
  starting transfers between devices  20.1 us (11%)
  local copies, waits for them, and re-layouts  10.4 us (6%)
    pallas_call x14, Pallas kernels, call(): pl.pallas_call(body, out_shape=tuple((jax.ShapeDtypeStruct(s, jnp.float32...  109 us
    ppermute x9, waiting for transfers between devices, swapped(): return lax.ppermute(array, 'slab', pairs)  28 us
    ppermute x9, starting transfers between devices, swapped(): return lax.ppermute(array, 'slab', pairs)  15 us
    unnamed x30, local copies, waits for them, and re-layouts  8.93 us
    ppermute x3, waiting for transfers between devices, pair(): return lax.ppermute(array, 'slab', [(s, s ^ 1) for s in range(slabs)])  7.17 us
  transfers between devices with their start and end apart: 14, of which 7 were waited for; matrix products, arithmetic and copies ran while one was open for 1% of the time, Pallas kernels for 49%

profile of v4, /device:TPU:32, one launch (start us, length us, event | category | flops | bytes accessed | tf_op | source)
XLA Modules:
  0.0 178.3 jit_solution(15771521924685247165)
XLA Ops:
  0.6 1.7 collective-permute-start
  2.4 1.3 collective-permute-start.1
  4.4 2.5 %collective-permute-done.1.high = f32[2,2,192]{2,1,0:T(2,128)S(1)} collective-permute-done((f32[2,2,192]{2,1,0:T(2,128)}, f32[2,2,192]{2,1,0:T(2,128)S(1)}, u32[]{:S(2)}, u32[]{:S(2)}) %collective-permute-start.1) | collective-permute-done | bytes 3104 | tf_op jit(solution)/shard_map/ppermute | solution.py:481
  7.5 1.6 shard_map.95
  9.1 1.6 collective-permute-start.2
  11.9 1.0 collective-permute-done.2.theirs
  13.5 26.3 %shard_map.96 = (f32[2,2,192,192]{3,2,1,0:T(8,128)}, f32[2,192,192]{2,1,0:T(8,128)}, f32[2,192,192]{2,1,0:T(8,128)}, f32[6,192,128]{2,1,0:T(8,128)}, f32[6,192,128]{2,1,0:T(8,128)}, /*index=5*/f32[3,192,128]{2,1,0:T(8,128)}) custom-call(s32[7]{0:T(128)} %stack.47.info, f32[192,192]{1,0:T(8,128)} %onsite.1, f32[192,192]{1,0:T(8,128)} %hop.5, ...), custom_call_target="tpu_custom_call" | custom-call | flops 32999999488 | bytes 1048576 | tf_op jit(solution)/shard_map/pallas_call | solution.py:226
  39.8 3.0 %collective-permute-start.4 = (f32[3,192,128]{2,1,0:T(8,128)}, f32[3,192,128]{2,1,0:T(8,128)S(1)}, u32[]{:S(2)}, u32[]{:S(2)}) collective-permute-start(f32[3,192,128]{2,1,0:T(8,128)} %get-tuple-element.37.own), channel_id=1, source_target_pairs={{8,16},{0,24},{16,8},{24,0},{40,48},{32,56},{48,40},{56,32},{72,80... | collective-permute-start | bytes 884744 | tf_op jit(solution)/shard_map/ppermute | solution.py:490
  43.6 3.3 %shard_map.97 = (f32[2,2,192,128]{3,2,1,0:T(8,128)}, f32[4,192,128]{2,1,0:T(8,128)}, f32[4,192,128]{2,1,0:T(8,128)}) custom-call(s32[7]{0:T(128)} %stack.47.info, f32[2,2,192,192]{3,2,1,0:T(8,128)} %get-tuple-element.35.xa.refs_9_, f32[192,192]{1,0:T(8,128)} %hop.5, f32[2,2,192,128]{3,2,1,0:T(8,128)} %get-tuple-element.65.kept, f32[2,2,192,128]{3,2,1,0:T(8,128)} %copy-done.7), custom_call_target="tpu_custom_call" | custom-call | flops 3300000000 | bytes 1048576 | tf_op jit(solution)/shard_map/pallas_call | solution.py:226
  46.9 4.3 %shard_map.99 = (f32[2,192,128]{2,1,0:T(8,128)}, f32[2,192,192]{2,1,0:T(8,128)}, f32[6,192,128]{2,1,0:T(8,128)}, f32[4,192,128]{2,1,0:T(8,128)}) custom-call(s32[7]{0:T(128)} %stack.47.info, f32[2,192,192]{2,1,0:T(8,128)} %get-tuple-element.38.x, f32[2,192,192]{2,1,0:T(8,128)} %get-tuple-element.39.zn.refs_1_, f32[6,192,128]{2,1,0:T(8,128)} %get-tuple-element.40.own, ...), custom_call_target="tpu_custom_call" | custom-call | flops 5500000256 | bytes 1048576 | tf_op jit(solution)/shard_map/pallas_call | solution.py:226
  51.4 3.0 %collective-permute-start.5 = (f32[6,192,128]{2,1,0:T(8,128)}, f32[6,192,128]{2,1,0:T(8,128)S(1)}, u32[]{:S(2)}, u32[]{:S(2)}) collective-permute-start(f32[6,192,128]{2,1,0:T(8,128)} %get-tuple-element.44.own), channel_id=1, source_target_pairs={{8,16},{0,24},{16,8},{24,0},{40,48},{32,56},{48,40},{56,32},{72,80... | collective-permute-start | bytes 1769480 | tf_op jit(solution)/shard_map/ppermute | solution.py:490
  55.1 12.0 %shard_map.98.x = f32[2,192,192]{2,1,0:T(8,128)} custom-call(f32[3,192,128]{2,1,0:T(8,128)} %get-tuple-element.37.own, f32[3,192,128]{2,1,0:T(8,128)} %copy-done.9), custom_call_target="tpu_custom_call" | custom-call | flops 13200000000 | bytes 1048576 | tf_op jit(solution)/shard_map/pallas_call | solution.py:226
  67.2 9.7 %collective-permute-done.5.other = f32[6,192,128]{2,1,0:T(8,128)S(1)} collective-permute-done((f32[6,192,128]{2,1,0:T(8,128)}, f32[6,192,128]{2,1,0:T(8,128)S(1)}, u32[]{:S(2)}, u32[]{:S(2)}) %collective-permute-start.5) | collective-permute-done | bytes 589856 | tf_op jit(solution)/shard_map/ppermute | solution.py:490
  76.9 0.8 copy-done.2
  77.7 3.0 %shard_map.100 = (f32[2,192,192]{2,1,0:T(8,128)}, f32[3,192,128]{2,1,0:T(8,128)}) custom-call(s32[7]{0:T(128)} %stack.47.info, f32[2,192,192]{2,1,0:T(8,128)} %shard_map.98.x, f32[6,192,128]{2,1,0:T(8,128)} %get-tuple-element.44.own, f32[6,192,128]{2,1,0:T(8,128)} %copy-done.2), custom_call_target="tpu_custom_call" | custom-call | flops 3300000000 | bytes 1048576 | tf_op jit(solution)/shard_map/pallas_call | solution.py:226
  81.6 4.3 %shard_map.102 = (f32[2,192,128]{2,1,0:T(8,128)}, f32[2,192,192]{2,1,0:T(8,128)}, f32[6,192,128]{2,1,0:T(8,128)}, f32[4,192,128]{2,1,0:T(8,128)}) custom-call(s32[7]{0:T(128)} %stack.47.info, f32[2,192,192]{2,1,0:T(8,128)} %shard_map.98.x, f32[2,192,192]{2,1,0:T(8,128)} %get-tuple-element.46.zn.refs_4_, f32[6,192,128]{2,1,0:T(8,128)} %get-tuple-element.44.own, ...), custom_call_target="tpu_custom_call" | custom-call | flops 5500000256 | bytes 1048576 | tf_op jit(solution)/shard_map/pallas_call | solution.py:226
  85.9 1.9 %collective-permute-start.10 = (f32[4,192,128]{2,1,0:T(8,128)}, f32[4,192,128]{2,1,0:T(8,128)S(1)}, u32[]{:S(2)}, u32[]{:S(2)}) collective-permute-start(f32[4,192,128]{2,1,0:T(8,128)} %get-tuple-element.51.own_r), channel_id=1, source_target_pairs={{8,40},{0,32},{16,48},{24,56},{40,8},{32,0},{48,16},{56,24},{72,10... | collective-permute-start | bytes 1179656 | tf_op jit(solution)/shard_map/ppermute | solution.py:490
  88.1 2.8 %collective-permute-done.6.other = f32[3,192,128]{2,1,0:T(8,128)S(1)} collective-permute-done((f32[3,192,128]{2,1,0:T(8,128)}, f32[3,192,128]{2,1,0:T(8,128)S(1)}, u32[]{:S(2)}, u32[]{:S(2)}) %collective-permute-start.6) | collective-permute-done | bytes 294944 | tf_op jit(solution)/shard_map/ppermute | solution.py:490
  91.6 12.0 %shard_map.101.x = f32[2,192,192]{2,1,0:T(8,128)} custom-call(f32[3,192,128]{2,1,0:T(8,128)} %get-tuple-element.45.own, f32[3,192,128]{2,1,0:T(8,128)} %copy-done.10), custom_call_target="tpu_custom_call" | custom-call | flops 13200000000 | bytes 1048576 | tf_op jit(solution)/shard_map/pallas_call | solution.py:226
  103.6 7.5 %collective-permute-done.8.other = f32[6,192,128]{2,1,0:T(8,128)S(1)} collective-permute-done((f32[6,192,128]{2,1,0:T(8,128)}, f32[6,192,128]{2,1,0:T(8,128)S(1)}, u32[]{:S(2)}, u32[]{:S(2)}) %collective-permute-start.8) | collective-permute-done | bytes 589856 | tf_op jit(solution)/shard_map/ppermute | solution.py:490
  111.1 0.8 copy-done.3
  111.9 3.0 %shard_map.103 = (f32[2,192,192]{2,1,0:T(8,128)}, f32[3,192,128]{2,1,0:T(8,128)}) custom-call(s32[7]{0:T(128)} %stack.47.info, f32[2,192,192]{2,1,0:T(8,128)} %shard_map.101.x, f32[6,192,128]{2,1,0:T(8,128)} %get-tuple-element.48.own, f32[6,192,128]{2,1,0:T(8,128)} %copy-done.3), custom_call_target="tpu_custom_call" | custom-call | flops 3300000000 | bytes 1048576 | tf_op jit(solution)/shard_map/pallas_call | solution.py:226
  114.9 3.0 %collective-permute-start.9 = (f32[3,192,128]{2,1,0:T(8,128)}, f32[3,192,128]{2,1,0:T(8,128)S(1)}, u32[]{:S(2)}, u32[]{:S(2)}) collective-permute-start(f32[3,192,128]{2,1,0:T(8,128)} %get-tuple-element.49.own), channel_id=1, source_target_pairs={{8,72},{0,64},{16,80},{24,88},{40,104},{32,96},{48,112},{56,120},{... | collective-permute-start | bytes 884744 | tf_op jit(solution)/shard_map/ppermute | solution.py:490
  118.7 4.2 %shard_map.105 = (f32[2,192,128]{2,1,0:T(8,128)}, f32[2,192,192]{2,1,0:T(8,128)}, f32[6,192,128]{2,1,0:T(8,128)}, f32[4,192,128]{2,1,0:T(8,128)}) custom-call(s32[7]{0:T(128)} %stack.47.info, f32[2,192,192]{2,1,0:T(8,128)} %shard_map.101.x, f32[2,192,192]{2,1,0:T(8,128)} %get-tuple-element.50.zn.refs_7_, f32[6,192,128]{2,1,0:T(8,128)} %get-tuple-element.48.own, ...), custom_call_target="tpu_custom_call" | custom-call | flops 5500000256 | bytes 1048576 | tf_op jit(solution)/shard_map/pallas_call | solution.py:226
  123.4 3.0 %collective-permute-start.11 = (f32[6,192,128]{2,1,0:T(8,128)}, f32[6,192,128]{2,1,0:T(8,128)S(1)}, u32[]{:S(2)}, u32[]{:S(2)}) collective-permute-start(f32[6,192,128]{2,1,0:T(8,128)} %get-tuple-element.52.own), channel_id=1, source_target_pairs={{8,72},{0,64},{16,80},{24,88},{40,104},{32,96},{48,112},{56,120},{... | collective-permute-start | bytes 1769480 | tf_op jit(solution)/shard_map/ppermute | solution.py:490
  127.2 12.1 %shard_map.104.x = f32[2,192,192]{2,1,0:T(8,128)} custom-call(f32[3,192,128]{2,1,0:T(8,128)} %get-tuple-element.49.own, f32[3,192,128]{2,1,0:T(8,128)} %copy-done.11), custom_call_target="tpu_custom_call" | custom-call | flops 13200000000 | bytes 1048576 | tf_op jit(solution)/shard_map/pallas_call | solution.py:226
  139.2 8.0 %collective-permute-done.11.other = f32[6,192,128]{2,1,0:T(8,128)S(1)} collective-permute-done((f32[6,192,128]{2,1,0:T(8,128)}, f32[6,192,128]{2,1,0:T(8,128)S(1)}, u32[]{:S(2)}, u32[]{:S(2)}) %collective-permute-start.11) | collective-permute-done | bytes 589856 | tf_op jit(solution)/shard_map/ppermute | solution.py:490
  147.3 0.9 copy-done.1
  148.1 18.0 %shard_map.106 = (f32[2,192,128]{2,1,0:T(8,128)}, f32[2,192,128]{2,1,0:T(8,128)}, f32[2,192,128]{2,1,0:T(8,128)}, f32[2,2,192,128]{3,2,1,0:T(8,128)}) custom-call(s32[7]{0:T(128)} %stack.47.info, f32[2,192,192]{2,1,0:T(8,128)} %shard_map.104.x, f32[6,192,128]{2,1,0:T(8,128)} %get-tuple-element.52.own, f32[6,192,128]{2,1,0:T(8,128)} %copy-done.1, ...), custom_call_target="tpu_custom_call" | custom-call | flops 24199999488 | bytes 1048576 | tf_op jit(solution)/shard_map/pallas_call | solution.py:226
  166.1 3.2 %shard_map.107.mine = f32[2,2,192,128]{3,2,1,0:T(8,128)} custom-call(s32[7]{0:T(128)} %stack.47.info, f32[2,2,192,192]{3,2,1,0:T(8,128)} %get-tuple-element.35.xa.refs_9_, f32[2,2,192,128]{3,2,1,0:T(8,128)} %get-tuple-element.36.refs_10_.ia, f32[2,192,128]{2,1,0:T(8,128)} %get-tuple-element.60.mid, f32[192,192]{1,0:T(8,128)} %hop.5, ...), custom_call_target="tpu_custom_call" | custom-call | flops 2200000000 | bytes 1048576 | tf_op jit(solution)/shard_map/pallas_call | solution.py:226
  169.3 6.2 %collective-permute-done.13.other = f32[2,2,192,128]{3,2,1,0:T(8,128)S(1)} collective-permute-done((f32[2,2,192,128]{3,2,1,0:T(8,128)}, f32[2,2,192,128]{3,2,1,0:T(8,128)S(1)}, u32[]{:S(2)}, u32[]{:S(2)}) %collective-permute-start.13) | collective-permute-done | bytes 393248 | tf_op jit(solution)/shard_map/ppermute | solution.py:476
  176.2 2.1 %shard_map.108 = (f32[2,2,2,192,128]{4,3,2,1,0:T(8,128)}, f32[2,2,192]{2,1,0:T(2,128)}) custom-call(s32[7]{0:T(128)} %stack.47.info, f32[2,2,192,128]{3,2,1,0:T(8,128)} %shard_map.107.mine, f32[2,2,192,128]{3,2,1,0:T(8,128)} %copy-done.8), custom_call_target="tpu_custom_call" | custom-call | flops 2200000000 | bytes 1048576 | tf_op jit(solution)/shard_map/pallas_call | solution.py:226
  (42 shorter events, 9.5 us)
Async XLA Ops:
  0.6 3.8 %collective-permute-start = (f32[2,2,192]{2,1,0:T(2,128)}, f32[2,2,192]{2,1,0:T(2,128)S(1)}, u32[]{:S(2)}, u32[]{:S(2)}) collective-permute-start(f32[2,2,192]{2,1,0:T(2,128)} %occ.1), channel_id=1, source_target_pairs={{0,1},{1,2},{2,3},{3,4},{4,5},{5,6},{6,7},{8,9},{9,10},{10,11},{11... | collective-permute-start | bytes 9224 | tf_op jit(solution)/shard_map/ppermute | solution.py:481
  2.4 4.6 %collective-permute-start.1 = (f32[2,2,192]{2,1,0:T(2,128)}, f32[2,2,192]{2,1,0:T(2,128)S(1)}, u32[]{:S(2)}, u32[]{:S(2)}) collective-permute-start(f32[2,2,192]{2,1,0:T(2,128)} %occ.1), channel_id=1, source_target_pairs={{1,0},{2,1},{3,2},{4,3},{5,4},{6,5},{7,6},{9,8},{10,9},{11,10},{12... | collective-permute-start | bytes 9224 | tf_op jit(solution)/shard_map/ppermute | solution.py:481
  4.4 6.3 %copy-start = (f32[2,2,2,192,128]{4,3,2,1,0:T(8,128)S(1)}, f32[2,2,2,192,128]{4,3,2,1,0:T(8,128)}, u32[]{:S(2)}) copy-start(f32[2,2,2,192,128]{4,3,2,1,0:T(8,128)} %param.8) | copy-start | bytes 2359300
  4.4 2.5 %copy-start.12 = (f32[2,2,192]{2,1,0:T(2,128)}, f32[2,2,192]{2,1,0:T(2,128)S(1)}, u32[]{:S(2)}) copy-start(f32[2,2,192]{2,1,0:T(2,128)S(1)} %collective-permute-done.low) | copy-start | bytes 9220
  6.9 0.6 copy-start.13
  9.1 3.8 %collective-permute-start.2 = (f32[2,2,192]{2,1,0:T(2,128)}, f32[2,2,192]{2,1,0:T(2,128)S(1)}, u32[]{:S(2)}, u32[]{:S(2)}) collective-permute-start(f32[2,2,192]{2,1,0:T(2,128)} %get-tuple-element.34), channel_id=1, source_target_pairs={{0,8},{8,0},{16,24},{24,16},{32,40},{40,32},{48,56},{56,48},{64,72... | collective-permute-start | bytes 9224 | tf_op jit(solution)/shard_map/ppermute | solution.py:476
  11.5 31.3 %collective-permute-start.3 = (f32[2,2,192,128]{3,2,1,0:T(8,128)S(1)}, f32[2,2,192,128]{3,2,1,0:T(8,128)S(1)}, u32[]{:S(2)}, u32[]{:S(2)}) collective-permute-start(f32[2,2,192,128]{3,2,1,0:T(8,128)S(1)} %get-tuple-element.64), channel_id=1, source_target_pairs={{0,8},{8,0},{16,24},{24,16},{32,40},{40,32},{48,56},{56,48},{64,72... | collective-permute-start | bytes 1179656 | tf_op jit(solution)/shard_map/ppermute | solution.py:476
  12.9 0.6 copy-start.14
  39.8 14.6 %collective-permute-start.4 = (f32[3,192,128]{2,1,0:T(8,128)}, f32[3,192,128]{2,1,0:T(8,128)S(1)}, u32[]{:S(2)}, u32[]{:S(2)}) collective-permute-start(f32[3,192,128]{2,1,0:T(8,128)} %get-tuple-element.37.own), channel_id=1, source_target_pairs={{8,16},{0,24},{16,8},{24,0},{40,48},{32,56},{48,40},{56,32},{72,80... | collective-permute-start | bytes 884744 | tf_op jit(solution)/shard_map/ppermute | solution.py:490
  42.8 0.8 copy-start.7
  51.1 29.7 %collective-permute-start.7 = (f32[4,192,128]{2,1,0:T(8,128)}, f32[4,192,128]{2,1,0:T(8,128)S(1)}, u32[]{:S(2)}, u32[]{:S(2)}) collective-permute-start(f32[4,192,128]{2,1,0:T(8,128)} %get-tuple-element.47.own_r), channel_id=1, source_target_pairs={{8,16},{0,24},{16,8},{24,0},{40,48},{32,56},{48,40},{56,32},{72,80... | collective-permute-start | bytes 1179656 | tf_op jit(solution)/shard_map/ppermute | solution.py:490
  51.4 25.5 %collective-permute-start.5 = (f32[6,192,128]{2,1,0:T(8,128)}, f32[6,192,128]{2,1,0:T(8,128)S(1)}, u32[]{:S(2)}, u32[]{:S(2)}) collective-permute-start(f32[6,192,128]{2,1,0:T(8,128)} %get-tuple-element.44.own), channel_id=1, source_target_pairs={{8,16},{0,24},{16,8},{24,0},{40,48},{32,56},{48,40},{56,32},{72,80... | collective-permute-start | bytes 1769480 | tf_op jit(solution)/shard_map/ppermute | solution.py:490
  54.4 0.7 copy-start.9
  76.9 0.8 copy-start.2
  80.8 10.1 %collective-permute-start.6 = (f32[3,192,128]{2,1,0:T(8,128)}, f32[3,192,128]{2,1,0:T(8,128)S(1)}, u32[]{:S(2)}, u32[]{:S(2)}) collective-permute-start(f32[3,192,128]{2,1,0:T(8,128)} %get-tuple-element.45.own), channel_id=1, source_target_pairs={{8,40},{0,32},{16,48},{24,56},{40,8},{32,0},{48,16},{56,24},{72,10... | collective-permute-start | bytes 884744 | tf_op jit(solution)/shard_map/ppermute | solution.py:490
  80.9 0.8 copy-start.5
  85.9 32.0 %collective-permute-start.10 = (f32[4,192,128]{2,1,0:T(8,128)}, f32[4,192,128]{2,1,0:T(8,128)S(1)}, u32[]{:S(2)}, u32[]{:S(2)}) collective-permute-start(f32[4,192,128]{2,1,0:T(8,128)} %get-tuple-element.51.own_r), channel_id=1, source_target_pairs={{8,40},{0,32},{16,48},{24,56},{40,8},{32,0},{48,16},{56,24},{72,10... | collective-permute-start | bytes 1179656 | tf_op jit(solution)/shard_map/ppermute | solution.py:490
  87.8 23.2 %collective-permute-start.8 = (f32[6,192,128]{2,1,0:T(8,128)}, f32[6,192,128]{2,1,0:T(8,128)S(1)}, u32[]{:S(2)}, u32[]{:S(2)}) collective-permute-start(f32[6,192,128]{2,1,0:T(8,128)} %get-tuple-element.48.own), channel_id=1, source_target_pairs={{8,40},{0,32},{16,48},{24,56},{40,8},{32,0},{48,16},{56,24},{72,10... | collective-permute-start | bytes 1769480 | tf_op jit(solution)/shard_map/ppermute | solution.py:490
  90.9 0.7 copy-start.10
  111.1 0.8 copy-start.3
  114.9 11.5 %collective-permute-start.9 = (f32[3,192,128]{2,1,0:T(8,128)}, f32[3,192,128]{2,1,0:T(8,128)S(1)}, u32[]{:S(2)}, u32[]{:S(2)}) collective-permute-start(f32[3,192,128]{2,1,0:T(8,128)} %get-tuple-element.49.own), channel_id=1, source_target_pairs={{8,72},{0,64},{16,80},{24,88},{40,104},{32,96},{48,112},{56,120},{... | collective-permute-start | bytes 884744 | tf_op jit(solution)/shard_map/ppermute | solution.py:490
  117.9 0.7 copy-start.6
  122.9 16.3 %collective-permute-start.12 = (f32[4,192,128]{2,1,0:T(8,128)}, f32[4,192,128]{2,1,0:T(8,128)S(1)}, u32[]{:S(2)}, u32[]{:S(2)}) collective-permute-start(f32[4,192,128]{2,1,0:T(8,128)} %get-tuple-element.53.own_r), channel_id=1, source_target_pairs={{8,72},{0,64},{16,80},{24,88},{40,104},{32,96},{48,112},{56,120},{... | collective-permute-start | bytes 1179656 | tf_op jit(solution)/shard_map/ppermute | solution.py:490
  123.4 23.8 %collective-permute-start.11 = (f32[6,192,128]{2,1,0:T(8,128)}, f32[6,192,128]{2,1,0:T(8,128)S(1)}, u32[]{:S(2)}, u32[]{:S(2)}) collective-permute-start(f32[6,192,128]{2,1,0:T(8,128)} %get-tuple-element.52.own), channel_id=1, source_target_pairs={{8,72},{0,64},{16,80},{24,88},{40,104},{32,96},{48,112},{56,120},{... | collective-permute-start | bytes 1769480 | tf_op jit(solution)/shard_map/ppermute | solution.py:490
  126.4 0.7 copy-start.11
  139.2 8.0 %copy-start.4 = (f32[4,192,128]{2,1,0:T(8,128)}, f32[4,192,128]{2,1,0:T(8,128)S(1)}, u32[]{:S(2)}) copy-start(f32[4,192,128]{2,1,0:T(8,128)S(1)} %collective-permute-done.12.other_r) | copy-start | bytes 1179652
  147.3 0.9 copy-start.1
  166.1 9.4 %collective-permute-start.13 = (f32[2,2,192,128]{3,2,1,0:T(8,128)}, f32[2,2,192,128]{3,2,1,0:T(8,128)S(1)}, u32[]{:S(2)}, u32[]{:S(2)}) collective-permute-start(f32[2,2,192,128]{3,2,1,0:T(8,128)} %get-tuple-element.63), channel_id=1, source_target_pairs={{0,8},{8,0},{16,24},{24,16},{32,40},{40,32},{48,56},{56,48},{64,72... | collective-permute-start | bytes 1179656 | tf_op jit(solution)/shard_map/ppermute | solution.py:476
  175.5 0.8 copy-start.8

commit v5 on v4

--- a/solution.py
+++ b/solution.py
@@ -230,6 +230,7 @@
         + [pl.BlockSpec(memory_space=pltpu.VMEM)] * (len(args) - scalars),
         out_specs=tuple(pl.BlockSpec(memory_space=pltpu.VMEM) for _ in outs),
         scratch_shapes=list(scratch),
+        compiler_params=pltpu.CompilerParams(vmem_limit_bytes=24 * 1024 * 1024),
         cost_estimate=pl.CostEstimate(
             flops=int(cost * 1.1e9), bytes_accessed=1 << 20, transcendentals=0
         ),
@@ -405,25 +406,28 @@
     put(out.at[1], second)
 
 
-def back_body(count, info, x, own, other, own_r, other_r, *refs):
-    levels = [refs[3 * i : 3 * i + 3] for i in range(count)]
-    xa, ia, hop, prev_out, mid, last_out, out, zn, ar, ai, m = refs[3 * count :]
-    flag = info[3 + count]
-    xs = get(x)
-
+def last_body(level, info, x, own, other, zn, end, ar, ai, m):
     def store(v):
         ar[0, :, 0:N] = v[0]
         ai[0, :, 0:N] = v[1]
 
-    near_end(flag, xs, own, other, zn, store)
+    near_end(info[3 + level], get(x), own, other, zn, store)
+    sweep(1, ar, ai, m)
+    put(end, (-ar[0, :, 0:N], -ai[0, :, 0:N]))
+
+
+def back_body(count, info, x, zn, end, own_r, other_r, *refs):
+    levels = [refs[3 * i : 3 * i + 3] for i in range(count)]
+    xa, ia, hop, prev_out, mid, last_out, out = refs[3 * count :]
+    flag = info[3 + count]
     mine, mine_far = rhs_ends(own_r)
     theirs, theirs_far = rhs_ends(other_r)
     r = add(mine, theirs)
-    w = vdot(nn, csplit(xs), r)
-    rest = sub(choose(flag, theirs_far, mine_far), vdot(nn, csplit(get(zn)), r))
-    sweep(1, ar, ai, m)
-    end = vdot(nn, csplit((-ar[0, :, 0:N], -ai[0, :, 0:N])), rest)
-    one = sub(w, vdot(tn, csplit(get(zn)), end))
+    zns = csplit(get(zn))
+    w = vdot(nn, csplit(get(x)), r)
+    rest = sub(choose(flag, theirs_far, mine_far), vdot(nn, zns, r))
+    end = vdot(nn, csplit(get(end)), rest)
+    one = sub(w, vdot(tn, zns, end))
     near, far = one, choose(flag, (jnp.zeros((N, COLS), jnp.float32),) * 2, end)
     for i in range(count - 1, -1, -1):
         w, z_near, z_far = levels[i]
@@ -554,12 +558,19 @@
                 (info, x, own, other),
                 scalars=1,
             )
+    zn, end = call(
+        functools.partial(last_body, count),
+        15,
+        [MATRIX, MATRIX],
+        (info, x, own, other),
+        work(1),
+        scalars=1,
+    )
     prev, mid, last, sent = call(
         functools.partial(back_body, count),
-        22,
+        7,
         [VECTOR, VECTOR, VECTOR, (2,) + VECTOR],
-        (info, x, own, other, own_r, other_r, *held, xa, ia, hopping_block),
-        [pltpu.VMEM(MATRIX, jnp.float32)] + work(1),
+        (info, x, zn, end, own_r, other_r, *held, xa, ia, hopping_block),
         scalars=1,
     )
     back = pair(sent)

time: 179 us -> 161 us (0.90)
  Pallas kernels: 109 us -> 86.1 us
  waiting for transfers between devices: 37.7 us -> 51.7 us
  local copies, waits for them, and re-layouts: 10.4 us -> 0.17 us
    pallas_call x14 -> x15, Pallas kernels: 109 us -> 86.1 us  [call(): pl.pallas_call(body, out_shape=tuple((jax.ShapeDtypeStruct(s, jnp.float32...]
    ppermute x9, waiting for transfers between devices: 28 us -> 39.1 us  [swapped(): return lax.ppermute(array, 'slab', pairs)]
    unnamed x30 -> x16, local copies, waits for them, and re-layouts: 8.93 us -> 0.04 us
    ppermute x3, waiting for transfers between devices: 7.17 us -> 9.58 us  [pair(): return lax.ppermute(array, 'slab', [(s, s ^ 1) for s in range(slabs)])]
  transfers between devices with their start and end apart: 14 -> 14, of which waited for: 7 -> 9; matrix products, arithmetic and copies ran while one was open for 1% -> 0% of each run, Pallas kernels for 49% -> 50%
where the time goes in v5:
time: 161 us; the launch traced here: 160 us
  Pallas kernels  86.1 us (53%)
  waiting for transfers between devices  51.7 us (32%)
  starting transfers between devices  21 us (13%)
    pallas_call x15, Pallas kernels, call(): pl.pallas_call(body, out_shape=tuple((jax.ShapeDtypeStruct(s, jnp.float32...  86.1 us
    ppermute x9, waiting for transfers between devices, swapped(): return lax.ppermute(array, 'slab', pairs)  39.1 us
    ppermute x9, starting transfers between devices, swapped(): return lax.ppermute(array, 'slab', pairs)  15.5 us
    ppermute x3, waiting for transfers between devices, pair(): return lax.ppermute(array, 'slab', [(s, s ^ 1) for s in range(slabs)])  9.58 us
  transfers between devices with their start and end apart: 14, of which 9 were waited for; matrix products, arithmetic and copies ran while one was open for 0% of the time, Pallas kernels for 50%

profile of v5, /device:TPU:32, one launch (start us, length us, event | category | flops | bytes accessed | tf_op | source)
XLA Modules:
  0.0 159.9 jit_solution(11329105066121221262)
XLA Ops:
  0.6 1.7 %collective-permute-start = (f32[2,2,192]{2,1,0:T(2,128)}, f32[2,2,192]{2,1,0:T(2,128)S(1)}, u32[]{:S(2)}, u32[]{:S(2)}) collective-permute-start(f32[2,2,192]{2,1,0:T(2,128)} %occ.1), channel_id=1, source_target_pairs={{0,1},{1,2},{2,3},{3,4},{4,5},{5,6},{6,7},{8,9},{9,10},{10,11},{11... | collective-permute-start | bytes 9224 | tf_op jit(solution)/shard_map/ppermute | solution.py:485
  2.4 1.3 collective-permute-start.1
  3.9 3.0 %collective-permute-done.1.high = f32[2,2,192]{2,1,0:T(2,128)S(1)} collective-permute-done((f32[2,2,192]{2,1,0:T(2,128)}, f32[2,2,192]{2,1,0:T(2,128)S(1)}, u32[]{:S(2)}, u32[]{:S(2)}) %collective-permute-start.1) | collective-permute-done | bytes 3104 | tf_op jit(solution)/shard_map/ppermute | solution.py:485
  7.0 0.7 shard_map.95
  7.7 1.7 %collective-permute-start.2 = (f32[2,2,192]{2,1,0:T(2,128)S(1)}, f32[2,2,192]{2,1,0:T(2,128)S(1)}, u32[]{:S(2)}, u32[]{:S(2)}) collective-permute-start(f32[2,2,192]{2,1,0:T(2,128)S(1)} %get-tuple-element.36), channel_id=1, source_target_pairs={{0,8},{8,0},{16,24},{24,16},{32,40},{40,32},{48,56},{56,48},{64,72... | collective-permute-start | bytes 9224 | tf_op jit(solution)/shard_map/ppermute | solution.py:480
  10.0 1.4 collective-permute-done.2.theirs
  11.4 25.1 %shard_map.96 = (f32[2,2,192,192]{3,2,1,0:T(8,128)S(1)}, f32[2,192,192]{2,1,0:T(8,128)S(1)}, f32[2,192,192]{2,1,0:T(8,128)S(1)}, f32[6,192,128]{2,1,0:T(8,128)S(...) custom-call(s32[7]{0:T(128)S(1)} %stack.47.info, f32[192,192]{1,0:T(8,128)S(1)} %copy-done, ...), custom_call_target="tpu_custom_call" | custom-call | flops 32999999488 | bytes 1048576 | tf_op jit(solution)/shard_map/pallas_call | solution.py:226
  36.5 3.1 %collective-permute-start.4 = (f32[3,192,128]{2,1,0:T(8,128)S(1)}, f32[3,192,128]{2,1,0:T(8,128)S(1)}, u32[]{:S(2)}, u32[]{:S(2)}) collective-permute-start(f32[3,192,128]{2,1,0:T(8,128)S(1)} %get-tuple-element.39.own), channel_id=1, source_target_pairs={{8,16},{0,24},{16,8},{24,0},{40,48},{32,56},{48,40},{56,32},{72,80... | collective-permute-start | bytes 884744 | tf_op jit(solution)/shard_map/ppermute | solution.py:494
  39.6 1.5 shard_map.97
  41.1 2.2 %shard_map.99 = (f32[2,192,128]{2,1,0:T(8,128)S(1)}, f32[2,192,192]{2,1,0:T(8,128)S(1)}, f32[6,192,128]{2,1,0:T(8,128)S(1)}, f32[4,192,128]{2,1,0:T(8,128)S(1)}) custom-call(s32[7]{0:T(128)S(1)} %stack.47.info, f32[2,192,192]{2,1,0:T(8,128)S(1)} %get-tuple-element.40.x, f32[2,192,192]{2,1,0:T(8,128)S(1)} %get-tuple-element.41.zn.refs_1_, ...), custom_call_target="tpu_custom_call" | custom-call | flops 5500000256 | bytes 1048576 | tf_op jit(solution)/shard_map/pallas_call | solution.py:226
  43.6 3.0 %collective-permute-start.5 = (f32[6,192,128]{2,1,0:T(8,128)S(1)}, f32[6,192,128]{2,1,0:T(8,128)S(1)}, u32[]{:S(2)}, u32[]{:S(2)}) collective-permute-start(f32[6,192,128]{2,1,0:T(8,128)S(1)} %get-tuple-element.46.own), channel_id=1, source_target_pairs={{8,16},{0,24},{16,8},{24,0},{40,48},{32,56},{48,40},{56,32},{72,80... | collective-permute-start | bytes 1769480 | tf_op jit(solution)/shard_map/ppermute | solution.py:494
  47.0 10.2 %shard_map.98.x = f32[2,192,192]{2,1,0:T(8,128)S(1)} custom-call(f32[3,192,128]{2,1,0:T(8,128)S(1)} %get-tuple-element.39.own, f32[3,192,128]{2,1,0:T(8,128)S(1)} %collective-permute-done.4.other), custom_call_target="tpu_custom_call" | custom-call | flops 13200000000 | bytes 1048576 | tf_op jit(solution)/shard_map/pallas_call | solution.py:226
  57.3 11.6 %collective-permute-done.5.other = f32[6,192,128]{2,1,0:T(8,128)S(1)} collective-permute-done((f32[6,192,128]{2,1,0:T(8,128)S(1)}, f32[6,192,128]{2,1,0:T(8,128)S(1)}, u32[]{:S(2)}, u32[]{:S(2)}) %collective-permute-start.5) | collective-permute-done | bytes 589856 | tf_op jit(solution)/shard_map/ppermute | solution.py:494
  68.9 1.5 shard_map.100
  70.6 2.2 %shard_map.102 = (f32[2,192,128]{2,1,0:T(8,128)S(1)}, f32[2,192,192]{2,1,0:T(8,128)S(1)}, f32[6,192,128]{2,1,0:T(8,128)S(1)}, f32[4,192,128]{2,1,0:T(8,128)S(1)}) custom-call(s32[7]{0:T(128)S(1)} %stack.47.info, f32[2,192,192]{2,1,0:T(8,128)S(1)} %shard_map.98.x, f32[2,192,192]{2,1,0:T(8,128)S(1)} %get-tuple-element.48.zn.refs_4_, ...), custom_call_target="tpu_custom_call" | custom-call | flops 5500000256 | bytes 1048576 | tf_op jit(solution)/shard_map/pallas_call | solution.py:226
  72.8 2.0 %collective-permute-start.10 = (f32[4,192,128]{2,1,0:T(8,128)S(1)}, f32[4,192,128]{2,1,0:T(8,128)S(1)}, u32[]{:S(2)}, u32[]{:S(2)}) collective-permute-start(f32[4,192,128]{2,1,0:T(8,128)S(1)} %get-tuple-element.53.own_r), channel_id=1, source_target_pairs={{8,40},{0,32},{16,48},{24,56},{40,8},{32,0},{48,16},{56,24},{72,10... | collective-permute-start | bytes 1179656 | tf_op jit(solution)/shard_map/ppermute | solution.py:494
  75.1 5.3 %collective-permute-done.6.other = f32[3,192,128]{2,1,0:T(8,128)S(1)} collective-permute-done((f32[3,192,128]{2,1,0:T(8,128)S(1)}, f32[3,192,128]{2,1,0:T(8,128)S(1)}, u32[]{:S(2)}, u32[]{:S(2)}) %collective-permute-start.6) | collective-permute-done | bytes 294944 | tf_op jit(solution)/shard_map/ppermute | solution.py:494
  80.4 10.3 %shard_map.101.x = f32[2,192,192]{2,1,0:T(8,128)S(1)} custom-call(f32[3,192,128]{2,1,0:T(8,128)S(1)} %get-tuple-element.47.own, f32[3,192,128]{2,1,0:T(8,128)S(1)} %collective-permute-done.6.other), custom_call_target="tpu_custom_call" | custom-call | flops 13200000000 | bytes 1048576 | tf_op jit(solution)/shard_map/pallas_call | solution.py:226
  90.6 10.0 %collective-permute-done.8.other = f32[6,192,128]{2,1,0:T(8,128)S(1)} collective-permute-done((f32[6,192,128]{2,1,0:T(8,128)S(1)}, f32[6,192,128]{2,1,0:T(8,128)S(1)}, u32[]{:S(2)}, u32[]{:S(2)}) %collective-permute-start.8) | collective-permute-done | bytes 589856 | tf_op jit(solution)/shard_map/ppermute | solution.py:494
  100.6 1.5 shard_map.103
  102.1 3.1 %collective-permute-start.9 = (f32[3,192,128]{2,1,0:T(8,128)S(1)}, f32[3,192,128]{2,1,0:T(8,128)S(1)}, u32[]{:S(2)}, u32[]{:S(2)}) collective-permute-start(f32[3,192,128]{2,1,0:T(8,128)S(1)} %get-tuple-element.51.own), channel_id=1, source_target_pairs={{8,72},{0,64},{16,80},{24,88},{40,104},{32,96},{48,112},{56,120},{... | collective-permute-start | bytes 884744 | tf_op jit(solution)/shard_map/ppermute | solution.py:494
  105.2 2.2 %shard_map.105 = (f32[2,192,128]{2,1,0:T(8,128)S(1)}, f32[2,192,192]{2,1,0:T(8,128)S(1)}, f32[6,192,128]{2,1,0:T(8,128)S(1)}, f32[4,192,128]{2,1,0:T(8,128)S(1)}) custom-call(s32[7]{0:T(128)S(1)} %stack.47.info, f32[2,192,192]{2,1,0:T(8,128)S(1)} %shard_map.101.x, f32[2,192,192]{2,1,0:T(8,128)S(1)} %get-tuple-element.52.zn.refs_7_, ...), custom_call_target="tpu_custom_call" | custom-call | flops 5500000256 | bytes 1048576 | tf_op jit(solution)/shard_map/pallas_call | solution.py:226
  107.3 0.6 collective-permute-start.12
  108.0 3.0 %collective-permute-start.11 = (f32[6,192,128]{2,1,0:T(8,128)S(1)}, f32[6,192,128]{2,1,0:T(8,128)S(1)}, u32[]{:S(2)}, u32[]{:S(2)}) collective-permute-start(f32[6,192,128]{2,1,0:T(8,128)S(1)} %get-tuple-element.54.own), channel_id=1, source_target_pairs={{8,72},{0,64},{16,80},{24,88},{40,104},{32,96},{48,112},{56,120},{... | collective-permute-start | bytes 1769480 | tf_op jit(solution)/shard_map/ppermute | solution.py:494
  110.9 2.3 %collective-permute-done.9.other = f32[3,192,128]{2,1,0:T(8,128)S(1)} collective-permute-done((f32[3,192,128]{2,1,0:T(8,128)S(1)}, f32[3,192,128]{2,1,0:T(8,128)S(1)}, u32[]{:S(2)}, u32[]{:S(2)}) %collective-permute-start.9) | collective-permute-done | bytes 294944 | tf_op jit(solution)/shard_map/ppermute | solution.py:494
  113.2 10.3 %shard_map.104.x = f32[2,192,192]{2,1,0:T(8,128)S(1)} custom-call(f32[3,192,128]{2,1,0:T(8,128)S(1)} %get-tuple-element.51.own, f32[3,192,128]{2,1,0:T(8,128)S(1)} %collective-permute-done.9.other), custom_call_target="tpu_custom_call" | custom-call | flops 13200000000 | bytes 1048576 | tf_op jit(solution)/shard_map/pallas_call | solution.py:226
  123.5 9.4 %collective-permute-done.11.other = f32[6,192,128]{2,1,0:T(8,128)S(1)} collective-permute-done((f32[6,192,128]{2,1,0:T(8,128)S(1)}, f32[6,192,128]{2,1,0:T(8,128)S(1)}, u32[]{:S(2)}, u32[]{:S(2)}) %collective-permute-start.11) | collective-permute-done | bytes 589856 | tf_op jit(solution)/shard_map/ppermute | solution.py:494
  132.9 11.5 %shard_map.106 = (f32[2,192,192]{2,1,0:T(8,128)S(1)}, f32[2,192,192]{2,1,0:T(8,128)S(1)}) custom-call(s32[7]{0:T(128)S(1)} %stack.47.info, f32[2,192,192]{2,1,0:T(8,128)S(1)} %shard_map.104.x, f32[6,192,128]{2,1,0:T(8,128)S(1)} %get-tuple-element.54.own, f32[6,192,128]{2,1,0:T(8,128)S(1)} %collective-permute-done.11.other), custom_call_target="tpu_custom_call" | custom-call | flops 16499999744 | bytes 1048576 | tf_op jit(solution)/shard_map/pallas_call | solution.py:226
  144.5 4.1 %shard_map.107 = (f32[2,192,128]{2,1,0:T(8,128)S(1)}, f32[2,192,128]{2,1,0:T(8,128)S(1)}, f32[2,192,128]{2,1,0:T(8,128)S(1)}, f32[2,2,192,128]{3,2,1,0:T(8,128)S(1)}) custom-call(s32[7]{0:T(128)S(1)} %stack.47.info, f32[2,192,192]{2,1,0:T(8,128)S(1)} %shard_map.104.x, f32[2,192,192]{2,1,0:T(8,128)S(1)} %get-tuple-element.55.zn, ...), custom_call_target="tpu_custom_call" | custom-call | flops 7699999744 | bytes 1048576 | tf_op jit(solution)/shard_map/pallas_call | solution.py:226
  148.8 1.5 shard_map.108.mine
  150.3 8.1 %collective-permute-done.13.other = f32[2,2,192,128]{3,2,1,0:T(8,128)S(1)} collective-permute-done((f32[2,2,192,128]{3,2,1,0:T(8,128)S(1)}, f32[2,2,192,128]{3,2,1,0:T(8,128)S(1)}, u32[]{:S(2)}, u32[]{:S(2)}) %collective-permute-start.13) | collective-permute-done | bytes 393248 | tf_op jit(solution)/shard_map/ppermute | solution.py:480
  158.4 1.5 shard_map.109
  (29 shorter events, 2.1 us)
Async XLA Ops:
  0.6 3.3 %collective-permute-start = (f32[2,2,192]{2,1,0:T(2,128)}, f32[2,2,192]{2,1,0:T(2,128)S(1)}, u32[]{:S(2)}, u32[]{:S(2)}) collective-permute-start(f32[2,2,192]{2,1,0:T(2,128)} %occ.1), channel_id=1, source_target_pairs={{0,1},{1,2},{2,3},{3,4},{4,5},{5,6},{6,7},{8,9},{9,10},{10,11},{11... | collective-permute-start | bytes 9224 | tf_op jit(solution)/shard_map/ppermute | solution.py:485
  2.4 4.5 %collective-permute-start.1 = (f32[2,2,192]{2,1,0:T(2,128)}, f32[2,2,192]{2,1,0:T(2,128)S(1)}, u32[]{:S(2)}, u32[]{:S(2)}) collective-permute-start(f32[2,2,192]{2,1,0:T(2,128)} %occ.1), channel_id=1, source_target_pairs={{1,0},{2,1},{3,2},{4,3},{5,4},{6,5},{7,6},{9,8},{10,9},{11,10},{12... | collective-permute-start | bytes 9224 | tf_op jit(solution)/shard_map/ppermute | solution.py:485
  3.7 3.2 %copy-start.2 = (f32[16,192]{1,0:T(8,128)S(1)}, f32[16,192]{1,0:T(8,128)}, u32[]{:S(2)}) copy-start(f32[16,192]{1,0:T(8,128)} %table.1) | copy-start | bytes 36868
  3.8 3.2 %copy-start.3 = (f32[2,2,192]{2,1,0:T(2,128)S(1)}, f32[2,2,192]{2,1,0:T(2,128)}, u32[]{:S(2)}) copy-start(f32[2,2,192]{2,1,0:T(2,128)} %occ.1) | copy-start | bytes 9220
  3.8 3.2 %copy-start.4 = (s32[4]{0:T(128)S(1)}, s32[4]{0:T(128)}, u32[]{:S(2)}) copy-start(s32[4]{0:T(128)} %shift.1) | copy-start | bytes 52
  3.8 3.2 %copy-start.5 = (s32[2]{0:T(128)S(1)}, s32[2]{0:T(128)}, u32[]{:S(2)}) copy-start(s32[2]{0:T(128)} %profile.1) | copy-start | bytes 28
  3.8 3.2 %copy-start.6 = (f32[4]{0:T(128)S(1)}, f32[4]{0:T(128)}, u32[]{:S(2)}) copy-start(f32[4]{0:T(128)} %coupling.1) | copy-start | bytes 52
  3.9 5.5 %copy-start.7 = (f32[2,2,2,192,128]{4,3,2,1,0:T(8,128)S(1)}, f32[2,2,2,192,128]{4,3,2,1,0:T(8,128)}, u32[]{:S(2)}) copy-start(f32[2,2,2,192,128]{4,3,2,1,0:T(8,128)} %param.8) | copy-start | bytes 2359300
  7.7 3.7 %copy-start = (f32[192,192]{1,0:T(8,128)S(1)}, f32[192,192]{1,0:T(8,128)}, u32[]{:S(2)}) copy-start(f32[192,192]{1,0:T(8,128)} %onsite.1) | copy-start | bytes 442372
  7.7 3.7 %copy-start.1 = (f32[192,192]{1,0:T(8,128)S(1)}, f32[192,192]{1,0:T(8,128)}, u32[]{:S(2)}) copy-start(f32[192,192]{1,0:T(8,128)} %hop.5) | copy-start | bytes 442372
  7.7 3.7 %collective-permute-start.2 = (f32[2,2,192]{2,1,0:T(2,128)S(1)}, f32[2,2,192]{2,1,0:T(2,128)S(1)}, u32[]{:S(2)}, u32[]{:S(2)}) collective-permute-start(f32[2,2,192]{2,1,0:T(2,128)S(1)} %get-tuple-element.36), channel_id=1, source_target_pairs={{0,8},{8,0},{16,24},{24,16},{32,40},{40,32},{48,56},{56,48},{64,72... | collective-permute-start | bytes 9224 | tf_op jit(solution)/shard_map/ppermute | solution.py:480
  9.4 30.2 %collective-permute-start.3 = (f32[2,2,192,128]{3,2,1,0:T(8,128)S(1)}, f32[2,2,192,128]{3,2,1,0:T(8,128)S(1)}, u32[]{:S(2)}, u32[]{:S(2)}) collective-permute-start(f32[2,2,192,128]{3,2,1,0:T(8,128)S(1)} %get-tuple-element.68), channel_id=1, source_target_pairs={{0,8},{8,0},{16,24},{24,16},{32,40},{40,32},{48,56},{56,48},{64,72... | collective-permute-start | bytes 1179656 | tf_op jit(solution)/shard_map/ppermute | solution.py:480
  36.5 10.5 %collective-permute-start.4 = (f32[3,192,128]{2,1,0:T(8,128)S(1)}, f32[3,192,128]{2,1,0:T(8,128)S(1)}, u32[]{:S(2)}, u32[]{:S(2)}) collective-permute-start(f32[3,192,128]{2,1,0:T(8,128)S(1)} %get-tuple-element.39.own), channel_id=1, source_target_pairs={{8,16},{0,24},{16,8},{24,0},{40,48},{32,56},{48,40},{56,32},{72,80... | collective-permute-start | bytes 884744 | tf_op jit(solution)/shard_map/ppermute | solution.py:494
  43.3 27.3 %collective-permute-start.7 = (f32[4,192,128]{2,1,0:T(8,128)S(1)}, f32[4,192,128]{2,1,0:T(8,128)S(1)}, u32[]{:S(2)}, u32[]{:S(2)}) collective-permute-start(f32[4,192,128]{2,1,0:T(8,128)S(1)} %get-tuple-element.49.own_r), channel_id=1, source_target_pairs={{8,16},{0,24},{16,8},{24,0},{40,48},{32,56},{48,40},{56,32},{72,80... | collective-permute-start | bytes 1179656 | tf_op jit(solution)/shard_map/ppermute | solution.py:494
  43.6 25.3 %collective-permute-start.5 = (f32[6,192,128]{2,1,0:T(8,128)S(1)}, f32[6,192,128]{2,1,0:T(8,128)S(1)}, u32[]{:S(2)}, u32[]{:S(2)}) collective-permute-start(f32[6,192,128]{2,1,0:T(8,128)S(1)} %get-tuple-element.46.own), channel_id=1, source_target_pairs={{8,16},{0,24},{16,8},{24,0},{40,48},{32,56},{48,40},{56,32},{72,80... | collective-permute-start | bytes 1769480 | tf_op jit(solution)/shard_map/ppermute | solution.py:494
  70.4 10.0 %collective-permute-start.6 = (f32[3,192,128]{2,1,0:T(8,128)S(1)}, f32[3,192,128]{2,1,0:T(8,128)S(1)}, u32[]{:S(2)}, u32[]{:S(2)}) collective-permute-start(f32[3,192,128]{2,1,0:T(8,128)S(1)} %get-tuple-element.47.own), channel_id=1, source_target_pairs={{8,40},{0,32},{16,48},{24,56},{40,8},{32,0},{48,16},{56,24},{72,10... | collective-permute-start | bytes 884744 | tf_op jit(solution)/shard_map/ppermute | solution.py:494
  72.8 32.4 %collective-permute-start.10 = (f32[4,192,128]{2,1,0:T(8,128)S(1)}, f32[4,192,128]{2,1,0:T(8,128)S(1)}, u32[]{:S(2)}, u32[]{:S(2)}) collective-permute-start(f32[4,192,128]{2,1,0:T(8,128)S(1)} %get-tuple-element.53.own_r), channel_id=1, source_target_pairs={{8,40},{0,32},{16,48},{24,56},{40,8},{32,0},{48,16},{56,24},{72,10... | collective-permute-start | bytes 1179656 | tf_op jit(solution)/shard_map/ppermute | solution.py:494
  74.8 25.8 %collective-permute-start.8 = (f32[6,192,128]{2,1,0:T(8,128)S(1)}, f32[6,192,128]{2,1,0:T(8,128)S(1)}, u32[]{:S(2)}, u32[]{:S(2)}) collective-permute-start(f32[6,192,128]{2,1,0:T(8,128)S(1)} %get-tuple-element.50.own), channel_id=1, source_target_pairs={{8,40},{0,32},{16,48},{24,56},{40,8},{32,0},{48,16},{56,24},{72,10... | collective-permute-start | bytes 1769480 | tf_op jit(solution)/shard_map/ppermute | solution.py:494
  102.1 11.1 %collective-permute-start.9 = (f32[3,192,128]{2,1,0:T(8,128)S(1)}, f32[3,192,128]{2,1,0:T(8,128)S(1)}, u32[]{:S(2)}, u32[]{:S(2)}) collective-permute-start(f32[3,192,128]{2,1,0:T(8,128)S(1)} %get-tuple-element.51.own), channel_id=1, source_target_pairs={{8,72},{0,64},{16,80},{24,88},{40,104},{32,96},{48,112},{56,120},{... | collective-permute-start | bytes 884744 | tf_op jit(solution)/shard_map/ppermute | solution.py:494
  107.3 37.1 %collective-permute-start.12 = (f32[4,192,128]{2,1,0:T(8,128)S(1)}, f32[4,192,128]{2,1,0:T(8,128)S(1)}, u32[]{:S(2)}, u32[]{:S(2)}) collective-permute-start(f32[4,192,128]{2,1,0:T(8,128)S(1)} %get-tuple-element.57.own_r), channel_id=1, source_target_pairs={{8,72},{0,64},{16,80},{24,88},{40,104},{32,96},{48,112},{56,120},{... | collective-permute-start | bytes 1179656 | tf_op jit(solution)/shard_map/ppermute | solution.py:494
  108.0 25.0 %collective-permute-start.11 = (f32[6,192,128]{2,1,0:T(8,128)S(1)}, f32[6,192,128]{2,1,0:T(8,128)S(1)}, u32[]{:S(2)}, u32[]{:S(2)}) collective-permute-start(f32[6,192,128]{2,1,0:T(8,128)S(1)} %get-tuple-element.54.own), channel_id=1, source_target_pairs={{8,72},{0,64},{16,80},{24,88},{40,104},{32,96},{48,112},{56,120},{... | collective-permute-start | bytes 1769480 | tf_op jit(solution)/shard_map/ppermute | solution.py:494
  148.6 9.8 %collective-permute-start.13 = (f32[2,2,192,128]{3,2,1,0:T(8,128)S(1)}, f32[2,2,192,128]{3,2,1,0:T(8,128)S(1)}, u32[]{:S(2)}, u32[]{:S(2)}) collective-permute-start(f32[2,2,192,128]{3,2,1,0:T(8,128)S(1)} %get-tuple-element.67), channel_id=1, source_target_pairs={{0,8},{8,0},{16,24},{24,16},{32,40},{40,32},{48,56},{56,48},{64,72... | collective-permute-start | bytes 1179656 | tf_op jit(solution)/shard_map/ppermute | solution.py:480

commit v6 on v5

--- a/solution.py
+++ b/solution.py
@@ -74,9 +74,9 @@
         return jnp.where(real, -pltpu.roll(x, 96, 1), pltpu.roll(x, 32, 1))
 
     def group(g, _):
-        o = pl.multiple_of(8 * g, 8)
-        own = m[pl.ds(o, 8), :]
-        parts = [m[8 * h : 8 * h + 8, :] for h in range(4)]
+        o = 8 * g
+        own = m[0:8, :]
+        parts = [m[8 * h : 8 * h + 8, :] for h in range(1, 4)]
         at = [start + (o + j) for j in range(8)]
         far = [a + 32 for a in at]
         cr = [take(own, a) for a in at]
@@ -87,14 +87,14 @@
         eye = jnp.where(real & (off - o == row), 1.0, 0.0)
         now = jnp.where(inside, eye, own)
         out, turn = solve_eight(cr, ci, now, turned(now))
-        for h in range(4):
+        for h in range(3):
             x = jnp.where(inside, 0.0, parts[h])
             for j in range(8):
                 x = x - (
                     wide_r[h][j] * spread(out[j : j + 1]) + wide_i[h][j] * spread(turn[j : j + 1])
                 )
             m[8 * h : 8 * h + 8, :] = x
-        m[pl.ds(o, 8), :] = out
+        m[24:32, :] = out
         return 0
 
     lax.fori_loop(0, 4, group, 0)
@@ -484,12 +484,13 @@
         pairs = [(e, e + by) for e in range(width) if 0 <= e + by < width]
         return lax.ppermute(array, "energy", pairs)
 
-    def swapped(array, distance):
+    def swapped(array, distance, one_way=False):
         spot = lambda g, chain: 2 * g + ((1 - chain) if g % 2 == 0 else chain)
         pairs = [
             (spot(g, chain), spot(g ^ distance, chain))
             for g in range(slabs // 2)
             for chain in range(2)
+            if g & distance or not one_way
         ]
         return lax.ppermute(array, "slab", pairs)
 
@@ -546,7 +547,7 @@
             scalars=1,
         )
         held += [w, zn, zf]
-        other = swapped(ends, distance)
+        other = swapped(ends, distance, one_way=level == count - 1)
         other_r = swapped(sides, distance)
         own, own_r = ends, sides
         (x,) = call(invert_body, 12, [MATRIX], (near, facing_block), work(1))

time: 161 us -> 158 us (0.981)
  Pallas kernels: 86.1 us -> 79.6 us
  waiting for transfers between devices: 51.7 us -> 56.8 us
    pallas_call x15, Pallas kernels: 86.1 us -> 79.6 us  [call(): pl.pallas_call(body, out_shape=tuple((jax.ShapeDtypeStruct(s, jnp.float32...]
    ppermute x9, waiting for transfers between devices: 39.1 us -> 44.2 us  [swapped(): return lax.ppermute(array, 'slab', pairs)]
    ppermute x9, starting transfers between devices: 15.5 us -> 13.9 us  [swapped(): return lax.ppermute(array, 'slab', pairs)]
  transfers between devices with their start and end apart: 14 -> 14, of which waited for: 9 -> 9; matrix products, arithmetic and copies ran while one was open for 0% -> 0% of each run, Pallas kernels for 50% -> 47%
where the time goes in v6:
time: 158 us; the launch traced here: 157 us
  Pallas kernels  79.6 us (50%)
  waiting for transfers between devices  56.8 us (36%)
  starting transfers between devices  19.4 us (12%)
    pallas_call x15, Pallas kernels, call(): pl.pallas_call(body, out_shape=tuple((jax.ShapeDtypeStruct(s, jnp.float32...  79.6 us
    ppermute x9, waiting for transfers between devices, swapped(): return lax.ppermute(array, 'slab', pairs)  44.2 us
    ppermute x9, starting transfers between devices, swapped(): return lax.ppermute(array, 'slab', pairs)  13.9 us
    ppermute x3, waiting for transfers between devices, pair(): return lax.ppermute(array, 'slab', [(s, s ^ 1) for s in range(slabs)])  9.58 us
  transfers between devices with their start and end apart: 14, of which 9 were waited for; matrix products, arithmetic and copies ran while one was open for 0% of the time, Pallas kernels for 47%

profile of v6, /device:TPU:32, one launch (start us, length us, event | category | flops | bytes accessed | tf_op | source)
XLA Modules:
  0.0 156.8 jit_solution(9331391011470290090)
XLA Ops:
  0.6 1.7 %collective-permute-start = (f32[2,2,192]{2,1,0:T(2,128)}, f32[2,2,192]{2,1,0:T(2,128)S(1)}, u32[]{:S(2)}, u32[]{:S(2)}) collective-permute-start(f32[2,2,192]{2,1,0:T(2,128)} %occ.1), channel_id=1, source_target_pairs={{0,1},{1,2},{2,3},{3,4},{4,5},{5,6},{6,7},{8,9},{9,10},{10,11},{11... | collective-permute-start | bytes 9224 | tf_op jit(solution)/shard_map/ppermute | solution.py:485
  2.4 1.3 collective-permute-start.1
  3.9 3.0 %collective-permute-done.1.high = f32[2,2,192]{2,1,0:T(2,128)S(1)} collective-permute-done((f32[2,2,192]{2,1,0:T(2,128)}, f32[2,2,192]{2,1,0:T(2,128)S(1)}, u32[]{:S(2)}, u32[]{:S(2)}) %collective-permute-start.1) | collective-permute-done | bytes 3104 | tf_op jit(solution)/shard_map/ppermute | solution.py:485
  7.0 0.7 shard_map.95
  7.7 1.7 %collective-permute-start.2 = (f32[2,2,192]{2,1,0:T(2,128)S(1)}, f32[2,2,192]{2,1,0:T(2,128)S(1)}, u32[]{:S(2)}, u32[]{:S(2)}) collective-permute-start(f32[2,2,192]{2,1,0:T(2,128)S(1)} %get-tuple-element.36), channel_id=1, source_target_pairs={{0,8},{8,0},{16,24},{24,16},{32,40},{40,32},{48,56},{56,48},{64,72... | collective-permute-start | bytes 9224 | tf_op jit(solution)/shard_map/ppermute | solution.py:480
  10.0 1.4 collective-permute-done.2.theirs
  11.4 22.9 %shard_map.96 = (f32[2,2,192,192]{3,2,1,0:T(8,128)S(1)}, f32[2,192,192]{2,1,0:T(8,128)S(1)}, f32[2,192,192]{2,1,0:T(8,128)S(1)}, f32[6,192,128]{2,1,0:T(8,128)S(...) custom-call(s32[7]{0:T(128)S(1)} %stack.47.info, f32[192,192]{1,0:T(8,128)S(1)} %copy-done, ...), custom_call_target="tpu_custom_call" | custom-call | flops 32999999488 | bytes 1048576 | tf_op jit(solution)/shard_map/pallas_call | solution.py:226
  34.3 3.1 %collective-permute-start.4 = (f32[3,192,128]{2,1,0:T(8,128)S(1)}, f32[3,192,128]{2,1,0:T(8,128)S(1)}, u32[]{:S(2)}, u32[]{:S(2)}) collective-permute-start(f32[3,192,128]{2,1,0:T(8,128)S(1)} %get-tuple-element.39.own), channel_id=1, source_target_pairs={{8,16},{0,24},{16,8},{24,0},{40,48},{32,56},{48,40},{56,32},{72,80... | collective-permute-start | bytes 884744 | tf_op jit(solution)/shard_map/ppermute | solution.py:495
  37.4 1.5 shard_map.97
  38.9 2.2 %shard_map.99 = (f32[2,192,128]{2,1,0:T(8,128)S(1)}, f32[2,192,192]{2,1,0:T(8,128)S(1)}, f32[6,192,128]{2,1,0:T(8,128)S(1)}, f32[4,192,128]{2,1,0:T(8,128)S(1)}) custom-call(s32[7]{0:T(128)S(1)} %stack.47.info, f32[2,192,192]{2,1,0:T(8,128)S(1)} %get-tuple-element.40.x, f32[2,192,192]{2,1,0:T(8,128)S(1)} %get-tuple-element.41.zn.refs_1_, ...), custom_call_target="tpu_custom_call" | custom-call | flops 5500000256 | bytes 1048576 | tf_op jit(solution)/shard_map/pallas_call | solution.py:226
  41.4 3.0 %collective-permute-start.5 = (f32[6,192,128]{2,1,0:T(8,128)S(1)}, f32[6,192,128]{2,1,0:T(8,128)S(1)}, u32[]{:S(2)}, u32[]{:S(2)}) collective-permute-start(f32[6,192,128]{2,1,0:T(8,128)S(1)} %get-tuple-element.46.own), channel_id=1, source_target_pairs={{8,16},{0,24},{16,8},{24,0},{40,48},{32,56},{48,40},{56,32},{72,80... | collective-permute-start | bytes 1769480 | tf_op jit(solution)/shard_map/ppermute | solution.py:495
  44.8 9.2 %shard_map.98.x = f32[2,192,192]{2,1,0:T(8,128)S(1)} custom-call(f32[3,192,128]{2,1,0:T(8,128)S(1)} %get-tuple-element.39.own, f32[3,192,128]{2,1,0:T(8,128)S(1)} %collective-permute-done.4.other), custom_call_target="tpu_custom_call" | custom-call | flops 13200000000 | bytes 1048576 | tf_op jit(solution)/shard_map/pallas_call | solution.py:226
  54.0 12.7 %collective-permute-done.5.other = f32[6,192,128]{2,1,0:T(8,128)S(1)} collective-permute-done((f32[6,192,128]{2,1,0:T(8,128)S(1)}, f32[6,192,128]{2,1,0:T(8,128)S(1)}, u32[]{:S(2)}, u32[]{:S(2)}) %collective-permute-start.5) | collective-permute-done | bytes 589856 | tf_op jit(solution)/shard_map/ppermute | solution.py:495
  66.7 1.5 shard_map.100
  68.4 2.2 %shard_map.102 = (f32[2,192,128]{2,1,0:T(8,128)S(1)}, f32[2,192,192]{2,1,0:T(8,128)S(1)}, f32[6,192,128]{2,1,0:T(8,128)S(1)}, f32[4,192,128]{2,1,0:T(8,128)S(1)}) custom-call(s32[7]{0:T(128)S(1)} %stack.47.info, f32[2,192,192]{2,1,0:T(8,128)S(1)} %shard_map.98.x, f32[2,192,192]{2,1,0:T(8,128)S(1)} %get-tuple-element.48.zn.refs_4_, ...), custom_call_target="tpu_custom_call" | custom-call | flops 5500000256 | bytes 1048576 | tf_op jit(solution)/shard_map/pallas_call | solution.py:226
  70.6 2.0 %collective-permute-start.10 = (f32[4,192,128]{2,1,0:T(8,128)S(1)}, f32[4,192,128]{2,1,0:T(8,128)S(1)}, u32[]{:S(2)}, u32[]{:S(2)}) collective-permute-start(f32[4,192,128]{2,1,0:T(8,128)S(1)} %get-tuple-element.53.own_r), channel_id=1, source_target_pairs={{8,40},{0,32},{16,48},{24,56},{40,8},{32,0},{48,16},{56,24},{72,10... | collective-permute-start | bytes 1179656 | tf_op jit(solution)/shard_map/ppermute | solution.py:495
  72.7 5.5 %collective-permute-done.6.other = f32[3,192,128]{2,1,0:T(8,128)S(1)} collective-permute-done((f32[3,192,128]{2,1,0:T(8,128)S(1)}, f32[3,192,128]{2,1,0:T(8,128)S(1)}, u32[]{:S(2)}, u32[]{:S(2)}) %collective-permute-start.6) | collective-permute-done | bytes 294944 | tf_op jit(solution)/shard_map/ppermute | solution.py:495
  78.2 9.2 %shard_map.101.x = f32[2,192,192]{2,1,0:T(8,128)S(1)} custom-call(f32[3,192,128]{2,1,0:T(8,128)S(1)} %get-tuple-element.47.own, f32[3,192,128]{2,1,0:T(8,128)S(1)} %collective-permute-done.6.other), custom_call_target="tpu_custom_call" | custom-call | flops 13200000000 | bytes 1048576 | tf_op jit(solution)/shard_map/pallas_call | solution.py:226
  87.3 11.1 %collective-permute-done.8.other = f32[6,192,128]{2,1,0:T(8,128)S(1)} collective-permute-done((f32[6,192,128]{2,1,0:T(8,128)S(1)}, f32[6,192,128]{2,1,0:T(8,128)S(1)}, u32[]{:S(2)}, u32[]{:S(2)}) %collective-permute-start.8) | collective-permute-done | bytes 589856 | tf_op jit(solution)/shard_map/ppermute | solution.py:495
  98.4 1.5 shard_map.103
  99.9 3.2 %collective-permute-start.9 = (f32[3,192,128]{2,1,0:T(8,128)S(1)}, f32[3,192,128]{2,1,0:T(8,128)S(1)}, u32[]{:S(2)}, u32[]{:S(2)}) collective-permute-start(f32[3,192,128]{2,1,0:T(8,128)S(1)} %get-tuple-element.51.own), channel_id=1, source_target_pairs={{8,72},{0,64},{16,80},{24,88},{40,104},{32,96},{48,112},{56,120},{... | collective-permute-start | bytes 884744 | tf_op jit(solution)/shard_map/ppermute | solution.py:495
  103.2 2.2 %shard_map.105 = (f32[2,192,128]{2,1,0:T(8,128)S(1)}, f32[2,192,192]{2,1,0:T(8,128)S(1)}, f32[6,192,128]{2,1,0:T(8,128)S(1)}, f32[4,192,128]{2,1,0:T(8,128)S(1)}) custom-call(s32[7]{0:T(128)S(1)} %stack.47.info, f32[2,192,192]{2,1,0:T(8,128)S(1)} %shard_map.101.x, f32[2,192,192]{2,1,0:T(8,128)S(1)} %get-tuple-element.52.zn.refs_7_, ...), custom_call_target="tpu_custom_call" | custom-call | flops 5500000256 | bytes 1048576 | tf_op jit(solution)/shard_map/pallas_call | solution.py:226
  105.3 0.6 collective-permute-start.12
  106.0 1.3 collective-permute-start.11
  107.2 4.0 %collective-permute-done.9.other = f32[3,192,128]{2,1,0:T(8,128)S(1)} collective-permute-done((f32[3,192,128]{2,1,0:T(8,128)S(1)}, f32[3,192,128]{2,1,0:T(8,128)S(1)}, u32[]{:S(2)}, u32[]{:S(2)}) %collective-permute-start.9) | collective-permute-done | bytes 294944 | tf_op jit(solution)/shard_map/ppermute | solution.py:495
  111.2 9.2 %shard_map.104.x = f32[2,192,192]{2,1,0:T(8,128)S(1)} custom-call(f32[3,192,128]{2,1,0:T(8,128)S(1)} %get-tuple-element.51.own, f32[3,192,128]{2,1,0:T(8,128)S(1)} %collective-permute-done.9.other), custom_call_target="tpu_custom_call" | custom-call | flops 13200000000 | bytes 1048576 | tf_op jit(solution)/shard_map/pallas_call | solution.py:226
  120.4 10.5 %collective-permute-done.11.other = f32[6,192,128]{2,1,0:T(8,128)S(1)} collective-permute-done((f32[6,192,128]{2,1,0:T(8,128)S(1)}, f32[6,192,128]{2,1,0:T(8,128)S(1)}, u32[]{:S(2)}, u32[]{:S(2)}) %collective-permute-start.11) | collective-permute-done | bytes 589856 | tf_op jit(solution)/shard_map/ppermute | solution.py:495
  130.9 10.4 %shard_map.106 = (f32[2,192,192]{2,1,0:T(8,128)S(1)}, f32[2,192,192]{2,1,0:T(8,128)S(1)}) custom-call(s32[7]{0:T(128)S(1)} %stack.47.info, f32[2,192,192]{2,1,0:T(8,128)S(1)} %shard_map.104.x, f32[6,192,128]{2,1,0:T(8,128)S(1)} %get-tuple-element.54.own, f32[6,192,128]{2,1,0:T(8,128)S(1)} %collective-permute-done.11.other), custom_call_target="tpu_custom_call" | custom-call | flops 16499999744 | bytes 1048576 | tf_op jit(solution)/shard_map/pallas_call | solution.py:226
  141.4 4.1 %shard_map.107 = (f32[2,192,128]{2,1,0:T(8,128)S(1)}, f32[2,192,128]{2,1,0:T(8,128)S(1)}, f32[2,192,128]{2,1,0:T(8,128)S(1)}, f32[2,2,192,128]{3,2,1,0:T(8,128)S(1)}) custom-call(s32[7]{0:T(128)S(1)} %stack.47.info, f32[2,192,192]{2,1,0:T(8,128)S(1)} %shard_map.104.x, f32[2,192,192]{2,1,0:T(8,128)S(1)} %get-tuple-element.55.zn, ...), custom_call_target="tpu_custom_call" | custom-call | flops 7699999744 | bytes 1048576 | tf_op jit(solution)/shard_map/pallas_call | solution.py:226
  145.7 1.5 shard_map.108.mine
  147.2 8.1 %collective-permute-done.13.other = f32[2,2,192,128]{3,2,1,0:T(8,128)S(1)} collective-permute-done((f32[2,2,192,128]{3,2,1,0:T(8,128)S(1)}, f32[2,2,192,128]{3,2,1,0:T(8,128)S(1)}, u32[]{:S(2)}, u32[]{:S(2)}) %collective-permute-start.13) | collective-permute-done | bytes 393248 | tf_op jit(solution)/shard_map/ppermute | solution.py:480
  155.3 1.5 shard_map.109
  (29 shorter events, 2.0 us)
Async XLA Ops:
  0.6 3.3 %collective-permute-start = (f32[2,2,192]{2,1,0:T(2,128)}, f32[2,2,192]{2,1,0:T(2,128)S(1)}, u32[]{:S(2)}, u32[]{:S(2)}) collective-permute-start(f32[2,2,192]{2,1,0:T(2,128)} %occ.1), channel_id=1, source_target_pairs={{0,1},{1,2},{2,3},{3,4},{4,5},{5,6},{6,7},{8,9},{9,10},{10,11},{11... | collective-permute-start | bytes 9224 | tf_op jit(solution)/shard_map/ppermute | solution.py:485
  2.4 4.5 %collective-permute-start.1 = (f32[2,2,192]{2,1,0:T(2,128)}, f32[2,2,192]{2,1,0:T(2,128)S(1)}, u32[]{:S(2)}, u32[]{:S(2)}) collective-permute-start(f32[2,2,192]{2,1,0:T(2,128)} %occ.1), channel_id=1, source_target_pairs={{1,0},{2,1},{3,2},{4,3},{5,4},{6,5},{7,6},{9,8},{10,9},{11,10},{12... | collective-permute-start | bytes 9224 | tf_op jit(solution)/shard_map/ppermute | solution.py:485
  3.7 3.2 %copy-start.2 = (f32[16,192]{1,0:T(8,128)S(1)}, f32[16,192]{1,0:T(8,128)}, u32[]{:S(2)}) copy-start(f32[16,192]{1,0:T(8,128)} %table.1) | copy-start | bytes 36868
  3.8 3.2 %copy-start.3 = (f32[2,2,192]{2,1,0:T(2,128)S(1)}, f32[2,2,192]{2,1,0:T(2,128)}, u32[]{:S(2)}) copy-start(f32[2,2,192]{2,1,0:T(2,128)} %occ.1) | copy-start | bytes 9220
  3.8 3.2 %copy-start.4 = (s32[4]{0:T(128)S(1)}, s32[4]{0:T(128)}, u32[]{:S(2)}) copy-start(s32[4]{0:T(128)} %shift.1) | copy-start | bytes 52
  3.8 3.2 %copy-start.5 = (s32[2]{0:T(128)S(1)}, s32[2]{0:T(128)}, u32[]{:S(2)}) copy-start(s32[2]{0:T(128)} %profile.1) | copy-start | bytes 28
  3.8 3.2 %copy-start.6 = (f32[4]{0:T(128)S(1)}, f32[4]{0:T(128)}, u32[]{:S(2)}) copy-start(f32[4]{0:T(128)} %coupling.1) | copy-start | bytes 52
  3.9 5.5 %copy-start.7 = (f32[2,2,2,192,128]{4,3,2,1,0:T(8,128)S(1)}, f32[2,2,2,192,128]{4,3,2,1,0:T(8,128)}, u32[]{:S(2)}) copy-start(f32[2,2,2,192,128]{4,3,2,1,0:T(8,128)} %param.8) | copy-start | bytes 2359300
  7.7 3.7 %copy-start = (f32[192,192]{1,0:T(8,128)S(1)}, f32[192,192]{1,0:T(8,128)}, u32[]{:S(2)}) copy-start(f32[192,192]{1,0:T(8,128)} %onsite.1) | copy-start | bytes 442372
  7.7 3.7 %copy-start.1 = (f32[192,192]{1,0:T(8,128)S(1)}, f32[192,192]{1,0:T(8,128)}, u32[]{:S(2)}) copy-start(f32[192,192]{1,0:T(8,128)} %hop.5) | copy-start | bytes 442372
  7.7 3.7 %collective-permute-start.2 = (f32[2,2,192]{2,1,0:T(2,128)S(1)}, f32[2,2,192]{2,1,0:T(2,128)S(1)}, u32[]{:S(2)}, u32[]{:S(2)}) collective-permute-start(f32[2,2,192]{2,1,0:T(2,128)S(1)} %get-tuple-element.36), channel_id=1, source_target_pairs={{0,8},{8,0},{16,24},{24,16},{32,40},{40,32},{48,56},{56,48},{64,72... | collective-permute-start | bytes 9224 | tf_op jit(solution)/shard_map/ppermute | solution.py:480
  9.4 28.0 %collective-permute-start.3 = (f32[2,2,192,128]{3,2,1,0:T(8,128)S(1)}, f32[2,2,192,128]{3,2,1,0:T(8,128)S(1)}, u32[]{:S(2)}, u32[]{:S(2)}) collective-permute-start(f32[2,2,192,128]{3,2,1,0:T(8,128)S(1)} %get-tuple-element.68), channel_id=1, source_target_pairs={{0,8},{8,0},{16,24},{24,16},{32,40},{40,32},{48,56},{56,48},{64,72... | collective-permute-start | bytes 1179656 | tf_op jit(solution)/shard_map/ppermute | solution.py:480
  34.3 10.5 %collective-permute-start.4 = (f32[3,192,128]{2,1,0:T(8,128)S(1)}, f32[3,192,128]{2,1,0:T(8,128)S(1)}, u32[]{:S(2)}, u32[]{:S(2)}) collective-permute-start(f32[3,192,128]{2,1,0:T(8,128)S(1)} %get-tuple-element.39.own), channel_id=1, source_target_pairs={{8,16},{0,24},{16,8},{24,0},{40,48},{32,56},{48,40},{56,32},{72,80... | collective-permute-start | bytes 884744 | tf_op jit(solution)/shard_map/ppermute | solution.py:495
  41.1 27.3 %collective-permute-start.7 = (f32[4,192,128]{2,1,0:T(8,128)S(1)}, f32[4,192,128]{2,1,0:T(8,128)S(1)}, u32[]{:S(2)}, u32[]{:S(2)}) collective-permute-start(f32[4,192,128]{2,1,0:T(8,128)S(1)} %get-tuple-element.49.own_r), channel_id=1, source_target_pairs={{8,16},{0,24},{16,8},{24,0},{40,48},{32,56},{48,40},{56,32},{72,80... | collective-permute-start | bytes 1179656 | tf_op jit(solution)/shard_map/ppermute | solution.py:495
  41.4 25.3 %collective-permute-start.5 = (f32[6,192,128]{2,1,0:T(8,128)S(1)}, f32[6,192,128]{2,1,0:T(8,128)S(1)}, u32[]{:S(2)}, u32[]{:S(2)}) collective-permute-start(f32[6,192,128]{2,1,0:T(8,128)S(1)} %get-tuple-element.46.own), channel_id=1, source_target_pairs={{8,16},{0,24},{16,8},{24,0},{40,48},{32,56},{48,40},{56,32},{72,80... | collective-permute-start | bytes 1769480 | tf_op jit(solution)/shard_map/ppermute | solution.py:495
  68.2 10.0 %collective-permute-start.6 = (f32[3,192,128]{2,1,0:T(8,128)S(1)}, f32[3,192,128]{2,1,0:T(8,128)S(1)}, u32[]{:S(2)}, u32[]{:S(2)}) collective-permute-start(f32[3,192,128]{2,1,0:T(8,128)S(1)} %get-tuple-element.47.own), channel_id=1, source_target_pairs={{8,40},{0,32},{16,48},{24,56},{40,8},{32,0},{48,16},{56,24},{72,10... | collective-permute-start | bytes 884744 | tf_op jit(solution)/shard_map/ppermute | solution.py:495
  70.6 32.5 %collective-permute-start.10 = (f32[4,192,128]{2,1,0:T(8,128)S(1)}, f32[4,192,128]{2,1,0:T(8,128)S(1)}, u32[]{:S(2)}, u32[]{:S(2)}) collective-permute-start(f32[4,192,128]{2,1,0:T(8,128)S(1)} %get-tuple-element.53.own_r), channel_id=1, source_target_pairs={{8,40},{0,32},{16,48},{24,56},{40,8},{32,0},{48,16},{56,24},{72,10... | collective-permute-start | bytes 1179656 | tf_op jit(solution)/shard_map/ppermute | solution.py:495
  72.6 25.8 %collective-permute-start.8 = (f32[6,192,128]{2,1,0:T(8,128)S(1)}, f32[6,192,128]{2,1,0:T(8,128)S(1)}, u32[]{:S(2)}, u32[]{:S(2)}) collective-permute-start(f32[6,192,128]{2,1,0:T(8,128)S(1)} %get-tuple-element.50.own), channel_id=1, source_target_pairs={{8,40},{0,32},{16,48},{24,56},{40,8},{32,0},{48,16},{56,24},{72,10... | collective-permute-start | bytes 1769480 | tf_op jit(solution)/shard_map/ppermute | solution.py:495
  99.9 11.3 %collective-permute-start.9 = (f32[3,192,128]{2,1,0:T(8,128)S(1)}, f32[3,192,128]{2,1,0:T(8,128)S(1)}, u32[]{:S(2)}, u32[]{:S(2)}) collective-permute-start(f32[3,192,128]{2,1,0:T(8,128)S(1)} %get-tuple-element.51.own), channel_id=1, source_target_pairs={{8,72},{0,64},{16,80},{24,88},{40,104},{32,96},{48,112},{56,120},{... | collective-permute-start | bytes 884744 | tf_op jit(solution)/shard_map/ppermute | solution.py:495
  105.3 36.0 %collective-permute-start.12 = (f32[4,192,128]{2,1,0:T(8,128)S(1)}, f32[4,192,128]{2,1,0:T(8,128)S(1)}, u32[]{:S(2)}, u32[]{:S(2)}) collective-permute-start(f32[4,192,128]{2,1,0:T(8,128)S(1)} %get-tuple-element.57.own_r), channel_id=1, source_target_pairs={{8,72},{0,64},{16,80},{24,88},{40,104},{32,96},{48,112},{56,120},{... | collective-permute-start | bytes 1179656 | tf_op jit(solution)/shard_map/ppermute | solution.py:495
  106.0 25.0 %collective-permute-start.11 = (f32[6,192,128]{2,1,0:T(8,128)S(1)}, f32[6,192,128]{2,1,0:T(8,128)S(1)}, u32[]{:S(2)}, u32[]{:S(2)}) collective-permute-start(f32[6,192,128]{2,1,0:T(8,128)S(1)} %get-tuple-element.54.own), channel_id=1, source_target_pairs={{72,8},{64,0},{80,16},{88,24},{104,40},{96,32},{112,48},{120,56},{... | collective-permute-start | bytes 1769480 | tf_op jit(solution)/shard_map/ppermute | solution.py:495
  145.5 9.9 %collective-permute-start.13 = (f32[2,2,192,128]{3,2,1,0:T(8,128)S(1)}, f32[2,2,192,128]{3,2,1,0:T(8,128)S(1)}, u32[]{:S(2)}, u32[]{:S(2)}) collective-permute-start(f32[2,2,192,128]{3,2,1,0:T(8,128)S(1)} %get-tuple-element.67), channel_id=1, source_target_pairs={{0,8},{8,0},{16,24},{24,16},{32,40},{40,32},{48,56},{56,48},{64,72... | collective-permute-start | bytes 1179656 | tf_op jit(solution)/shard_map/ppermute | solution.py:480

commit v7 on v6

--- a/solution.py
+++ b/solution.py
@@ -208,18 +208,38 @@
     return x[0] - y[0], x[1] - y[1]
 
 
-def pack(ref, x):
-    ref[0] = x[0][:, 0:128]
-    ref[1] = x[1][:, 0:128]
-    ref[2] = jnp.concatenate([x[0][:, 128:N], x[1][:, 128:N]], axis=1)
-
-
-def unpack(ref):
-    rest = ref[2]
+def pack(ref, base, x):
+    ref[base : base + 192, :] = x[0][:, 0:128]
+    ref[base + 192 : base + 384, :] = x[1][:, 0:128]
+    ref[base + 384 : base + 576, :] = jnp.concatenate([x[0][:, 128:N], x[1][:, 128:N]], axis=1)
+
+
+def unpack(ref, base):
+    rest = ref[base + 384 : base + 576, :]
     return (
-        jnp.concatenate([ref[0], rest[:, 0:64]], axis=1),
-        jnp.concatenate([ref[1], rest[:, 64:128]], axis=1),
-    )
+        jnp.concatenate([ref[base : base + 192, :], rest[:, 0:64]], axis=1),
+        jnp.concatenate([ref[base + 192 : base + 384, :], rest[:, 64:128]], axis=1),
+    )
+
+
+def pack_symmetric(ref, base, x):
+    ref[base : base + 192, :] = x[0][:, 0:128]
+    ref[base + 192 : base + 384, :] = x[1][:, 0:128]
+    ref[base + 384 : base + 448, :] = jnp.concatenate(
+        [x[0][128:N, 128:N], x[1][128:N, 128:N]], axis=1
+    )
+
+
+def unpack_symmetric(ref, base):
+    corner = ref[base + 384 : base + 448, :]
+    out = []
+    for part in range(2):
+        left = ref[base + 192 * part : base + 192 * part + 192, :]
+        right = jnp.concatenate(
+            [left[128:N].T, corner[:, 64 * part : 64 * part + 64]], axis=0
+        )
+        out.append(jnp.concatenate([left, right], axis=1))
+    return tuple(out)
 
 
 def call(body, cost, outs, args, scratch=(), scalars=0):
@@ -238,9 +258,9 @@
 
 
 MATRIX = (2, N, N)
-PACKED = (3, N, 128)
+PACKED = (448, 128)
 VECTOR = (2, N, COLS)
-ENDS = (6, N, 128)
+ENDS = (1024, 128)
 RHS = (4, N, COLS)
 
 
@@ -313,15 +333,15 @@
         got.append((up, down))
     (up0, down0), (up2, down2) = got
     middle = sub(sub(block(1), real_right(nn, down0, h)), real_right(nn, up2, ht))
-    pack(left.at[pl.ds(0, 3)], neg(real_right(nn, up0, h)))
-    pack(left.at[pl.ds(3, 3)], neg(real_right(nn, up0, ht)))
-    pack(right.at[pl.ds(0, 3)], neg(real_right(nn, down2, ht)))
-    pack(right.at[pl.ds(3, 3)], sub(block(3), real_right(nn, down2, h)))
+    pack(left, 0, neg(real_right(nn, up0, h)))
+    pack_symmetric(left, 576, neg(real_right(nn, up0, ht)))
+    pack(right, 0, neg(real_right(nn, down2, ht)))
+    pack_symmetric(right, 576, sub(block(3), real_right(nn, down2, h)))
     ar[0, :, 0:N] = middle[0]
     ai[0, :, 0:N] = middle[1]
     sweep(1, ar, ai, m)
     put(x, (-ar[0, :, 0:N], -ai[0, :, 0:N]))
-    near_end(info[3], get(x), left, right, zn, lambda v: pack(near, v))
+    near_end(info[3], get(x), left, right, zn, lambda v: pack_symmetric(near, 0, v))
 
 
 def first_rhs_body(info, xa, hop, kept, other, ia, left, right):
@@ -345,7 +365,7 @@
 
 
 def invert_body(own, other, x, ar, ai, m):
-    now = add(unpack(own), unpack(other))
+    now = add(unpack_symmetric(own, 0), unpack_symmetric(other, 0))
     ar[0, :, 0:N] = now[0]
     ai[0, :, 0:N] = now[1]
     sweep(1, ar, ai, m)
@@ -353,11 +373,11 @@
 
 
 def coupling_of(ref):
-    return unpack(ref.at[pl.ds(0, 3)])
+    return unpack(ref, 0)
 
 
 def end_block(ref):
-    return unpack(ref.at[pl.ds(3, 3)])
+    return unpack_symmetric(ref, 576)
 
 
 def near_end(flag, x, own, other, zn, store):
@@ -369,7 +389,7 @@
 
 
 def near_body(level, info, x, own, other, zn, near):
-    near_end(info[3 + level], get(x), own, other, zn, lambda v: pack(near, v))
+    near_end(info[3 + level], get(x), own, other, zn, lambda v: pack_symmetric(near, 0, v))
 
 
 def rhs_ends(ref):
@@ -390,9 +410,9 @@
     put(out_r.at[pl.ds(0, 2)], sub(choose(flag, theirs_far, mine_far), vdot(nn, zns, r)))
     put(zf, z)
     z = csplit(z)
-    pack(out.at[pl.ds(0, 3)], neg(cdot(nt, z, t_near)))
+    pack(out, 0, neg(cdot(nt, z, t_near)))
     f = choose(flag, end_block(own), end_block(other))
-    pack(out.at[pl.ds(3, 3)], sub(f, cdot(nt, z, t_far)))
+    pack_symmetric(out, 576, sub(f, cdot(nt, z, t_far)))
     put(out_r.at[pl.ds(2, 2)], sub(choose(flag, mine_far, theirs_far), vdot(nn, z, r)))
 
 

time: 158 us -> 150 us (0.949)
  waiting for transfers between devices: 56.8 us -> 49.2 us
    ppermute x9, waiting for transfers between devices: 44.2 us -> 37.1 us  [swapped(): return lax.ppermute(array, 'slab', pairs)]
  transfers between devices with their start and end apart: 14 -> 14, of which waited for: 9 -> 8; matrix products, arithmetic and copies ran while one was open for 0% -> 0% of each run, Pallas kernels for 47% -> 49%
where the time goes in v7:
time: 150 us; the launch traced here: 149 us
  Pallas kernels  79.7 us (53%)
  waiting for transfers between devices  49.2 us (33%)
  starting transfers between devices  19.2 us (13%)
    pallas_call x15, Pallas kernels, call(): pl.pallas_call(body, out_shape=tuple((jax.ShapeDtypeStruct(s, jnp.float32...  79.7 us
    ppermute x9, waiting for transfers between devices, swapped(): return lax.ppermute(array, 'slab', pairs)  37.1 us
    ppermute x9, starting transfers between devices, swapped(): return lax.ppermute(array, 'slab', pairs)  13.9 us
    ppermute x3, waiting for transfers between devices, pair(): return lax.ppermute(array, 'slab', [(s, s ^ 1) for s in range(slabs)])  9.1 us
    ppermute x2, waiting for transfers between devices, along(): return lax.ppermute(array, 'energy', pairs)  3.04 us
    ppermute x2, starting transfers between devices, along(): return lax.ppermute(array, 'energy', pairs)  3.03 us
  transfers between devices with their start and end apart: 14, of which 8 were waited for; matrix products, arithmetic and copies ran while one was open for 0% of the time, Pallas kernels for 49%

profile of v7, /device:TPU:32, one launch (start us, length us, event | category | flops | bytes accessed | tf_op | source)
XLA Modules:
  0.0 149.2 jit_solution(7532804721831085397)
XLA Ops:
  0.6 1.7 %collective-permute-start = (f32[2,2,192]{2,1,0:T(2,128)}, f32[2,2,192]{2,1,0:T(2,128)S(1)}, u32[]{:S(2)}, u32[]{:S(2)}) collective-permute-start(f32[2,2,192]{2,1,0:T(2,128)} %occ.1), channel_id=1, source_target_pairs={{0,1},{1,2},{2,3},{3,4},{4,5},{5,6},{6,7},{8,9},{9,10},{10,11},{11... | collective-permute-start | bytes 9224 | tf_op jit(solution)/shard_map/ppermute | solution.py:505
  2.4 1.3 collective-permute-start.1
  3.9 3.0 %collective-permute-done.1.high = f32[2,2,192]{2,1,0:T(2,128)S(1)} collective-permute-done((f32[2,2,192]{2,1,0:T(2,128)}, f32[2,2,192]{2,1,0:T(2,128)S(1)}, u32[]{:S(2)}, u32[]{:S(2)}) %collective-permute-start.1) | collective-permute-done | bytes 3104 | tf_op jit(solution)/shard_map/ppermute | solution.py:505
  7.0 0.7 shard_map.95
  7.7 1.7 %collective-permute-start.2 = (f32[2,2,192]{2,1,0:T(2,128)S(1)}, f32[2,2,192]{2,1,0:T(2,128)S(1)}, u32[]{:S(2)}, u32[]{:S(2)}) collective-permute-start(f32[2,2,192]{2,1,0:T(2,128)S(1)} %get-tuple-element.36), channel_id=1, source_target_pairs={{0,8},{8,0},{16,24},{24,16},{32,40},{40,32},{48,56},{56,48},{64,72... | collective-permute-start | bytes 9224 | tf_op jit(solution)/shard_map/ppermute | solution.py:500
  10.0 1.4 collective-permute-done.2.theirs
  11.4 22.9 %shard_map.96 = (f32[2,2,192,192]{3,2,1,0:T(8,128)S(1)}, f32[2,192,192]{2,1,0:T(8,128)S(1)}, f32[2,192,192]{2,1,0:T(8,128)S(1)}, f32[1024,128]{1,0:T(8,128)S(1)}...) custom-call(s32[7]{0:T(128)S(1)} %stack.47.info, f32[192,192]{1,0:T(8,128)S(1)} %copy-done, f32[192,192]{1,0:T(8,128)S(1)} %copy-done.1, ...), custom_call_target="tpu_custom_call" | custom-call | flops 32999999488 | bytes 1048576 | tf_op jit(solution)/shard_map/pallas_call | solution.py:246
  34.3 3.1 %collective-permute-start.4 = (f32[448,128]{1,0:T(8,128)S(1)}, f32[448,128]{1,0:T(8,128)S(1)}, u32[]{:S(2)}, u32[]{:S(2)}) collective-permute-start(f32[448,128]{1,0:T(8,128)S(1)} %get-tuple-element.39.own), channel_id=1, source_target_pairs={{8,16},{0,24},{16,8},{24,0},{40,48},{32,56},{48,40},{56,32},{72,80... | collective-permute-start | bytes 688136 | tf_op jit(solution)/shard_map/ppermute | solution.py:515
  37.4 1.5 %shard_map.97 = (f32[2,2,192,128]{3,2,1,0:T(8,128)S(1)}, f32[4,192,128]{2,1,0:T(8,128)S(1)}, f32[4,192,128]{2,1,0:T(8,128)S(1)}) custom-call(s32[7]{0:T(128)S(1)} %stack.47.info, f32[2,2,192,192]{3,2,1,0:T(8,128)S(1)} %get-tuple-element.37.xa.refs_9_, f32[192,192]{1,0:T(8,128)S(1)} %copy-done.1, f32[2,2,192,128]{3,2,1,0:T(8,128)S(1)} %get-tuple-element.69.kept, ...), custom_call_target="tpu_custom_call" | custom-call | flops 3300000000 | bytes 1048576 | tf_op jit(solution)/shard_map/pallas_call | solution.py:246
  38.9 2.2 %shard_map.99 = (f32[2,192,128]{2,1,0:T(8,128)S(1)}, f32[2,192,192]{2,1,0:T(8,128)S(1)}, f32[1024,128]{1,0:T(8,128)S(1)}, f32[4,192,128]{2,1,0:T(8,128)S(1)}) custom-call(s32[7]{0:T(128)S(1)} %stack.47.info, f32[2,192,192]{2,1,0:T(8,128)S(1)} %get-tuple-element.40.x, f32[2,192,192]{2,1,0:T(8,128)S(1)} %get-tuple-element.41.zn.refs_1_, ...), custom_call_target="tpu_custom_call" | custom-call | flops 5500000256 | bytes 1048576 | tf_op jit(solution)/shard_map/pallas_call | solution.py:246
  41.4 3.0 %collective-permute-start.5 = (f32[1024,128]{1,0:T(8,128)S(1)}, f32[1024,128]{1,0:T(8,128)S(1)}, u32[]{:S(2)}, u32[]{:S(2)}) collective-permute-start(f32[1024,128]{1,0:T(8,128)S(1)} %get-tuple-element.46.own), channel_id=1, source_target_pairs={{8,16},{0,24},{16,8},{24,0},{40,48},{32,56},{48,40},{56,32},{72,80... | collective-permute-start | bytes 1572872 | tf_op jit(solution)/shard_map/ppermute | solution.py:515
  44.4 9.2 %shard_map.98.x = f32[2,192,192]{2,1,0:T(8,128)S(1)} custom-call(f32[448,128]{1,0:T(8,128)S(1)} %get-tuple-element.39.own, f32[448,128]{1,0:T(8,128)S(1)} %collective-permute-done.4.other), custom_call_target="tpu_custom_call" | custom-call | flops 13200000000 | bytes 1048576 | tf_op jit(solution)/shard_map/pallas_call | solution.py:246
  53.6 11.7 %collective-permute-done.5.other = f32[1024,128]{1,0:T(8,128)S(1)} collective-permute-done((f32[1024,128]{1,0:T(8,128)S(1)}, f32[1024,128]{1,0:T(8,128)S(1)}, u32[]{:S(2)}, u32[]{:S(2)}) %collective-permute-start.5) | collective-permute-done | bytes 524320 | tf_op jit(solution)/shard_map/ppermute | solution.py:515
  65.3 1.5 %shard_map.100 = (f32[2,192,192]{2,1,0:T(8,128)S(1)}, f32[448,128]{1,0:T(8,128)S(1)}) custom-call(s32[7]{0:T(128)S(1)} %stack.47.info, f32[2,192,192]{2,1,0:T(8,128)S(1)} %shard_map.98.x, f32[1024,128]{1,0:T(8,128)S(1)} %get-tuple-element.46.own, f32[1024,128]{1,0:T(8,128)S(1)} %collective-permute-done.5.other), custom_call_target="tpu_custom_call" | custom-call | flops 3300000000 | bytes 1048576 | tf_op jit(solution)/shard_map/pallas_call | solution.py:246
  67.0 2.2 %shard_map.102 = (f32[2,192,128]{2,1,0:T(8,128)S(1)}, f32[2,192,192]{2,1,0:T(8,128)S(1)}, f32[1024,128]{1,0:T(8,128)S(1)}, f32[4,192,128]{2,1,0:T(8,128)S(1)}) custom-call(s32[7]{0:T(128)S(1)} %stack.47.info, f32[2,192,192]{2,1,0:T(8,128)S(1)} %shard_map.98.x, f32[2,192,192]{2,1,0:T(8,128)S(1)} %get-tuple-element.48.zn.refs_4_, ...), custom_call_target="tpu_custom_call" | custom-call | flops 5500000256 | bytes 1048576 | tf_op jit(solution)/shard_map/pallas_call | solution.py:246
  69.2 2.0 %collective-permute-start.10 = (f32[4,192,128]{2,1,0:T(8,128)S(1)}, f32[4,192,128]{2,1,0:T(8,128)S(1)}, u32[]{:S(2)}, u32[]{:S(2)}) collective-permute-start(f32[4,192,128]{2,1,0:T(8,128)S(1)} %get-tuple-element.53.own_r), channel_id=1, source_target_pairs={{8,40},{0,32},{16,48},{24,56},{40,8},{32,0},{48,16},{56,24},{72,10... | collective-permute-start | bytes 1179656 | tf_op jit(solution)/shard_map/ppermute | solution.py:515
  71.3 4.1 %collective-permute-done.6.other = f32[448,128]{1,0:T(8,128)S(1)} collective-permute-done((f32[448,128]{1,0:T(8,128)S(1)}, f32[448,128]{1,0:T(8,128)S(1)}, u32[]{:S(2)}, u32[]{:S(2)}) %collective-permute-start.6) | collective-permute-done | bytes 229408 | tf_op jit(solution)/shard_map/ppermute | solution.py:515
  75.4 9.2 %shard_map.101.x = f32[2,192,192]{2,1,0:T(8,128)S(1)} custom-call(f32[448,128]{1,0:T(8,128)S(1)} %get-tuple-element.47.own, f32[448,128]{1,0:T(8,128)S(1)} %collective-permute-done.6.other), custom_call_target="tpu_custom_call" | custom-call | flops 13200000000 | bytes 1048576 | tf_op jit(solution)/shard_map/pallas_call | solution.py:246
  84.6 9.6 %collective-permute-done.8.other = f32[1024,128]{1,0:T(8,128)S(1)} collective-permute-done((f32[1024,128]{1,0:T(8,128)S(1)}, f32[1024,128]{1,0:T(8,128)S(1)}, u32[]{:S(2)}, u32[]{:S(2)}) %collective-permute-start.8) | collective-permute-done | bytes 524320 | tf_op jit(solution)/shard_map/ppermute | solution.py:515
  94.2 1.5 %shard_map.103 = (f32[2,192,192]{2,1,0:T(8,128)S(1)}, f32[448,128]{1,0:T(8,128)S(1)}) custom-call(s32[7]{0:T(128)S(1)} %stack.47.info, f32[2,192,192]{2,1,0:T(8,128)S(1)} %shard_map.101.x, f32[1024,128]{1,0:T(8,128)S(1)} %get-tuple-element.50.own, f32[1024,128]{1,0:T(8,128)S(1)} %collective-permute-done.8.other), custom_call_target="tpu_custom_call" | custom-call | flops 3300000000 | bytes 1048576 | tf_op jit(solution)/shard_map/pallas_call | solution.py:246
  95.7 3.2 %collective-permute-start.9 = (f32[448,128]{1,0:T(8,128)S(1)}, f32[448,128]{1,0:T(8,128)S(1)}, u32[]{:S(2)}, u32[]{:S(2)}) collective-permute-start(f32[448,128]{1,0:T(8,128)S(1)} %get-tuple-element.51.own), channel_id=1, source_target_pairs={{8,72},{0,64},{16,80},{24,88},{40,104},{32,96},{48,112},{56,120},{... | collective-permute-start | bytes 688136 | tf_op jit(solution)/shard_map/ppermute | solution.py:515
  98.9 2.2 %shard_map.105 = (f32[2,192,128]{2,1,0:T(8,128)S(1)}, f32[2,192,192]{2,1,0:T(8,128)S(1)}, f32[1024,128]{1,0:T(8,128)S(1)}, f32[4,192,128]{2,1,0:T(8,128)S(1)}) custom-call(s32[7]{0:T(128)S(1)} %stack.47.info, f32[2,192,192]{2,1,0:T(8,128)S(1)} %shard_map.101.x, f32[2,192,192]{2,1,0:T(8,128)S(1)} %get-tuple-element.52.zn.refs_7_, ...), custom_call_target="tpu_custom_call" | custom-call | flops 5500000256 | bytes 1048576 | tf_op jit(solution)/shard_map/pallas_call | solution.py:246
  101.1 0.6 collective-permute-start.12
  101.7 1.3 collective-permute-start.11
  103.0 1.9 %collective-permute-done.9.other = f32[448,128]{1,0:T(8,128)S(1)} collective-permute-done((f32[448,128]{1,0:T(8,128)S(1)}, f32[448,128]{1,0:T(8,128)S(1)}, u32[]{:S(2)}, u32[]{:S(2)}) %collective-permute-start.9) | collective-permute-done | bytes 229408 | tf_op jit(solution)/shard_map/ppermute | solution.py:515
  104.9 9.2 %shard_map.104.x = f32[2,192,192]{2,1,0:T(8,128)S(1)} custom-call(f32[448,128]{1,0:T(8,128)S(1)} %get-tuple-element.51.own, f32[448,128]{1,0:T(8,128)S(1)} %collective-permute-done.9.other), custom_call_target="tpu_custom_call" | custom-call | flops 13200000000 | bytes 1048576 | tf_op jit(solution)/shard_map/pallas_call | solution.py:246
  114.1 9.8 %collective-permute-done.11.other = f32[1024,128]{1,0:T(8,128)S(1)} collective-permute-done((f32[1024,128]{1,0:T(8,128)S(1)}, f32[1024,128]{1,0:T(8,128)S(1)}, u32[]{:S(2)}, u32[]{:S(2)}) %collective-permute-start.11) | collective-permute-done | bytes 524320 | tf_op jit(solution)/shard_map/ppermute | solution.py:515
  123.9 10.5 %shard_map.106 = (f32[2,192,192]{2,1,0:T(8,128)S(1)}, f32[2,192,192]{2,1,0:T(8,128)S(1)}) custom-call(s32[7]{0:T(128)S(1)} %stack.47.info, f32[2,192,192]{2,1,0:T(8,128)S(1)} %shard_map.104.x, f32[1024,128]{1,0:T(8,128)S(1)} %get-tuple-element.54.own, f32[1024,128]{1,0:T(8,128)S(1)} %collective-permute-done.11.other), custom_call_target="tpu_custom_call" | custom-call | flops 16499999744 | bytes 1048576 | tf_op jit(solution)/shard_map/pallas_call | solution.py:246
  134.4 4.1 %shard_map.107 = (f32[2,192,128]{2,1,0:T(8,128)S(1)}, f32[2,192,128]{2,1,0:T(8,128)S(1)}, f32[2,192,128]{2,1,0:T(8,128)S(1)}, f32[2,2,192,128]{3,2,1,0:T(8,128)S(1)}) custom-call(s32[7]{0:T(128)S(1)} %stack.47.info, f32[2,192,192]{2,1,0:T(8,128)S(1)} %shard_map.104.x, f32[2,192,192]{2,1,0:T(8,128)S(1)} %get-tuple-element.55.zn, ...), custom_call_target="tpu_custom_call" | custom-call | flops 7699999744 | bytes 1048576 | tf_op jit(solution)/shard_map/pallas_call | solution.py:246
  138.5 1.5 shard_map.108.mine
  140.0 7.7 %collective-permute-done.13.other = f32[2,2,192,128]{3,2,1,0:T(8,128)S(1)} collective-permute-done((f32[2,2,192,128]{3,2,1,0:T(8,128)S(1)}, f32[2,2,192,128]{3,2,1,0:T(8,128)S(1)}, u32[]{:S(2)}, u32[]{:S(2)}) %collective-permute-start.13) | collective-permute-done | bytes 393248 | tf_op jit(solution)/shard_map/ppermute | solution.py:500
  147.7 1.5 shard_map.109
  (29 shorter events, 1.4 us)
Async XLA Ops:
  0.6 3.3 %collective-permute-start = (f32[2,2,192]{2,1,0:T(2,128)}, f32[2,2,192]{2,1,0:T(2,128)S(1)}, u32[]{:S(2)}, u32[]{:S(2)}) collective-permute-start(f32[2,2,192]{2,1,0:T(2,128)} %occ.1), channel_id=1, source_target_pairs={{0,1},{1,2},{2,3},{3,4},{4,5},{5,6},{6,7},{8,9},{9,10},{10,11},{11... | collective-permute-start | bytes 9224 | tf_op jit(solution)/shard_map/ppermute | solution.py:505
  2.4 4.5 %collective-permute-start.1 = (f32[2,2,192]{2,1,0:T(2,128)}, f32[2,2,192]{2,1,0:T(2,128)S(1)}, u32[]{:S(2)}, u32[]{:S(2)}) collective-permute-start(f32[2,2,192]{2,1,0:T(2,128)} %occ.1), channel_id=1, source_target_pairs={{1,0},{2,1},{3,2},{4,3},{5,4},{6,5},{7,6},{9,8},{10,9},{11,10},{12... | collective-permute-start | bytes 9224 | tf_op jit(solution)/shard_map/ppermute | solution.py:505
  3.7 3.2 %copy-start.2 = (f32[16,192]{1,0:T(8,128)S(1)}, f32[16,192]{1,0:T(8,128)}, u32[]{:S(2)}) copy-start(f32[16,192]{1,0:T(8,128)} %table.1) | copy-start | bytes 36868
  3.8 3.2 %copy-start.3 = (f32[2,2,192]{2,1,0:T(2,128)S(1)}, f32[2,2,192]{2,1,0:T(2,128)}, u32[]{:S(2)}) copy-start(f32[2,2,192]{2,1,0:T(2,128)} %occ.1) | copy-start | bytes 9220
  3.8 3.2 %copy-start.4 = (s32[4]{0:T(128)S(1)}, s32[4]{0:T(128)}, u32[]{:S(2)}) copy-start(s32[4]{0:T(128)} %shift.1) | copy-start | bytes 52
  3.8 3.2 %copy-start.5 = (s32[2]{0:T(128)S(1)}, s32[2]{0:T(128)}, u32[]{:S(2)}) copy-start(s32[2]{0:T(128)} %profile.1) | copy-start | bytes 28
  3.8 3.2 %copy-start.6 = (f32[4]{0:T(128)S(1)}, f32[4]{0:T(128)}, u32[]{:S(2)}) copy-start(f32[4]{0:T(128)} %coupling.1) | copy-start | bytes 52
  3.9 5.5 %copy-start.7 = (f32[2,2,2,192,128]{4,3,2,1,0:T(8,128)S(1)}, f32[2,2,2,192,128]{4,3,2,1,0:T(8,128)}, u32[]{:S(2)}) copy-start(f32[2,2,2,192,128]{4,3,2,1,0:T(8,128)} %param.8) | copy-start | bytes 2359300
  7.7 3.7 %copy-start = (f32[192,192]{1,0:T(8,128)S(1)}, f32[192,192]{1,0:T(8,128)}, u32[]{:S(2)}) copy-start(f32[192,192]{1,0:T(8,128)} %onsite.1) | copy-start | bytes 442372
  7.7 3.7 %copy-start.1 = (f32[192,192]{1,0:T(8,128)S(1)}, f32[192,192]{1,0:T(8,128)}, u32[]{:S(2)}) copy-start(f32[192,192]{1,0:T(8,128)} %hop.5) | copy-start | bytes 442372
  7.7 3.7 %collective-permute-start.2 = (f32[2,2,192]{2,1,0:T(2,128)S(1)}, f32[2,2,192]{2,1,0:T(2,128)S(1)}, u32[]{:S(2)}, u32[]{:S(2)}) collective-permute-start(f32[2,2,192]{2,1,0:T(2,128)S(1)} %get-tuple-element.36), channel_id=1, source_target_pairs={{0,8},{8,0},{16,24},{24,16},{32,40},{40,32},{48,56},{56,48},{64,72... | collective-permute-start | bytes 9224 | tf_op jit(solution)/shard_map/ppermute | solution.py:500
  9.4 28.0 %collective-permute-start.3 = (f32[2,2,192,128]{3,2,1,0:T(8,128)S(1)}, f32[2,2,192,128]{3,2,1,0:T(8,128)S(1)}, u32[]{:S(2)}, u32[]{:S(2)}) collective-permute-start(f32[2,2,192,128]{3,2,1,0:T(8,128)S(1)} %get-tuple-element.68), channel_id=1, source_target_pairs={{0,8},{8,0},{16,24},{24,16},{32,40},{40,32},{48,56},{56,48},{64,72... | collective-permute-start | bytes 1179656 | tf_op jit(solution)/shard_map/ppermute | solution.py:500
  34.3 10.1 %collective-permute-start.4 = (f32[448,128]{1,0:T(8,128)S(1)}, f32[448,128]{1,0:T(8,128)S(1)}, u32[]{:S(2)}, u32[]{:S(2)}) collective-permute-start(f32[448,128]{1,0:T(8,128)S(1)} %get-tuple-element.39.own), channel_id=1, source_target_pairs={{8,16},{0,24},{16,8},{24,0},{40,48},{32,56},{48,40},{56,32},{72,80... | collective-permute-start | bytes 688136 | tf_op jit(solution)/shard_map/ppermute | solution.py:515
  41.1 25.9 %collective-permute-start.7 = (f32[4,192,128]{2,1,0:T(8,128)S(1)}, f32[4,192,128]{2,1,0:T(8,128)S(1)}, u32[]{:S(2)}, u32[]{:S(2)}) collective-permute-start(f32[4,192,128]{2,1,0:T(8,128)S(1)} %get-tuple-element.49.own_r), channel_id=1, source_target_pairs={{8,16},{0,24},{16,8},{24,0},{40,48},{32,56},{48,40},{56,32},{72,80... | collective-permute-start | bytes 1179656 | tf_op jit(solution)/shard_map/ppermute | solution.py:515
  41.4 23.9 %collective-permute-start.5 = (f32[1024,128]{1,0:T(8,128)S(1)}, f32[1024,128]{1,0:T(8,128)S(1)}, u32[]{:S(2)}, u32[]{:S(2)}) collective-permute-start(f32[1024,128]{1,0:T(8,128)S(1)} %get-tuple-element.46.own), channel_id=1, source_target_pairs={{8,16},{0,24},{16,8},{24,0},{40,48},{32,56},{48,40},{56,32},{72,80... | collective-permute-start | bytes 1572872 | tf_op jit(solution)/shard_map/ppermute | solution.py:515
  66.8 8.6 %collective-permute-start.6 = (f32[448,128]{1,0:T(8,128)S(1)}, f32[448,128]{1,0:T(8,128)S(1)}, u32[]{:S(2)}, u32[]{:S(2)}) collective-permute-start(f32[448,128]{1,0:T(8,128)S(1)} %get-tuple-element.47.own), channel_id=1, source_target_pairs={{8,40},{0,32},{16,48},{24,56},{40,8},{32,0},{48,16},{56,24},{72,10... | collective-permute-start | bytes 688136 | tf_op jit(solution)/shard_map/ppermute | solution.py:515
  69.2 29.7 %collective-permute-start.10 = (f32[4,192,128]{2,1,0:T(8,128)S(1)}, f32[4,192,128]{2,1,0:T(8,128)S(1)}, u32[]{:S(2)}, u32[]{:S(2)}) collective-permute-start(f32[4,192,128]{2,1,0:T(8,128)S(1)} %get-tuple-element.53.own_r), channel_id=1, source_target_pairs={{8,40},{0,32},{16,48},{24,56},{40,8},{32,0},{48,16},{56,24},{72,10... | collective-permute-start | bytes 1179656 | tf_op jit(solution)/shard_map/ppermute | solution.py:515
  71.2 23.0 %collective-permute-start.8 = (f32[1024,128]{1,0:T(8,128)S(1)}, f32[1024,128]{1,0:T(8,128)S(1)}, u32[]{:S(2)}, u32[]{:S(2)}) collective-permute-start(f32[1024,128]{1,0:T(8,128)S(1)} %get-tuple-element.50.own), channel_id=1, source_target_pairs={{8,40},{0,32},{16,48},{24,56},{40,8},{32,0},{48,16},{56,24},{72,10... | collective-permute-start | bytes 1572872 | tf_op jit(solution)/shard_map/ppermute | solution.py:515
  95.7 9.2 %collective-permute-start.9 = (f32[448,128]{1,0:T(8,128)S(1)}, f32[448,128]{1,0:T(8,128)S(1)}, u32[]{:S(2)}, u32[]{:S(2)}) collective-permute-start(f32[448,128]{1,0:T(8,128)S(1)} %get-tuple-element.51.own), channel_id=1, source_target_pairs={{8,72},{0,64},{16,80},{24,88},{40,104},{32,96},{48,112},{56,120},{... | collective-permute-start | bytes 688136 | tf_op jit(solution)/shard_map/ppermute | solution.py:515
  101.1 33.3 %collective-permute-start.12 = (f32[4,192,128]{2,1,0:T(8,128)S(1)}, f32[4,192,128]{2,1,0:T(8,128)S(1)}, u32[]{:S(2)}, u32[]{:S(2)}) collective-permute-start(f32[4,192,128]{2,1,0:T(8,128)S(1)} %get-tuple-element.57.own_r), channel_id=1, source_target_pairs={{8,72},{0,64},{16,80},{24,88},{40,104},{32,96},{48,112},{56,120},{... | collective-permute-start | bytes 1179656 | tf_op jit(solution)/shard_map/ppermute | solution.py:515
  101.7 22.2 %collective-permute-start.11 = (f32[1024,128]{1,0:T(8,128)S(1)}, f32[1024,128]{1,0:T(8,128)S(1)}, u32[]{:S(2)}, u32[]{:S(2)}) collective-permute-start(f32[1024,128]{1,0:T(8,128)S(1)} %get-tuple-element.54.own), channel_id=1, source_target_pairs={{72,8},{64,0},{80,16},{88,24},{104,40},{96,32},{112,48},{120,56},{... | collective-permute-start | bytes 1572872 | tf_op jit(solution)/shard_map/ppermute | solution.py:515
  138.5 9.2 %collective-permute-start.13 = (f32[2,2,192,128]{3,2,1,0:T(8,128)S(1)}, f32[2,2,192,128]{3,2,1,0:T(8,128)S(1)}, u32[]{:S(2)}, u32[]{:S(2)}) collective-permute-start(f32[2,2,192,128]{3,2,1,0:T(8,128)S(1)} %get-tuple-element.67), channel_id=1, source_target_pairs={{0,8},{8,0},{16,24},{24,16},{32,40},{40,32},{48,56},{56,48},{64,72... | collective-permute-start | bytes 1179656 | tf_op jit(solution)/shard_map/ppermute | solution.py:500
